TPU v7x, 32 devices: a whole 2x2x4 slice. The times are simulated.
32 devices in a mesh: section: 4 (over y, x), row: 2 (over core), col: 4 (over z).
Axes of the slice: x: 2, y: 2, z: 4, core: 2. Of those that a mesh axis runs over, the one named last changes fastest.
Arguments:
- latent: bfloat16 [16, 8, 64, 256], P('section', 'row', 'col'), may hold values from -6 to 6
- w_first: bfloat16 [3, 3, 3, 256, 256], replicated, may hold values from -0.078125 to 0.078125
- w_second: bfloat16 [3, 3, 3, 256, 128], replicated, may hold values from -0.078125 to 0.078125
- w_third: bfloat16 [3, 3, 3, 128, 128], replicated, may hold values from -0.109375 to 0.109375
Outputs:
- decoded: bfloat16 [16, 16, 128, 128], P('section', 'row', 'col')
All inputs are finite; a program needn't handle non-finite values.
Results may differ from a plain program's by a relative error of at most 0.0057.
Values may be sent and summed in bfloat16 or wider, within the bound.
No kernel may reach another device: no remote copies, remote signals or barrier semaphores. Data moves between devices by JAX's collectives and lax.ppermute only.
A program may use at most 64 MiB of HBM per device.

v0:
```python
import jax
import jax.numpy as jnp
from jax import lax
from jax.sharding import PartitionSpec as P


def shifted(x, axis, by):
    size = lax.axis_size(axis)
    pairs = [(i, i + by) for i in range(size) if 0 <= i + by < size]
    return lax.ppermute(x, axis, pairs)


def extended_2(x, sides, width):
    for axis, dim in sides:
        size, length = (lax.axis_size(axis), x.shape[dim])
        up = [(i, (i + 1) % size) for i in range(size - 1)]
        down = [(j, i) for i, j in up]
        last = lax.slice_in_dim(x, length - width, length, axis=dim)
        leading = lax.slice_in_dim(x, 0, width, axis=dim)
        before = lax.ppermute(last, axis, up)
        after = lax.ppermute(leading, axis, down)
        x = jnp.concatenate([before, x, after], axis=dim)
    return x


def upsample(field):
    frames, height, breadth, width = field.shape
    grown = jnp.broadcast_to(field[:, :, None, :, None, :], (frames, height, 2, breadth, 2, width))
    return grown.reshape(frames, 2 * height, 2 * breadth, width)


def causal_conv(padded, kernel):
    frames = padded.shape[0] - 2
    height = padded.shape[1] - 2
    breadth = padded.shape[2] - 2
    in_width = padded.shape[3]
    out_width = kernel.shape[4]
    summed = jnp.zeros((frames * height * breadth, out_width), jnp.float32)
    for row_tap in range(3):
        for col_tap in range(3):
            window = padded[:, row_tap : row_tap + height, col_tap : col_tap + breadth, :]
            stacked = jnp.concatenate(
                [window[0:frames], window[1 : frames + 1], window[2 : frames + 2]], axis=-1
            )
            tap_matrix = kernel[:, row_tap, col_tap].reshape(3 * in_width, out_width)
            summed = summed + jnp.dot(
                stacked.reshape(-1, 3 * in_width), tap_matrix, preferred_element_type=jnp.float32
            )
    return summed.reshape(frames, height, breadth, out_width)


def with_earlier(field):
    earlier = shifted(field[-2:], "section", 1)
    return jnp.concatenate([earlier, field], axis=0)


def with_fine_earlier(field):
    earlier = shifted(field[-2:], "section", 1)
    return jnp.concatenate([earlier, field], axis=0)


def per_device(latent, w_first, w_second, w_third):
    padded = extended_2(with_earlier(latent), (("row", 1), ("col", 2)), 1)
    first = causal_conv(padded, w_first).astype(jnp.bfloat16)
    extended = with_earlier(first)
    margin = extended_2(extended, (("row", 1), ("col", 2)), 1)
    grown = jnp.maximum(upsample(margin)[:, 1:-1, 1:-1, :], 0)
    second = jnp.maximum(causal_conv(grown, w_second), 0.0).astype(jnp.bfloat16)
    second_ext = with_fine_earlier(second)
    margin_fine = extended_2(second_ext, (("row", 1), ("col", 2)), 1)
    return causal_conv(margin_fine, w_third).astype(jnp.bfloat16)


def solution(mesh):
    in_specs = (P("section", "row", "col", None), P(), P(), P())
    out_specs = P("section", "row", "col", None)
    return jax.shard_map(
        per_device, mesh=mesh, in_specs=in_specs, out_specs=out_specs, check_vma=False
    )
```

profile of v0, /device:TPU:28, one launch (start us, length us, event | category | flops | bytes accessed | tf_op | source)
XLA Modules:
  0.0 91.4 jit_solution(11723254497056689068)
XLA Ops:
  0.0 0.8 slice.488
  0.8 3.4 %collective-permute-start = (bf16[2,4,16,256]{3,2,1,0:T(8,128)(2,1)S(1)}, bf16[2,4,16,256]{3,2,1,0:T(8,128)(2,1)S(1)}, u32[]{:S(2)}, u32[]{:S(2)}) collective-permute-start(bf16[2,4,16,256]{3,2,1,0:T(8,128)(2,1)S(1)} %slice.488), channel_id=1, source_target_pairs={{0,8},{8,16},{16,24},{1,9},{9,17},{17,25},{2,10},{10,18},{18,26},{... | collective-permute-start | bytes 196616 | tf_op jit(solution)/shard_map/ppermute | solution.py:10
  4.2 3.7 %collective-permute-done = bf16[2,4,16,256]{3,2,1,0:T(8,128)(2,1)S(1)} collective-permute-done((bf16[2,4,16,256]{3,2,1,0:T(8,128)(2,1)S(1)}, bf16[2,4,16,256]{3,2,1,0:T(8,128)(2,1)S(1)}, u32[]{:S(2)}, u32[]{:S(2)}) %collective-permute-start) | collective-permute-done | bytes 65568 | tf_op jit(solution)/shard_map/ppermute | solution.py:10
  7.9 0.9 constant_dynamic-update-slice_fusion
  8.8 1.3 %collective-permute-start.2 = (bf16[6,1,16,256]{3,2,1,0:T(8,128)(2,1)S(1)}, bf16[6,1,16,256]{3,2,1,0:T(8,128)(2,1)S(1)}, u32[]{:S(2)}, u32[]{:S(2)}) collective-permute-start(bf16[6,1,16,256]{3,2,1,0:T(8,128)(2,1)S(1)} %get-tuple-element.128), channel_id=1, source_target_pairs={{4,0},{5,1},{6,2},{7,3},{12,8},{13,9},{14,10},{15,11},{20,16},{21,... | collective-permute-start | bytes 147464 | tf_op jit(solution)/shard_map/ppermute | solution.py:21
  10.1 3.0 %collective-permute-start.1 = (bf16[6,1,16,256]{3,2,1,0:T(8,128)(2,1)S(1)}, bf16[6,1,16,256]{3,2,1,0:T(8,128)(2,1)S(1)}, u32[]{:S(2)}, u32[]{:S(2)}) collective-permute-start(bf16[6,1,16,256]{3,2,1,0:T(8,128)(2,1)S(1)} %get-tuple-element.127), channel_id=1, source_target_pairs={{0,4},{1,5},{2,6},{3,7},{8,12},{9,13},{10,14},{11,15},{16,20},{17,... | collective-permute-start | bytes 147464 | tf_op jit(solution)/shard_map/ppermute | solution.py:20
  13.2 2.3 %fusion.13 = (bf16[3,1,1,256,256]{4,3,2,1,0:T(8,128)(2,1)S(1)}, bf16[3,1,1,256,256]{4,3,2,1,0:T(8,128)(2,1)S(1)}, bf16[3,1,1,256,256]{4,3,2,1,0:T(8,128)(2,1)S(1...) fusion(bf16[3,3,3,256,256]{4,3,2,1,0:T(8,128)(2,1)} %param.5), kind=kLoop, calls=%fused_computation.99 | loop fusion | bytes 7077888 | tf_op jit(solution)/shard_map/slice | solution.py:45
  15.6 2.4 %collective-permute-start.4 = (bf16[6,6,1,256]{3,2,1,0:T(2,128)(2,1)S(1)}, bf16[6,6,1,256]{3,2,1,0:T(2,128)(2,1)S(1)}, u32[]{:S(2)}, u32[]{:S(2)}) collective-permute-start(bf16[6,6,1,256]{3,2,1,0:T(2,128)(2,1)S(1)} %get-tuple-element.113), channel_id=1, source_target_pairs={{1,0},{2,1},{3,2},{5,4},{6,5},{7,6},{9,8},{10,9},{11,10},{13,12},{... | collective-permute-start | bytes 55304 | tf_op jit(solution)/shard_map/ppermute | solution.py:21
  18.0 1.3 %collective-permute-start.3 = (bf16[6,6,1,256]{3,2,1,0:T(2,128)(2,1)S(1)}, bf16[6,6,1,256]{3,2,1,0:T(2,128)(2,1)S(1)}, u32[]{:S(2)}, u32[]{:S(2)}) collective-permute-start(bf16[6,6,1,256]{3,2,1,0:T(2,128)(2,1)S(1)} %get-tuple-element.114), channel_id=1, source_target_pairs={{0,1},{1,2},{2,3},{4,5},{5,6},{6,7},{8,9},{9,10},{10,11},{12,13},{... | collective-permute-start | bytes 55304 | tf_op jit(solution)/shard_map/ppermute | solution.py:20
  19.6 4.2 %collective-permute-done.3 = bf16[6,6,1,256]{3,2,1,0:T(2,128)(2,1)S(1)} collective-permute-done((bf16[6,6,1,256]{3,2,1,0:T(2,128)(2,1)S(1)}, bf16[6,6,1,256]{3,2,1,0:T(2,128)(2,1)S(1)}, u32[]{:S(2)}, u32[]{:S(2)}) %collective-permute-start.3) | collective-permute-done | bytes 18464 | tf_op jit(solution)/shard_map/ppermute | solution.py:20
  27.1 2.6 %collective-permute-start.5 = (bf16[2,4,16,256]{3,2,1,0:T(8,128)(2,1)S(1)}, bf16[2,4,16,256]{3,2,1,0:T(8,128)(2,1)S(1)}, u32[]{:S(2)}, u32[]{:S(2)}) collective-permute-start(bf16[2,4,16,256]{3,2,1,0:T(8,128)(2,1)S(1)} %bitcast.177), channel_id=1, source_target_pairs={{0,8},{8,16},{16,24},{1,9},{9,17},{17,25},{2,10},{10,18},{18,26},{... | collective-permute-start | bytes 196616 | tf_op jit(solution)/shard_map/ppermute | solution.py:10
  29.7 4.6 %collective-permute-done.5 = bf16[2,4,16,256]{3,2,1,0:T(8,128)(2,1)S(1)} collective-permute-done((bf16[2,4,16,256]{3,2,1,0:T(8,128)(2,1)S(1)}, bf16[2,4,16,256]{3,2,1,0:T(8,128)(2,1)S(1)}, u32[]{:S(2)}, u32[]{:S(2)}) %collective-permute-start.5) | collective-permute-done | bytes 65568 | tf_op jit(solution)/shard_map/ppermute | solution.py:10
  34.3 1.3 %collective-permute-start.7 = (bf16[6,1,16,256]{3,2,1,0:T(8,128)(2,1)S(1)}, bf16[6,1,16,256]{3,2,1,0:T(8,128)(2,1)S(1)}, u32[]{:S(2)}, u32[]{:S(2)}) collective-permute-start(bf16[6,1,16,256]{3,2,1,0:T(8,128)(2,1)S(1)} %get-tuple-element.120), channel_id=1, source_target_pairs={{4,0},{5,1},{6,2},{7,3},{12,8},{13,9},{14,10},{15,11},{20,16},{21,... | collective-permute-start | bytes 147464 | tf_op jit(solution)/shard_map/ppermute | solution.py:21
  35.6 3.0 %collective-permute-start.6 = (bf16[6,1,16,256]{3,2,1,0:T(8,128)(2,1)S(1)}, bf16[6,1,16,256]{3,2,1,0:T(8,128)(2,1)S(1)}, u32[]{:S(2)}, u32[]{:S(2)}) collective-permute-start(bf16[6,1,16,256]{3,2,1,0:T(8,128)(2,1)S(1)} %get-tuple-element.119), channel_id=1, source_target_pairs={{0,4},{1,5},{2,6},{3,7},{8,12},{9,13},{10,14},{11,15},{16,20},{17,... | collective-permute-start | bytes 147464 | tf_op jit(solution)/shard_map/ppermute | solution.py:20
  38.7 0.9 collective-permute-done.6
  39.6 2.4 %collective-permute-start.9 = (bf16[6,6,1,256]{3,2,1,0:T(2,128)(2,1)S(1)}, bf16[6,6,1,256]{3,2,1,0:T(2,128)(2,1)S(1)}, u32[]{:S(2)}, u32[]{:S(2)}) collective-permute-start(bf16[6,6,1,256]{3,2,1,0:T(2,128)(2,1)S(1)} %get-tuple-element.110), channel_id=1, source_target_pairs={{1,0},{2,1},{3,2},{5,4},{6,5},{7,6},{9,8},{10,9},{11,10},{13,12},{... | collective-permute-start | bytes 55304 | tf_op jit(solution)/shard_map/ppermute | solution.py:21
  41.9 1.5 %collective-permute-start.8 = (bf16[6,6,1,256]{3,2,1,0:T(2,128)(2,1)S(1)}, bf16[6,6,1,256]{3,2,1,0:T(2,128)(2,1)S(1)}, u32[]{:S(2)}, u32[]{:S(2)}) collective-permute-start(bf16[6,6,1,256]{3,2,1,0:T(2,128)(2,1)S(1)} %get-tuple-element.109), channel_id=1, source_target_pairs={{0,1},{1,2},{2,3},{4,5},{5,6},{6,7},{8,9},{9,10},{10,11},{12,13},{... | collective-permute-start | bytes 55304 | tf_op jit(solution)/shard_map/ppermute | solution.py:20
  43.4 1.0 %fusion.14 = (bf16[3,1,1,256,128]{4,3,2,1,0:T(8,128)(2,1)S(1)}, bf16[3,1,1,256,128]{4,3,2,1,0:T(8,128)(2,1)}, bf16[3,1,1,256,128]{4,3,2,1,0:T(8,128)(2,1)}, bf16...) fusion(bf16[3,3,3,256,128]{4,3,2,1,0:T(8,128)(2,1)S(1)} %copy-done), kind=kLoop, calls=%fused_computation.100 | loop fusion | bytes 3538944 | tf_op jit(solution)/shard_map/slice | solution.py:45
  44.5 3.3 %collective-permute-done.8 = bf16[6,6,1,256]{3,2,1,0:T(2,128)(2,1)S(1)} collective-permute-done((bf16[6,6,1,256]{3,2,1,0:T(2,128)(2,1)S(1)}, bf16[6,6,1,256]{3,2,1,0:T(2,128)(2,1)S(1)}, u32[]{:S(2)}, u32[]{:S(2)}) %collective-permute-start.8) | collective-permute-done | bytes 18464 | tf_op jit(solution)/shard_map/ppermute | solution.py:20
  48.1 0.7 broadcast_in_dim.2
  48.8 0.6 reshape.104
  49.6 0.6 fusion.16
  50.3 2.6 %fusion.15 = (bf16[4,8,32,256]{3,2,1,0:T(8,128)(2,1)S(1)}, bf16[4,8,32,256]{3,2,1,0:T(8,128)(2,1)S(1)}, bf16[4,8,32,256]{3,2,1,0:T(8,128)(2,1)S(1)}, bf16[4,8,32...) fusion(bf16[6,10,34,256]{3,2,1,0:T(8,128)(2,1)S(1)} %slice_maxi, ...), kind=kLoop, calls=%fused_computation.101 | loop fusion | bytes 19922944 | tf_op jit(solution)/shard_map/slice | solution.py:43
  53.0 0.6 fusion.26
  53.7 0.8 copy-done.8
  54.5 0.6 convolution_add_fusion.15
  55.2 0.8 copy-done.7
  56.1 0.6 convolution_add_fusion.14
  56.8 0.8 copy-done.6
  57.6 0.6 convolution_add_fusion.13
  58.3 0.8 copy-done.5
  59.1 0.6 convolution_add_fusion.12
  59.8 0.8 copy-done.4
  60.6 0.6 convolution_add_fusion.11
  61.3 0.8 copy-done.3
  62.1 0.6 convolution_add_fusion.10
  62.8 0.6 convolution_add_fusion.9
  63.5 0.6 fusion.1
  64.1 1.9 %collective-permute-start.10 = (bf16[2,8,32,128]{3,2,1,0:T(8,128)(2,1)S(1)}, bf16[2,8,32,128]{3,2,1,0:T(8,128)(2,1)S(1)}, u32[]{:S(2)}, u32[]{:S(2)}) collective-permute-start(bf16[2,8,32,128]{3,2,1,0:T(8,128)(2,1)S(1)} %bitcast.176), channel_id=1, source_target_pairs={{0,8},{8,16},{16,24},{1,9},{9,17},{17,25},{2,10},{10,18},{18,26},{... | collective-permute-start | bytes 393224 | tf_op jit(solution)/shard_map/ppermute | solution.py:10
  66.1 5.7 %collective-permute-done.10 = bf16[2,8,32,128]{3,2,1,0:T(8,128)(2,1)S(1)} collective-permute-done((bf16[2,8,32,128]{3,2,1,0:T(8,128)(2,1)S(1)}, bf16[2,8,32,128]{3,2,1,0:T(8,128)(2,1)S(1)}, u32[]{:S(2)}, u32[]{:S(2)}) %collective-permute-start.10) | collective-permute-done | bytes 131104 | tf_op jit(solution)/shard_map/ppermute | solution.py:10
  71.9 1.3 %collective-permute-start.12 = (bf16[6,1,32,128]{3,2,1,0:T(8,128)(2,1)S(1)}, bf16[6,1,32,128]{3,2,1,0:T(8,128)(2,1)S(1)}, u32[]{:S(2)}, u32[]{:S(2)}) collective-permute-start(bf16[6,1,32,128]{3,2,1,0:T(8,128)(2,1)S(1)} %get-tuple-element.108), channel_id=1, source_target_pairs={{4,0},{5,1},{6,2},{7,3},{12,8},{13,9},{14,10},{15,11},{20,16},{21,... | collective-permute-start | bytes 147464 | tf_op jit(solution)/shard_map/ppermute | solution.py:21
  73.2 3.0 %collective-permute-start.11 = (bf16[6,1,32,128]{3,2,1,0:T(8,128)(2,1)S(1)}, bf16[6,1,32,128]{3,2,1,0:T(8,128)(2,1)S(1)}, u32[]{:S(2)}, u32[]{:S(2)}) collective-permute-start(bf16[6,1,32,128]{3,2,1,0:T(8,128)(2,1)S(1)} %get-tuple-element.107), channel_id=1, source_target_pairs={{0,4},{1,5},{2,6},{3,7},{8,12},{9,13},{10,14},{11,15},{16,20},{17,... | collective-permute-start | bytes 147464 | tf_op jit(solution)/shard_map/ppermute | solution.py:20
  76.3 0.7 collective-permute-done.11
  77.1 2.4 %collective-permute-start.14 = (bf16[6,10,1,128]{3,2,1,0:T(2,128)(2,1)S(1)}, bf16[6,10,1,128]{3,2,1,0:T(2,128)(2,1)S(1)}, u32[]{:S(2)}, u32[]{:S(2)}) collective-permute-start(bf16[6,10,1,128]{3,2,1,0:T(2,128)(2,1)S(1)} %get-tuple-element.79), channel_id=1, source_target_pairs={{1,0},{2,1},{3,2},{5,4},{6,5},{7,6},{9,8},{10,9},{11,10},{13,12},{... | collective-permute-start | bytes 46088 | tf_op jit(solution)/shard_map/ppermute | solution.py:21
  79.5 1.5 %collective-permute-start.13 = (bf16[6,10,1,128]{3,2,1,0:T(2,128)(2,1)S(1)}, bf16[6,10,1,128]{3,2,1,0:T(2,128)(2,1)S(1)}, u32[]{:S(2)}, u32[]{:S(2)}) collective-permute-start(bf16[6,10,1,128]{3,2,1,0:T(2,128)(2,1)S(1)} %get-tuple-element.80), channel_id=1, source_target_pairs={{0,1},{1,2},{2,3},{4,5},{5,6},{6,7},{8,9},{9,10},{10,11},{12,13},{... | collective-permute-start | bytes 46088 | tf_op jit(solution)/shard_map/ppermute | solution.py:20
  81.6 3.7 %collective-permute-done.13 = bf16[6,10,1,128]{3,2,1,0:T(2,128)(2,1)S(1)} collective-permute-done((bf16[6,10,1,128]{3,2,1,0:T(2,128)(2,1)S(1)}, bf16[6,10,1,128]{3,2,1,0:T(2,128)(2,1)S(1)}, u32[]{:S(2)}, u32[]{:S(2)}) %collective-permute-start.13) | collective-permute-done | bytes 15392 | tf_op jit(solution)/shard_map/ppermute | solution.py:20
  86.1 0.5 fusion.18
  90.3 1.1 %fusion.2 = bf16[1024,128]{1,0:T(8,128)(2,1)} fusion(f32[1024,128]{1,0:T(8,128)S(1)} %convolution_add_fusion.1, bf16[1024,384]{1,0:T(8,128)(2,1)S(1)} %bitcast.128, bf16[384,128]{1,0:T(8,128)(2,1)S(1)} %bitcast.167), kind=kOutput, calls=%fused_computation.28 | convolution fusion | flops 100925440 | bytes 1671168 | tf_op jit(solution)/shard_map/dot_general | solution.py:46
  (82 shorter events, 10.4 us)
Async XLA Ops:
  0.8 7.0 %collective-permute-start = (bf16[2,4,16,256]{3,2,1,0:T(8,128)(2,1)S(1)}, bf16[2,4,16,256]{3,2,1,0:T(8,128)(2,1)S(1)}, u32[]{:S(2)}, u32[]{:S(2)}) collective-permute-start(bf16[2,4,16,256]{3,2,1,0:T(8,128)(2,1)S(1)} %slice.488), channel_id=1, source_target_pairs={{0,8},{8,16},{16,24},{1,9},{9,17},{17,25},{2,10},{10,18},{18,26},{... | collective-permute-start | bytes 196616 | tf_op jit(solution)/shard_map/ppermute | solution.py:10
  8.8 6.7 %collective-permute-start.2 = (bf16[6,1,16,256]{3,2,1,0:T(8,128)(2,1)S(1)}, bf16[6,1,16,256]{3,2,1,0:T(8,128)(2,1)S(1)}, u32[]{:S(2)}, u32[]{:S(2)}) collective-permute-start(bf16[6,1,16,256]{3,2,1,0:T(8,128)(2,1)S(1)} %get-tuple-element.128), channel_id=1, source_target_pairs={{4,0},{5,1},{6,2},{7,3},{12,8},{13,9},{14,10},{15,11},{20,16},{21,... | collective-permute-start | bytes 147464 | tf_op jit(solution)/shard_map/ppermute | solution.py:21
  10.1 5.4 %collective-permute-start.1 = (bf16[6,1,16,256]{3,2,1,0:T(8,128)(2,1)S(1)}, bf16[6,1,16,256]{3,2,1,0:T(8,128)(2,1)S(1)}, u32[]{:S(2)}, u32[]{:S(2)}) collective-permute-start(bf16[6,1,16,256]{3,2,1,0:T(8,128)(2,1)S(1)} %get-tuple-element.127), channel_id=1, source_target_pairs={{0,4},{1,5},{2,6},{3,7},{8,12},{9,13},{10,14},{11,15},{16,20},{17,... | collective-permute-start | bytes 147464 | tf_op jit(solution)/shard_map/ppermute | solution.py:20
  15.5 3.8 %copy-start.2 = (bf16[4,4,16,256]{3,2,1,0:T(8,128)(2,1)S(1)}, bf16[4,4,16,256]{3,2,1,0:T(8,128)(2,1)}, u32[]{:S(2)}) copy-start(bf16[4,4,16,256]{3,2,1,0:T(8,128)(2,1)} %param.4) | copy-start | bytes 393220
  15.6 4.0 %collective-permute-start.4 = (bf16[6,6,1,256]{3,2,1,0:T(2,128)(2,1)S(1)}, bf16[6,6,1,256]{3,2,1,0:T(2,128)(2,1)S(1)}, u32[]{:S(2)}, u32[]{:S(2)}) collective-permute-start(bf16[6,6,1,256]{3,2,1,0:T(2,128)(2,1)S(1)} %get-tuple-element.113), channel_id=1, source_target_pairs={{1,0},{2,1},{3,2},{5,4},{6,5},{7,6},{9,8},{10,9},{11,10},{13,12},{... | collective-permute-start | bytes 55304 | tf_op jit(solution)/shard_map/ppermute | solution.py:21
  18.0 5.9 %collective-permute-start.3 = (bf16[6,6,1,256]{3,2,1,0:T(2,128)(2,1)S(1)}, bf16[6,6,1,256]{3,2,1,0:T(2,128)(2,1)S(1)}, u32[]{:S(2)}, u32[]{:S(2)}) collective-permute-start(bf16[6,6,1,256]{3,2,1,0:T(2,128)(2,1)S(1)} %get-tuple-element.114), channel_id=1, source_target_pairs={{0,1},{1,2},{2,3},{4,5},{5,6},{6,7},{8,9},{9,10},{10,11},{12,13},{... | collective-permute-start | bytes 55304 | tf_op jit(solution)/shard_map/ppermute | solution.py:20
  26.8 16.7 %copy-start = (bf16[3,3,3,256,128]{4,3,2,1,0:T(8,128)(2,1)S(1)}, bf16[3,3,3,256,128]{4,3,2,1,0:T(8,128)(2,1)}, u32[]{:S(2)}) copy-start(bf16[3,3,3,256,128]{4,3,2,1,0:T(8,128)(2,1)} %param.6) | copy-start | bytes 5308420
  27.1 7.2 %collective-permute-start.5 = (bf16[2,4,16,256]{3,2,1,0:T(8,128)(2,1)S(1)}, bf16[2,4,16,256]{3,2,1,0:T(8,128)(2,1)S(1)}, u32[]{:S(2)}, u32[]{:S(2)}) collective-permute-start(bf16[2,4,16,256]{3,2,1,0:T(8,128)(2,1)S(1)} %bitcast.177), channel_id=1, source_target_pairs={{0,8},{8,16},{16,24},{1,9},{9,17},{17,25},{2,10},{10,18},{18,26},{... | collective-permute-start | bytes 196616 | tf_op jit(solution)/shard_map/ppermute | solution.py:10
  34.3 4.3 %collective-permute-start.7 = (bf16[6,1,16,256]{3,2,1,0:T(8,128)(2,1)S(1)}, bf16[6,1,16,256]{3,2,1,0:T(8,128)(2,1)S(1)}, u32[]{:S(2)}, u32[]{:S(2)}) collective-permute-start(bf16[6,1,16,256]{3,2,1,0:T(8,128)(2,1)S(1)} %get-tuple-element.120), channel_id=1, source_target_pairs={{4,0},{5,1},{6,2},{7,3},{12,8},{13,9},{14,10},{15,11},{20,16},{21,... | collective-permute-start | bytes 147464 | tf_op jit(solution)/shard_map/ppermute | solution.py:21
  35.6 3.9 %collective-permute-start.6 = (bf16[6,1,16,256]{3,2,1,0:T(8,128)(2,1)S(1)}, bf16[6,1,16,256]{3,2,1,0:T(8,128)(2,1)S(1)}, u32[]{:S(2)}, u32[]{:S(2)}) collective-permute-start(bf16[6,1,16,256]{3,2,1,0:T(8,128)(2,1)S(1)} %get-tuple-element.119), channel_id=1, source_target_pairs={{0,4},{1,5},{2,6},{3,7},{8,12},{9,13},{10,14},{11,15},{16,20},{17,... | collective-permute-start | bytes 147464 | tf_op jit(solution)/shard_map/ppermute | solution.py:20
  39.6 4.9 %collective-permute-start.9 = (bf16[6,6,1,256]{3,2,1,0:T(2,128)(2,1)S(1)}, bf16[6,6,1,256]{3,2,1,0:T(2,128)(2,1)S(1)}, u32[]{:S(2)}, u32[]{:S(2)}) collective-permute-start(bf16[6,6,1,256]{3,2,1,0:T(2,128)(2,1)S(1)} %get-tuple-element.110), channel_id=1, source_target_pairs={{1,0},{2,1},{3,2},{5,4},{6,5},{7,6},{9,8},{10,9},{11,10},{13,12},{... | collective-permute-start | bytes 55304 | tf_op jit(solution)/shard_map/ppermute | solution.py:21
  41.9 5.9 %collective-permute-start.8 = (bf16[6,6,1,256]{3,2,1,0:T(2,128)(2,1)S(1)}, bf16[6,6,1,256]{3,2,1,0:T(2,128)(2,1)S(1)}, u32[]{:S(2)}, u32[]{:S(2)}) collective-permute-start(bf16[6,6,1,256]{3,2,1,0:T(2,128)(2,1)S(1)} %get-tuple-element.109), channel_id=1, source_target_pairs={{0,1},{1,2},{2,3},{4,5},{5,6},{6,7},{8,9},{9,10},{10,11},{12,13},{... | collective-permute-start | bytes 55304 | tf_op jit(solution)/shard_map/ppermute | solution.py:20
  53.6 0.9 %copy-start.8 = (bf16[3,1,1,256,128]{4,3,2,1,0:T(8,128)(2,1)S(1)}, bf16[3,1,1,256,128]{4,3,2,1,0:T(8,128)(2,1)}, u32[]{:S(2)}) copy-start(bf16[3,1,1,256,128]{4,3,2,1,0:T(8,128)(2,1)} %get-tuple-element.20) | copy-start | bytes 589828
  55.1 0.9 %copy-start.7 = (bf16[3,1,1,256,128]{4,3,2,1,0:T(8,128)(2,1)S(1)}, bf16[3,1,1,256,128]{4,3,2,1,0:T(8,128)(2,1)}, u32[]{:S(2)}) copy-start(bf16[3,1,1,256,128]{4,3,2,1,0:T(8,128)(2,1)} %get-tuple-element.19) | copy-start | bytes 589828
  56.6 0.9 %copy-start.6 = (bf16[3,1,1,256,128]{4,3,2,1,0:T(8,128)(2,1)S(1)}, bf16[3,1,1,256,128]{4,3,2,1,0:T(8,128)(2,1)}, u32[]{:S(2)}) copy-start(bf16[3,1,1,256,128]{4,3,2,1,0:T(8,128)(2,1)} %get-tuple-element.18) | copy-start | bytes 589828
  58.1 0.9 %copy-start.5 = (bf16[3,1,1,256,128]{4,3,2,1,0:T(8,128)(2,1)S(1)}, bf16[3,1,1,256,128]{4,3,2,1,0:T(8,128)(2,1)}, u32[]{:S(2)}) copy-start(bf16[3,1,1,256,128]{4,3,2,1,0:T(8,128)(2,1)} %get-tuple-element.17) | copy-start | bytes 589828
  59.6 0.9 %copy-start.4 = (bf16[3,1,1,256,128]{4,3,2,1,0:T(8,128)(2,1)S(1)}, bf16[3,1,1,256,128]{4,3,2,1,0:T(8,128)(2,1)}, u32[]{:S(2)}) copy-start(bf16[3,1,1,256,128]{4,3,2,1,0:T(8,128)(2,1)} %get-tuple-element.16) | copy-start | bytes 589828
  61.2 0.9 %copy-start.3 = (bf16[3,1,1,256,128]{4,3,2,1,0:T(8,128)(2,1)S(1)}, bf16[3,1,1,256,128]{4,3,2,1,0:T(8,128)(2,1)}, u32[]{:S(2)}) copy-start(bf16[3,1,1,256,128]{4,3,2,1,0:T(8,128)(2,1)} %get-tuple-element.15) | copy-start | bytes 589828
  63.5 2.6 %copy-start.1 = (bf16[3,3,3,128,128]{4,3,2,1,0:T(8,128)(2,1)S(1)}, bf16[3,3,3,128,128]{4,3,2,1,0:T(8,128)(2,1)}, u32[]{:S(2)}) copy-start(bf16[3,3,3,128,128]{4,3,2,1,0:T(8,128)(2,1)} %param.7) | copy-start | bytes 2654212
  64.1 7.8 %collective-permute-start.10 = (bf16[2,8,32,128]{3,2,1,0:T(8,128)(2,1)S(1)}, bf16[2,8,32,128]{3,2,1,0:T(8,128)(2,1)S(1)}, u32[]{:S(2)}, u32[]{:S(2)}) collective-permute-start(bf16[2,8,32,128]{3,2,1,0:T(8,128)(2,1)S(1)} %bitcast.176), channel_id=1, source_target_pairs={{0,8},{8,16},{16,24},{1,9},{9,17},{17,25},{2,10},{10,18},{18,26},{... | collective-permute-start | bytes 393224 | tf_op jit(solution)/shard_map/ppermute | solution.py:10
  71.9 4.5 %collective-permute-start.12 = (bf16[6,1,32,128]{3,2,1,0:T(8,128)(2,1)S(1)}, bf16[6,1,32,128]{3,2,1,0:T(8,128)(2,1)S(1)}, u32[]{:S(2)}, u32[]{:S(2)}) collective-permute-start(bf16[6,1,32,128]{3,2,1,0:T(8,128)(2,1)S(1)} %get-tuple-element.108), channel_id=1, source_target_pairs={{4,0},{5,1},{6,2},{7,3},{12,8},{13,9},{14,10},{15,11},{20,16},{21,... | collective-permute-start | bytes 147464 | tf_op jit(solution)/shard_map/ppermute | solution.py:21
  73.2 3.9 %collective-permute-start.11 = (bf16[6,1,32,128]{3,2,1,0:T(8,128)(2,1)S(1)}, bf16[6,1,32,128]{3,2,1,0:T(8,128)(2,1)S(1)}, u32[]{:S(2)}, u32[]{:S(2)}) collective-permute-start(bf16[6,1,32,128]{3,2,1,0:T(8,128)(2,1)S(1)} %get-tuple-element.107), channel_id=1, source_target_pairs={{0,4},{1,5},{2,6},{3,7},{8,12},{9,13},{10,14},{11,15},{16,20},{17,... | collective-permute-start | bytes 147464 | tf_op jit(solution)/shard_map/ppermute | solution.py:20
  77.1 4.5 %collective-permute-start.14 = (bf16[6,10,1,128]{3,2,1,0:T(2,128)(2,1)S(1)}, bf16[6,10,1,128]{3,2,1,0:T(2,128)(2,1)S(1)}, u32[]{:S(2)}, u32[]{:S(2)}) collective-permute-start(bf16[6,10,1,128]{3,2,1,0:T(2,128)(2,1)S(1)} %get-tuple-element.79), channel_id=1, source_target_pairs={{1,0},{2,1},{3,2},{5,4},{6,5},{7,6},{9,8},{10,9},{11,10},{13,12},{... | collective-permute-start | bytes 46088 | tf_op jit(solution)/shard_map/ppermute | solution.py:21
  79.5 5.8 %collective-permute-start.13 = (bf16[6,10,1,128]{3,2,1,0:T(2,128)(2,1)S(1)}, bf16[6,10,1,128]{3,2,1,0:T(2,128)(2,1)S(1)}, u32[]{:S(2)}, u32[]{:S(2)}) collective-permute-start(bf16[6,10,1,128]{3,2,1,0:T(2,128)(2,1)S(1)} %get-tuple-element.80), channel_id=1, source_target_pairs={{0,1},{1,2},{2,3},{4,5},{5,6},{6,7},{8,9},{9,10},{10,11},{12,13},{... | collective-permute-start | bytes 46088 | tf_op jit(solution)/shard_map/ppermute | solution.py:20
where the time goes:
time: 92.1 us; the launch traced here: 91.4 us
  starting transfers between devices  32.3 us (35%)
  waiting for transfers between devices  26.9 us (29%)
  local copies, waits for them, and re-layouts  16 us (17%)
  matrix products  11.6 us (13%)
  other arithmetic  3.8 us (4%)
    ppermute x3, waiting for transfers between devices, shifted(): return lax.ppermute(x, axis, pairs)  13.9 us
    ppermute x6, starting transfers between devices, extended_2(): before = lax.ppermute(last, axis, up)  13.4 us
    ppermute x6, waiting for transfers between devices, extended_2(): before = lax.ppermute(last, axis, up)  12.8 us
    dot_general x27, matrix products, causal_conv(): jnp.dot(stacked.reshape(-1, 3 * in_width), tap_matrix, preferred_element_...  11.6 us
    ppermute x6, starting transfers between devices, extended_2(): after = lax.ppermute(leading, axis, down)  11 us
    ppermute x3, starting transfers between devices, shifted(): return lax.ppermute(x, axis, pairs)  7.94 us
    unnamed x19, local copies, waits for them, and re-layouts  4.88 us
    slice x7, local copies, waits for them, and re-layouts, causal_conv(): window[0:frames]  4.67 us
  transfers between devices with their start and end apart: 15, of which 9 were waited for; matrix products, arithmetic and copies ran while one was open for 5% of the time, Pallas kernels for 0%

commit v1 on v0

v1 whole, which is shorter than its diff:
```python
import jax
import jax.numpy as jnp
from jax import lax
from jax.sharding import PartitionSpec as P


def ring(x, axis, by):
    size = lax.axis_size(axis)
    return lax.ppermute(x, axis, [(i, (i + by) % size) for i in range(size)])


def earlier_frames(x, count):
    size, length = lax.axis_size("section"), x.shape[0]
    place = lax.axis_index("section")
    pieces, by, left = [], 1, count
    while left > 0:
        take = min(left, length)
        got = ring(x[length - take :], "section", by % size)
        pieces.insert(0, jnp.where(place >= by, got, 0))
        left -= take
        by += 1
    return pieces


def edges(x, axis, dim, width):
    size, length = lax.axis_size(axis), x.shape[dim]
    place = lax.axis_index(axis)
    first = lax.slice_in_dim(x, 0, width, axis=dim)
    last = lax.slice_in_dim(x, length - width, length, axis=dim)
    if size % 2:
        before, after = ring(last, axis, 1), ring(first, axis, size - 1)
    else:
        even = place % 2 == 0
        pairs = [(i, i + 1) for i in range(0, size, 2)]
        swap = pairs + [(j, i) for i, j in pairs]
        got = lax.ppermute(jnp.where(even, last, first), axis, swap)
        if size == 2:
            before = after = got
        else:
            pairs = [(i, (i + 1) % size) for i in range(1, size, 2)]
            swap = pairs + [(j, i) for i, j in pairs]
            other = lax.ppermute(jnp.where(even, first, last), axis, swap)
            before = jnp.where(even, other, got)
            after = jnp.where(even, got, other)
    before = jnp.where(place > 0, before, 0)
    after = jnp.where(place < size - 1, after, 0)
    return before, after


def inside(shape, axis, dim, low, count):
    place = lax.axis_index(axis) * count + low + lax.broadcasted_iota(jnp.int32, shape, dim)
    return (place >= 0) & (place < lax.axis_size(axis) * count)


def conv(x, kernel):
    return lax.conv_general_dilated(
        x[None], kernel, (1, 1, 1), "VALID",
        dimension_numbers=("NDHWC", "DHWIO", "NDHWC"), preferred_element_type=jnp.float32,
    )[0]


def corner_kernel(kernel, dim):
    k = [lax.index_in_dim(kernel, i, dim, keepdims=False) for i in range(3)]
    return [[k[0] + k[1], k[2]], [k[0], k[1] + k[2]]]


def second_kernel(kernel):
    kernel = kernel.astype(jnp.float32)
    rows = corner_kernel(kernel, 1)
    outs = []
    for py in range(2):
        for px in range(2):
            taps = jnp.stack(
                [jnp.stack(corner_kernel(rows[py][di], 1)[px], 1) for di in range(2)], 1
            )
            outs.append(taps)
    return jnp.concatenate(outs, -1).astype(jnp.bfloat16)


def third_kernel(kernel):
    zero = jnp.zeros_like(kernel[:, 0, 0])
    rows = []
    for di in range(2):
        cols = []
        for dj in range(2):
            ins = []
            for py in range(2):
                for px in range(2):
                    outs = []
                    for qy in range(2):
                        for qx in range(2):
                            b, e = 2 * di + py - qy, 2 * dj + px - qx
                            outs.append(kernel[:, b, e] if 0 <= b < 3 and 0 <= e < 3 else zero)
                    ins.append(jnp.concatenate(outs, -1))
            cols.append(jnp.concatenate(ins, -2))
        rows.append(jnp.stack(cols, 1))
    return jnp.stack(rows, 1)


def per_device(latent, w_first, w_second, w_third):
    height, breadth = latent.shape[1:3]
    x = jnp.concatenate([*earlier_frames(latent, 6), latent], 0)
    before, after = edges(x, "row", 1, 2)
    x = jnp.concatenate([before, x, after], 1)
    before, after = edges(x, "col", 2, 2)
    x = jnp.concatenate([before, x, after], 2)
    first = jnp.maximum(conv(x, w_first).astype(jnp.bfloat16), 0)
    keep = inside(first.shape, "row", 1, -1, height) & inside(first.shape, "col", 2, -1, breadth)
    first = jnp.where(keep, first, 0)
    second = jnp.maximum(conv(first, second_kernel(w_second)), 0.0).astype(jnp.bfloat16)
    width = second.shape[-1] // 4
    part = lax.broadcasted_iota(jnp.int32, second.shape, 3) // width
    row = 2 * lax.broadcasted_iota(jnp.int32, second.shape, 1) + part // 2 - 1
    col = 2 * lax.broadcasted_iota(jnp.int32, second.shape, 2) + part % 2 - 1
    row += lax.axis_index("row") * 2 * height
    col += lax.axis_index("col") * 2 * breadth
    keep = (row >= 0) & (row < 2 * height * lax.axis_size("row"))
    keep &= (col >= 0) & (col < 2 * breadth * lax.axis_size("col"))
    second = jnp.where(keep, second, 0)
    out = conv(second, third_kernel(w_third)).astype(jnp.bfloat16)
    frames, width = out.shape[0], w_third.shape[-1]
    out = out.reshape(frames, height, breadth, 2, 2, width).transpose(0, 1, 3, 2, 4, 5)
    return out.reshape(frames, 2 * height, 2 * breadth, width)


def solution(mesh):
    in_specs = (P("section", "row", "col", None), P(), P(), P())
    out_specs = P("section", "row", "col", None)
    return jax.shard_map(
        per_device, mesh=mesh, in_specs=in_specs, out_specs=out_specs, check_vma=False
    )
```

time: 92.1 us -> 71.6 us (0.78)
  the two profiles are of different devices: /device:TPU:28 before, /device:TPU:0 now
where the time goes in v1:
time: 71.6 us; the launch traced here: 70.9 us
  local copies, waits for them, and re-layouts  24.9 us (35%)
  other arithmetic  20.5 us (29%)
  matrix products  11.7 us (16%)
  starting transfers between devices  8.67 us (12%)
  waiting for transfers between devices  4.67 us (7%)
    conv_general_dilated x3, matrix products, conv(): lax.conv_general_dilated(x[None], kernel, (1, 1, 1), 'VALID', dimension_n...  11.7 us
    another operation x4, other arithmetic, third_kernel(): rows.append(jnp.stack(cols, 1))  7.67 us
    conv_general_dilated x7, local copies, waits for them, and re-layouts, conv(): lax.conv_general_dilated(x[None], kernel, (1, 1, 1), 'VALID', dimension_n...  5.29 us
    convert_element_type x2, local copies, waits for them, and re-layouts, per_device(): jnp.maximum(conv(first, second_kernel(w_second)), 0.0).astype(jnp.bfloat16)  4.54 us
    ppermute x2, starting transfers between devices, ring(): return lax.ppermute(x, axis, [(i, (i + by) % size) for i in range(size)])  4.49 us
    unnamed x43, local copies, waits for them, and re-layouts  4.24 us
    ppermute x1, waiting for transfers between devices, edges(): other = lax.ppermute(jnp.where(even, first, last), axis, swap)  3.88 us
    convert_element_type x3, local copies, waits for them, and re-layouts, per_device(): out = conv(second, third_kernel(w_third)).astype(jnp.bfloat16)  2.74 us
  transfers between devices with their start and end apart: 5, of which 2 were waited for; matrix products, arithmetic and copies ran while one was open for 28% of the time, Pallas kernels for 0%

profile of v1, /device:TPU:0, one launch (start us, length us, event | category | flops | bytes accessed | tf_op | source)
XLA Modules:
  0.0 70.9 jit_solution(15890498055971437791)
XLA Ops:
  0.0 1.8 %copy.50 = bf16[4,4,16,256]{3,1,2,0:T(4,128)(2,1)} copy(bf16[4,4,16,256]{3,2,1,0:T(8,128)(2,1)} %param.4) | data formatting | bytes 262144 | tf_op args[0]
  1.8 3.0 %collective-permute-start.1 = (bf16[4,4,16,256]{3,1,2,0:T(4,128)(2,1)}, bf16[4,4,16,256]{3,1,2,0:T(4,128)(2,1)}, u32[]{:S(2)}, u32[]{:S(2)}) collective-permute-start(bf16[4,4,16,256]{3,1,2,0:T(4,128)(2,1)} %copy.50), channel_id=1, source_target_pairs={{0,8},{8,16},{16,24},{24,0},{1,9},{9,17},{17,25},{25,1},{2,10},{10... | collective-permute-start | bytes 393224 | tf_op jit(solution)/shard_map/ppermute | solution.py:9
  4.7 1.5 %slice.161 = bf16[2,4,16,256]{3,1,2,0:T(4,128)(2,1)} slice(bf16[4,4,16,256]{3,1,2,0:T(4,128)(2,1)} %copy.50), slice={[2:4], [0:4], [0:16], [0:256]} | slice | bytes 131072 | tf_op jit(solution)/shard_map/slice | solution.py:18
  6.3 1.5 %collective-permute-start = (bf16[2,4,16,256]{3,1,2,0:T(4,128)(2,1)}, bf16[2,4,16,256]{3,1,2,0:T(4,128)(2,1)}, u32[]{:S(2)}, u32[]{:S(2)}) collective-permute-start(bf16[2,4,16,256]{3,1,2,0:T(4,128)(2,1)} %slice.161), channel_id=1, source_target_pairs={{0,16},{8,24},{16,0},{24,8},{1,17},{9,25},{17,1},{25,9},{2,18},{10... | collective-permute-start | bytes 196616 | tf_op jit(solution)/shard_map/ppermute | solution.py:9
  7.8 1.9 %copy_convert_fusion = f32[3,3,3,256,128]{4,3,2,0,1:T(8,128)S(1)} fusion(bf16[3,3,3,256,128]{4,3,2,1,0:T(8,128)(2,1)} %param.6), kind=kLoop, calls=%fused_computation.40 | loop fusion | flops 884736 | bytes 5308416 | tf_op jit(solution)/shard_map/convert_element_type | solution.py:68
  9.7 0.3 fusion.72
  9.9 0.9 %fusion.102 = (bf16[3,1,256,128]{3,2,1,0:T(8,128)(2,1)}, bf16[3,1,256,128]{3,2,1,0:T(8,128)(2,1)}, bf16[3,1,256,128]{3,2,1,0:T(8,128)(2,1)}, bf16[3,1,256,128]{3,2,1,0:T(8,128)(2,1)}) fusion(f32[3,3,256,128]{3,2,1,0:T(8,128)S(1)} %get-tuple-element.8, f32[3,3,256,128]{3,2,1,0:T(8,128)S(1)} %get-tuple-element.9), kind=kLoop, calls=%fused_computation.179 | loop fusion | bytes 1572864 | tf_op jit(solution)/shard_map/slice | solution.py:63
  10.8 0.9 %add_convert_fusion.2 = (bf16[3,1,256,128]{3,2,1,0:T(8,128)(2,1)}, bf16[3,1,256,128]{3,2,1,0:T(8,128)(2,1)}, bf16[3,1,256,128]{3,2,1,0:T(8,128)(2,1)}, bf16[3,1,256,128]{3,2,1,0:T(8,128)(2,1)}) fusion(f32[3,3,256,128]{3,2,1,0:T(8,128)S(1)} %get-tuple-element.9, f32[3,3,256,128]{3,2,1,0:T(8,128)S(1)} %get-tuple-element.8), kind=kLoop, calls=%fused_computation.121 | loop fusion | flops 786432 | bytes 3145728 | tf_op jit(solution)/shard_map/convert.15
  11.8 0.2 slice_bitcast_fusion
  12.0 0.9 %fusion.103 = (bf16[3,1,256,128]{3,2,1,0:T(8,128)(2,1)}, bf16[3,1,256,128]{3,2,1,0:T(8,128)(2,1)}, bf16[3,1,256,128]{3,2,1,0:T(8,128)(2,1)}, bf16[3,1,256,128]{3,2,1,0:T(8,128)(2,1)}) fusion(f32[3,3,256,128]{3,2,1,0:T(8,128)S(1)} %get-tuple-element.10, f32[3,3,256,128]{3,2,1,0:T(8,128)S(1)} %get-tuple-element.11), kind=kLoop, calls=%fused_computation.180 | loop fusion | bytes 1572864 | tf_op jit(solution)/shard_map/slice | solution.py:63
  12.9 1.0 %add_convert_fusion.3 = (bf16[3,1,256,128]{3,2,1,0:T(8,128)(2,1)}, bf16[3,1,256,128]{3,2,1,0:T(8,128)(2,1)}, bf16[3,1,256,128]{3,2,1,0:T(8,128)(2,1)}, bf16[3,1,256,128]{3,2,1,0:T(8,128)(2,1)}) fusion(f32[3,3,256,128]{3,2,1,0:T(8,128)S(1)} %get-tuple-element.11, f32[3,3,256,128]{3,2,1,0:T(8,128)S(1)} %get-tuple-element.10), kind=kLoop, calls=%fused_computation.122 | loop fusion | flops 786432 | bytes 3145728 | tf_op jit(solution)/shard_map/convert.18
  13.9 0.6 iota_multiply_fusion.1
  14.5 1.3 %slice_bitcast_fusion.13 = (bf16[3,128,128]{2,1,0:T(8,128)(2,1)S(1)}, bf16[3,128,128]{2,1,0:T(8,128)(2,1)S(1)}, bf16[3,128,128]{2,1,0:T(8,128)(2,1)S(1)}, bf16[3...) fusion(bf16[3,3,3,128,128]{4,3,2,1,0:T(8,128)(2,1)} %param.7), kind=kLoop, calls=%fused_computation.148 | loop fusion | bytes 1769472 | tf_op jit(solution)/shard_map/squeeze | solution.py:93
  15.9 0.2 fusion.42
  16.1 2.4 %fusion.28 = bf16[3,1,512,512]{3,2,1,0:T(8,128)(2,1)S(1)} fusion(bf16[3,128,256]{2,1,0:T(8,128)(2,1)S(1)} %broadcast.264, bf16[3,128,128]{2,1,0:T(8,128)(2,1)S(1)} %broadcast_in_dim.38, bf16[3,128,128]{2,1,0:T(8,128)(2,1)S(1)} %get-tuple-element.36, bf16[3,128,128]{2,1,0:T(8,128)(2,1)S(1)} %get-tuple-element.29, ...), kind=kLoop, calls=%fused_computation.50 | loop fusion | flops 20447232 | bytes 2260992 | tf_op jit(solution)/shard_map/stack | solution.py:96
  18.5 3.4 %fusion.35 = bf16[3,1,512,512]{3,2,0,1:T(8,128)(2,1)} fusion(bf16[3,128,256]{2,1,0:T(8,128)(2,1)S(1)} %broadcast.264, bf16[3,128,128]{2,1,0:T(8,128)(2,1)S(1)} %broadcast_in_dim.38, bf16[3,128,128]{2,1,0:T(8,128)(2,1)S(1)} %get-tuple-element.28, bf16[3,128,128]{2,1,0:T(8,128)(2,1)S(1)} %get-tuple-element.35, bf16[3,128,128]{2,1,0:T(8,128)(2,1)S(1)} %get-tuple-element.34, ...), kind=kLoop, calls=%fused_computation.57 | loop fusion | flops 20447232 | bytes 2260992 | tf_op jit(solution)/shard_map/stack | solution.py:96
  21.9 1.7 %fusion.39 = bf16[3,1,512,512]{3,2,0,1:T(8,128)(2,1)} fusion(bf16[3,128,256]{2,1,0:T(8,128)(2,1)S(1)} %broadcast.264, bf16[3,128,128]{2,1,0:T(8,128)(2,1)S(1)} %broadcast_in_dim.38, bf16[3,128,128]{2,1,0:T(8,128)(2,1)S(1)} %get-tuple-element.32, bf16[3,128,128]{2,1,0:T(8,128)(2,1)S(1)} %get-tuple-element.31, bf16[3,128,128]{2,1,0:T(8,128)(2,1)S(1)} %get-tuple-element.35, ...), kind=kLoop, calls=%fused_computation.61 | loop fusion | flops 22020096 | bytes 2260992 | tf_op jit(solution)/shard_map/stack | solution.py:96
  23.8 0.7 copy-done.6
  25.1 0.6 copy-done.4
  26.2 1.1 %pad_maximum_fusion.11 = bf16[10,4,16,256]{3,1,2,0:T(4,128)(2,1)S(1)} fusion(bf16[4,4,16,256]{3,1,2,0:T(4,128)(2,1)} %copy.50, bf16[4,4,16,256]{3,1,2,0:T(4,128)(2,1)S(1)} %broadcast_select_fusion.3, bf16[2,4,16,256]{3,1,2,0:T(4,128)(2,1)S(1)} %broadcast_select_fusion.6), kind=kLoop, calls=%fused_computation.135 | loop fusion | flops 327680 | bytes 655360 | tf_op jit(solution)/shard_map/concatenate | solution.py:102
  27.4 0.3 broadcast_select_fusion.1
  27.7 1.9 %maximum_bitcast_fusion.1 = bf16[3,1,2,512,512]{4,3,2,1,0:T(8,128)(2,1)} fusion(bf16[3,1,512,512]{3,2,1,0:T(8,128)(2,1)S(1)} %fusion.28, bf16[3,1,512,512]{3,2,1,0:T(8,128)(2,1)S(1)} %fusion.42), kind=kLoop, calls=%fused_computation.23 | loop fusion | flops 1572864 | bytes 6291456 | tf_op jit(solution)/shard_map/stack | solution.py:97
  29.6 0.2 broadcast_select_fusion.2
  29.9 0.9 %broadcast_select_fusion.5 = (bf16[10,8,2,256]{3,1,2,0:T(8,128)(2,1)S(1)}, bf16[10,8,2,256]{3,1,2,0:T(8,128)(2,1)S(1)}, bf16[10,8,2,256]{3,1,2,0:T(8,128)(2,1)S(1)}) fusion(pred[]{:T(512)S(6)} %eq.11, bf16[10,2,16,256]{3,1,2,0:T(2,128)(2,1)S(1)} %get-tuple-element.40, bf16[4,4,16,256]{3,1,2,0:T(4,128)(2,1)} %copy.50, ...), kind=kLoop, calls=%fused_computation.157 | loop fusion | flops 860160 | bytes 901121 | tf_op jit(solution)/shard_map/jit(_where)/select_n | solution.py:42
  30.8 1.6 %collective-permute-start.4 = (bf16[10,8,2,256]{3,1,2,0:T(8,128)(2,1)S(1)}, bf16[10,8,2,256]{3,1,2,0:T(8,128)(2,1)S(1)}, u32[]{:S(2)}, u32[]{:S(2)}) collective-permute-start(bf16[10,8,2,256]{3,1,2,0:T(8,128)(2,1)S(1)} %broadcast_select_fusion.4), channel_id=1, source_target_pairs={{0,1},{2,3},{1,0},{3,2},{4,5},{6,7},{5,4},{7,6},{8,9},{10,11},{9,8... | collective-permute-start | bytes 245768 | tf_op jit(solution)/shard_map/ppermute | solution.py:36
  32.4 2.5 %collective-permute-start.3 = (bf16[10,8,2,256]{3,1,2,0:T(8,128)(2,1)S(1)}, bf16[10,8,2,256]{3,1,2,0:T(8,128)(2,1)S(1)}, u32[]{:S(2)}, u32[]{:S(2)}) collective-permute-start(bf16[10,8,2,256]{3,1,2,0:T(8,128)(2,1)S(1)} %get-tuple-element.5), channel_id=1, source_target_pairs={{1,2},{3,0},{2,1},{0,3},{5,6},{7,4},{6,5},{4,7},{9,10},{11,8},{10,... | collective-permute-start | bytes 245768 | tf_op jit(solution)/shard_map/ppermute | solution.py:42
  34.9 0.8 %collective-permute-done.4 = bf16[10,8,2,256]{3,1,2,0:T(8,128)(2,1)S(1)} collective-permute-done((bf16[10,8,2,256]{3,1,2,0:T(8,128)(2,1)S(1)}, bf16[10,8,2,256]{3,1,2,0:T(8,128)(2,1)S(1)}, u32[]{:S(2)}, u32[]{:S(2)}) %collective-permute-start.4) | collective-permute-done | bytes 81952 | tf_op jit(solution)/shard_map/ppermute | solution.py:36
  35.7 3.9 %collective-permute-done.3 = bf16[10,8,2,256]{3,1,2,0:T(8,128)(2,1)S(1)} collective-permute-done((bf16[10,8,2,256]{3,1,2,0:T(8,128)(2,1)S(1)}, bf16[10,8,2,256]{3,1,2,0:T(8,128)(2,1)S(1)}, u32[]{:S(2)}, u32[]{:S(2)}) %collective-permute-start.3) | collective-permute-done | bytes 81952 | tf_op jit(solution)/shard_map/ppermute | solution.py:42
  39.6 1.5 %maximum_bitcast_fusion.2 = bf16[10,8,1,20,256]{4,1,3,0,2:T(8,128)(2,1)S(1)} fusion(bf16[10,8,2,256]{3,1,2,0:T(8,128)(2,1)S(1)} %get-tuple-element.38, bf16[10,2,16,256]{3,1,2,0:T(2,128)(2,1)S(1)} %get-tuple-element.40, bf16[4,4,16,256]{3,1,2,0:T(4,128)(2,1)} %copy.50, bf16[4,4,16,256]{3,1,2,0:T(4,128)(2,1)S(1)} %broadcast_select_fusion.3, ...), kind=kLoop, calls=%fused_computation.96 | loop fusion | flops 5734400 | bytes 1638400 | tf_op jit(solution)/shard_map/broadcast_in_dim | solution.py:57
  41.2 0.2 copy.54
  41.4 0.2 slice.164
  41.6 0.3 copy-done.20
  41.8 4.3 %fusion.65 = bf16[8,6,8,3,256]{4,2,3,1,0:T(8,128)(2,1)S(1)} fusion(bf16[3,3,3,256,256]{4,3,2,1,0:T(8,128)(2,1)S(1)} %copy-done, bf16[10,8,1,7,2,256]{5,3,4,1,0,2:T(8,128)(2,1)S(1)} %slice.164, bf16[10,8,1,8,3,256]{5,3,4,1,0,2:T(8,128)(2,1)S(1)} %copy.54, pred[8,3]{0,1:T(4,128)(4,1)S(1)} %copy-done.20), kind=kOutput, calls=%fused_computation.82 | convolution fusion | flops 4082663424 | bytes 5685272 | tf_op jit(solution)/shard_map/conv_general_dilated | solution.py:56
  46.1 0.2 copy.55
  46.3 0.2 fusion.88
  46.7 0.2 copy-done.19
  47.0 2.4 %maximum_convert_fusion = bf16[6,5,8,3,512]{4,2,3,1,0:T(8,128)(2,1)S(1)} fusion(bf16[3,1,2,256,128]{4,3,2,1,0:T(8,128)(2,1)S(1)} %maximum_bitcast_fusion.10, bf16[3,1,2,256,128]{4,3,2,1,0:T(8,128)(2,1)S(1)} %maximum_bitcast_fusion.9, bf16[8,6,1,7,1,256]{5,3,4,1,0,2:T(8,128)(2,1)S(1)} %slice.166, bf16[8,6,1,8,3,256]{5,3,4,1,0,2:T(8,128)(2,1)S(1)} %copy.57, ...), kind=kOutput, calls=%fused_computation.76 | convolution fusion | flops 2284511232 | bytes 4644888 | tf_op jit(solution)/shard_map/conv_general_dilated | solution.py:56
  49.4 1.4 %copy.63 = bf16[6,5,8,3,512]{4,3,2,1,0:T(4,128)(2,1)} copy(bf16[6,5,8,3,512]{4,2,3,1,0:T(8,128)(2,1)S(1)} %maximum_convert_fusion) | data formatting | bytes 1474560 | tf_op jit(solution)/shard_map/convert_element_type | solution.py:110
  50.9 3.1 %reshape.136 = bf16[6,5,1,24,512]{4,3,1,0,2:T(8,128)(2,1)} reshape(bf16[6,5,8,3,512]{4,3,2,1,0:T(4,128)(2,1)} %copy.63) | data formatting | bytes 1474560 | tf_op jit(solution)/shard_map/convert_element_type | solution.py:110
  54.0 1.5 %fusion.86 = bf16[6,5,1,17,512]{4,3,1,0,2:T(8,128)(2,1)S(1)} fusion(bf16[6,5,1,24,512]{4,3,1,0,2:T(8,128)(2,1)} %reshape.136, s32[]{:T(128)S(6)} %mul.25, s32[17]{0:T(128)S(1)} %iota_multiply_fusion, s32[]{:T(128)S(6)} %mul.23, s32[512]{0:T(512)S(1)} %get-tuple-element.49, s32[512]{0:T(512)S(1)} %get-tuple-element.50, s32[5]{0:T(128)} %iota_multiply_fusion.1, ...), kind=kLoop, calls=%fused_computation.105 | loop fusion | flops 8878080 | bytes 1049184 | tf_op jit(solution)/shard_map/jit(_where)/select_n | solution.py:119
  55.5 1.0 %pad.6 = bf16[6,5,1,24,512]{4,3,1,0,2:T(8,128)(2,1)} pad(bf16[6,5,1,17,512]{4,3,1,0,2:T(8,128)(2,1)S(1)} %fusion.86, bf16[]{:T(256)} %constant.93.clone.1), padding=0_0x0_0x0_0x0_7x0_0 | pad | bytes 1259522 | tf_op jit(solution)/shard_map/jit(_where)/select_n | solution.py:119
  56.4 3.2 %reshape.128 = bf16[6,5,1,8,3,512]{5,4,3,1,0,2:T(4,128)(2,1)} reshape(bf16[6,5,1,24,512]{4,3,1,0,2:T(8,128)(2,1)} %pad.6) | data formatting | bytes 1474560 | tf_op jit(solution)/shard_map/conv_general_dilated | solution.py:56
  59.6 1.5 %copy.65 = bf16[6,5,1,8,3,512]{5,3,4,1,0,2:T(8,128)(2,1)S(1)} copy(bf16[6,5,1,8,3,512]{5,4,3,1,0,2:T(4,128)(2,1)} %reshape.128) | data formatting | bytes 1474560 | tf_op jit(solution)/shard_map/conv_general_dilated | solution.py:56
  61.3 4.9 %fusion.68 = bf16[4,4,8,3,512]{4,2,3,1,0:T(8,128)(2,1)S(1)} fusion(bf16[3,1,2,512,512]{4,3,2,1,0:T(8,128)(2,1)} %maximum_bitcast_fusion.1, bf16[6,5,1,7,1,512]{5,3,4,1,0,2:T(8,128)(2,1)S(1)} %slice.183, bf16[6,5,1,8,3,512]{5,3,4,1,0,2:T(8,128)(2,1)S(1)} %copy.65, pred[8,3]{0,1:T(4,128)(4,1)S(1)} %copy-done.18, bf16[3,1,512,512]{3,2,0,1:T(8,128)(2,1)} %fusion.39, ...), kind=kOutput, calls=%fused_computation.83 | convolution fusion | flops 2433417216 | bytes 7637016 | tf_op jit(solution)/shard_map/conv_general_dilated | solution.py:56
  66.3 0.2 copy.77
  66.5 0.8 %slice.184 = bf16[4,4,1,16,512]{4,1,3,0,2:T(4,128)(2,1)} slice(bf16[4,4,1,24,512]{4,1,3,0,2:T(4,128)(2,1)S(1)} %bitcast.131), slice={[0:4], [0:4], [0:1], [0:16], [0:512]} | slice | bytes 524288 | tf_op jit(solution)/shard_map/convert_element_type | solution.py:120
  67.3 1.7 %reshape.154 = bf16[4,4,16,2,2,128]{5,4,3,1,2,0:T(2,128)(2,1)} reshape(bf16[4,4,1,16,512]{4,1,3,0,2:T(4,128)(2,1)} %slice.184) | data formatting | bytes 524288 | tf_op jit(solution)/shard_map/convert_element_type | solution.py:120
  69.0 1.9 %copy.79 = bf16[4,4,2,16,2,128]{5,4,3,2,1,0:T(2,128)(2,1)} copy(bf16[4,4,2,16,2,128]{5,4,2,1,3,0:T(2,128)(2,1)} %bitcast.132) | data formatting | bytes 524288 | tf_op jit(solution)/shard_map/transpose | solution.py:122
  (68 shorter events, 1.8 us)
Async XLA Ops:
  0.0 41.5 %copy-start = (bf16[3,3,3,256,256]{4,3,2,1,0:T(8,128)(2,1)S(1)}, bf16[3,3,3,256,256]{4,3,2,1,0:T(8,128)(2,1)}, u32[]{:S(2)}) copy-start(bf16[3,3,3,256,256]{4,3,2,1,0:T(8,128)(2,1)} %param.5) | copy-start | bytes 10616836
  1.8 24.4 %collective-permute-start.1 = (bf16[4,4,16,256]{3,1,2,0:T(4,128)(2,1)}, bf16[4,4,16,256]{3,1,2,0:T(4,128)(2,1)}, u32[]{:S(2)}, u32[]{:S(2)}) collective-permute-start(bf16[4,4,16,256]{3,1,2,0:T(4,128)(2,1)} %copy.50), channel_id=1, source_target_pairs={{0,8},{8,16},{16,24},{24,0},{1,9},{9,17},{17,25},{25,1},{2,10},{10... | collective-permute-start | bytes 393224 | tf_op jit(solution)/shard_map/ppermute | solution.py:9
  6.3 19.8 %collective-permute-start = (bf16[2,4,16,256]{3,1,2,0:T(4,128)(2,1)}, bf16[2,4,16,256]{3,1,2,0:T(4,128)(2,1)}, u32[]{:S(2)}, u32[]{:S(2)}) collective-permute-start(bf16[2,4,16,256]{3,1,2,0:T(4,128)(2,1)} %slice.161), channel_id=1, source_target_pairs={{0,16},{8,24},{16,0},{24,8},{1,17},{9,25},{17,1},{25,9},{2,18},{10... | collective-permute-start | bytes 196616 | tf_op jit(solution)/shard_map/ppermute | solution.py:9
  18.5 5.1 %copy-start.10 = (bf16[3,1,256,128]{3,2,1,0:T(8,128)(2,1)S(1)}, bf16[3,1,256,128]{3,2,1,0:T(8,128)(2,1)}, u32[]{:S(2)}) copy-start(bf16[3,1,256,128]{3,2,1,0:T(8,128)(2,1)} %get-tuple-element.14) | copy-start | bytes 589828
  18.5 5.1 %copy-start.12 = (bf16[3,1,256,128]{3,2,1,0:T(8,128)(2,1)S(1)}, bf16[3,1,256,128]{3,2,1,0:T(8,128)(2,1)}, u32[]{:S(2)}) copy-start(bf16[3,1,256,128]{3,2,1,0:T(8,128)(2,1)} %get-tuple-element.42) | copy-start | bytes 589828
  21.9 1.8 %copy-start.16 = (bf16[3,1,256,128]{3,2,1,0:T(8,128)(2,1)S(1)}, bf16[3,1,256,128]{3,2,1,0:T(8,128)(2,1)}, u32[]{:S(2)}) copy-start(bf16[3,1,256,128]{3,2,1,0:T(8,128)(2,1)} %get-tuple-element.18) | copy-start | bytes 589828
  21.9 1.8 %copy-start.17 = (bf16[3,1,256,128]{3,2,1,0:T(8,128)(2,1)S(1)}, bf16[3,1,256,128]{3,2,1,0:T(8,128)(2,1)}, u32[]{:S(2)}) copy-start(bf16[3,1,256,128]{3,2,1,0:T(8,128)(2,1)} %get-tuple-element.46) | copy-start | bytes 589828
  23.6 0.9 %copy-start.6 = (bf16[3,1,256,128]{3,2,1,0:T(8,128)(2,1)S(1)}, bf16[3,1,256,128]{3,2,1,0:T(8,128)(2,1)}, u32[]{:S(2)}) copy-start(bf16[3,1,256,128]{3,2,1,0:T(8,128)(2,1)} %get-tuple-element.15) | copy-start | bytes 589828
  23.6 1.0 %copy-start.8 = (bf16[3,1,256,128]{3,2,1,0:T(8,128)(2,1)S(1)}, bf16[3,1,256,128]{3,2,1,0:T(8,128)(2,1)}, u32[]{:S(2)}) copy-start(bf16[3,1,256,128]{3,2,1,0:T(8,128)(2,1)} %get-tuple-element.41) | copy-start | bytes 589828
  23.6 1.1 %copy-start.14 = (bf16[3,1,256,128]{3,2,1,0:T(8,128)(2,1)S(1)}, bf16[3,1,256,128]{3,2,1,0:T(8,128)(2,1)}, u32[]{:S(2)}) copy-start(bf16[3,1,256,128]{3,2,1,0:T(8,128)(2,1)} %get-tuple-element.19) | copy-start | bytes 589828
  23.7 1.2 %copy-start.15 = (bf16[3,1,256,128]{3,2,1,0:T(8,128)(2,1)S(1)}, bf16[3,1,256,128]{3,2,1,0:T(8,128)(2,1)}, u32[]{:S(2)}) copy-start(bf16[3,1,256,128]{3,2,1,0:T(8,128)(2,1)} %get-tuple-element.45) | copy-start | bytes 589828
  23.8 1.2 %copy-start.11 = (bf16[3,1,256,128]{3,2,1,0:T(8,128)(2,1)S(1)}, bf16[3,1,256,128]{3,2,1,0:T(8,128)(2,1)}, u32[]{:S(2)}) copy-start(bf16[3,1,256,128]{3,2,1,0:T(8,128)(2,1)} %get-tuple-element.48) | copy-start | bytes 589828
  23.8 1.2 %copy-start.13 = (bf16[3,1,256,128]{3,2,1,0:T(8,128)(2,1)S(1)}, bf16[3,1,256,128]{3,2,1,0:T(8,128)(2,1)}, u32[]{:S(2)}) copy-start(bf16[3,1,256,128]{3,2,1,0:T(8,128)(2,1)} %get-tuple-element.20) | copy-start | bytes 589828
  24.7 1.0 %copy-start.4 = (bf16[3,1,256,128]{3,2,1,0:T(8,128)(2,1)S(1)}, bf16[3,1,256,128]{3,2,1,0:T(8,128)(2,1)}, u32[]{:S(2)}) copy-start(bf16[3,1,256,128]{3,2,1,0:T(8,128)(2,1)} %get-tuple-element.44) | copy-start | bytes 589828
  24.7 1.0 %copy-start.5 = (bf16[3,1,256,128]{3,2,1,0:T(8,128)(2,1)S(1)}, bf16[3,1,256,128]{3,2,1,0:T(8,128)(2,1)}, u32[]{:S(2)}) copy-start(bf16[3,1,256,128]{3,2,1,0:T(8,128)(2,1)} %get-tuple-element.24) | copy-start | bytes 589828
  24.9 1.0 %copy-start.7 = (bf16[3,1,256,128]{3,2,1,0:T(8,128)(2,1)S(1)}, bf16[3,1,256,128]{3,2,1,0:T(8,128)(2,1)}, u32[]{:S(2)}) copy-start(bf16[3,1,256,128]{3,2,1,0:T(8,128)(2,1)} %get-tuple-element.47) | copy-start | bytes 589828
  24.9 1.0 %copy-start.9 = (bf16[3,1,256,128]{3,2,1,0:T(8,128)(2,1)S(1)}, bf16[3,1,256,128]{3,2,1,0:T(8,128)(2,1)}, u32[]{:S(2)}) copy-start(bf16[3,1,256,128]{3,2,1,0:T(8,128)(2,1)} %get-tuple-element.21) | copy-start | bytes 589828
  24.9 1.1 %copy-start.2 = (bf16[3,1,256,128]{3,2,1,0:T(8,128)(2,1)S(1)}, bf16[3,1,256,128]{3,2,1,0:T(8,128)(2,1)}, u32[]{:S(2)}) copy-start(bf16[3,1,256,128]{3,2,1,0:T(8,128)(2,1)} %get-tuple-element.43) | copy-start | bytes 589828
  24.9 1.1 %copy-start.3 = (bf16[3,1,256,128]{3,2,1,0:T(8,128)(2,1)S(1)}, bf16[3,1,256,128]{3,2,1,0:T(8,128)(2,1)}, u32[]{:S(2)}) copy-start(bf16[3,1,256,128]{3,2,1,0:T(8,128)(2,1)} %get-tuple-element.25) | copy-start | bytes 589828
  27.6 2.0 %collective-permute-start.2 = (bf16[10,2,16,256]{3,1,2,0:T(2,128)(2,1)S(1)}, bf16[10,2,16,256]{3,1,2,0:T(2,128)(2,1)S(1)}, u32[]{:S(2)}, u32[]{:S(2)}) collective-permute-start(bf16[10,2,16,256]{3,1,2,0:T(2,128)(2,1)S(1)} %broadcast_select_fusion.1), channel_id=1, source_target_pairs={{0,4},{4,0},{1,5},{5,1},{2,6},{6,2},{3,7},{7,3},{8,12},{12,8},{9,1... | collective-permute-start | bytes 491528 | tf_op jit(solution)/shard_map/ppermute | solution.py:36
  30.8 4.9 %collective-permute-start.4 = (bf16[10,8,2,256]{3,1,2,0:T(8,128)(2,1)S(1)}, bf16[10,8,2,256]{3,1,2,0:T(8,128)(2,1)S(1)}, u32[]{:S(2)}, u32[]{:S(2)}) collective-permute-start(bf16[10,8,2,256]{3,1,2,0:T(8,128)(2,1)S(1)} %broadcast_select_fusion.4), channel_id=1, source_target_pairs={{0,1},{2,3},{1,0},{3,2},{4,5},{6,7},{5,4},{7,6},{8,9},{10,11},{9,8... | collective-permute-start | bytes 245768 | tf_op jit(solution)/shard_map/ppermute | solution.py:36
  32.4 7.1 %collective-permute-start.3 = (bf16[10,8,2,256]{3,1,2,0:T(8,128)(2,1)S(1)}, bf16[10,8,2,256]{3,1,2,0:T(8,128)(2,1)S(1)}, u32[]{:S(2)}, u32[]{:S(2)}) collective-permute-start(bf16[10,8,2,256]{3,1,2,0:T(8,128)(2,1)S(1)} %get-tuple-element.5), channel_id=1, source_target_pairs={{1,2},{3,0},{2,1},{0,3},{5,6},{7,4},{6,5},{4,7},{9,10},{11,8},{10,... | collective-permute-start | bytes 245768 | tf_op jit(solution)/shard_map/ppermute | solution.py:42
  41.1 0.7 copy-start.20
  46.3 0.7 copy-start.19
  56.4 4.8 %copy-start.18 = (pred[8,3]{0,1:T(4,128)(4,1)S(1)}, pred[8,3]{0,1:T(4,128)(4,1)}, u32[]{:S(2)}) copy-start(pred[8,3]{0,1:T(4,128)(4,1)} %constant.112) | copy-start | bytes 76
  59.6 1.7 %copy-start.1 = (bf16[3,1,512,512]{3,2,0,1:T(8,128)(2,1)S(1)}, bf16[3,1,512,512]{3,2,0,1:T(8,128)(2,1)}, u32[]{:S(2)}) copy-start(bf16[3,1,512,512]{3,2,0,1:T(8,128)(2,1)} %fusion.35) | copy-start | bytes 4718596

commit v2 on v0

v2 whole, which is shorter than its diff:
```python
import functools

import jax
import jax.numpy as jnp
from jax import lax
from jax.experimental import pallas as pl
from jax.experimental.pallas import tpu as pltpu
from jax.sharding import PartitionSpec as P

BF, F32 = jnp.bfloat16, jnp.float32
EARLIER = 6
RIM = 2


def call(body, outs, args, scratch=(), flops=0, name=None):
    spec = pl.BlockSpec(memory_space=pltpu.VMEM)
    outs = [jax.ShapeDtypeStruct(shape, kind) for shape, kind in outs]
    size = sum(a.size * a.dtype.itemsize for a in [*args, *outs])
    return pl.pallas_call(
        body, out_shape=outs, in_specs=[spec] * len(args), out_specs=[spec] * len(outs),
        scratch_shapes=[pltpu.VMEM(*s) for s in scratch], name=name,
        cost_estimate=pl.CostEstimate(flops=flops, bytes_accessed=size, transcendentals=0),
        compiler_params=pltpu.CompilerParams(vmem_limit_bytes=32 << 20),
    )(*args)


LANES = 128
SLACK = 8


def put(ref, rows, value, add=False):
    for k in range(ref.shape[0]):
        block = value[:, k * LANES : (k + 1) * LANES]
        ref[k, rows, :] = ref[k, rows, :] + block if add else block


def take(ref, rows, blocks=None):
    blocks = range(ref.shape[0]) if blocks is None else blocks
    return jnp.concatenate([ref[k, rows, :] for k in blocks], 1)


def blocked(rows, width):
    return (width // LANES, rows, LANES)


def swaps(size):
    assert size % 2 == 0
    rounds = [[(i, i + 1) for i in range(0, size, 2)]]
    if size > 2:
        rounds.append([(i, (i + 1) % size) for i in range(1, size, 2)])
    return [pairs + [(j, i) for i, j in pairs] for pairs in rounds]


def exchange(sends, axis):
    return [lax.ppermute(s, axis, pairs) for s, pairs in zip(sends, swaps(lax.axis_size(axis)))]


def arrived(axis, got):
    place, size = lax.axis_index(axis), lax.axis_size(axis)
    even = place % 2 == 0
    if len(got) == 1:
        before = after = got[0]
    else:
        before, after = jnp.where(even, got[1], got[0]), jnp.where(even, got[0], got[1])
    zero = jnp.zeros_like(before)
    return jnp.where(place > 0, before, zero), jnp.where(place < size - 1, after, zero)


def join_frames(*refs, pieces, rounds):
    own, got = refs[0], refs[1 : 1 + len(pieces)]
    field, sends = refs[1 + len(pieces)], refs[2 + len(pieces) :]
    place, at = lax.axis_index("section"), 0
    for (take, by), ref in zip(pieces, got):
        field[at : at + take] = jnp.where(place >= by, ref[...], jnp.zeros_like(ref))
        at += take
    field[at:] = own[...]
    even = lax.axis_index("row") % 2 == 0
    last = field.shape[1] - RIM
    for k in range(rounds):
        start = jnp.where(even, 0, last) if k else jnp.where(even, last, 0)
        sends[k][...] = field[:, pl.ds(start, RIM)]


def strips(*refs, rows):
    field, got = refs[0], refs[1 : 1 + rows]
    sends, wide = refs[1 + rows : -1], refs[-1]
    frames, height, breadth, width = field.shape
    before, after = arrived("row", [g[...].astype(F32) for g in got])
    tall = height + 2 * RIM
    for t in range(frames):
        whole = jnp.concatenate([before[t], field[t].astype(F32), after[t]], 0)
        size = tall * breadth
        put(wide, slice(t * size, (t + 1) * size), whole.reshape(size, width))
    first, last = (
        [take(wide, pl.ds(c, frames * tall, stride=breadth)).astype(BF) for c in cols]
        for cols in ([0, 1], [breadth - 2, breadth - 1])
    )
    even = lax.axis_index("col") % 2 == 0
    for k, send in enumerate(sends):
        for i in range(RIM):
            send[i] = jnp.where(even, first[i], last[i]) if k else jnp.where(even, last[i], first[i])


def first_inner(*refs, rows):
    field, got, kernel, out, wide = refs[0], refs[1 : 1 + rows], refs[1 + rows], refs[-2], refs[-1]
    frames, height, breadth, width = field.shape
    before, after = arrived("row", [g[...] for g in got])
    tall = height + 2 * RIM
    size = tall * breadth
    col = lax.broadcasted_iota(jnp.int32, (size, width), 0) % breadth
    for t in range(frames):
        whole = jnp.concatenate([before[t], field[t], after[t]], 0)
        wide[1, t] = whole
        flat = whole.reshape(size, width).astype(F32)
        lower = jnp.where(col == 0, 0.0, pltpu.roll(flat, 1, 0))
        upper = jnp.where(col == breadth - 1, 0.0, pltpu.roll(flat, size - 1, 0))
        wide[0, t] = lower.astype(BF).reshape(whole.shape)
        wide[2, t] = upper.astype(BF).reshape(whole.shape)
    taps = [
        wide[e, a : a + frames - 2, b : b + tall - 2].reshape(-1, width)
        for a in range(3) for b in range(3) for e in range(3)
    ]
    found = jnp.dot(
        jnp.concatenate(taps, 1), kernel[...].reshape(-1, kernel.shape[-1]), preferred_element_type=F32
    )
    out[...] = found.reshape(out.shape)


def kernels(second, third, summed, paired):
    fine = second.shape[-1]
    reads = [[(0, 1), (2,)], [(0,), (1, 2)]]
    for a in range(3):
        tap = [[second[a, b, e].astype(F32) for e in range(3)] for b in range(3)]
        for di in range(2):
            for dj in range(2):
                for py in range(2):
                    for px in range(2):
                        parts = [tap[b][e] for b in reads[py][di] for e in reads[px][dj]]
                        at = (2 * py + px) * fine
                        summed[a, di, dj, :, at : at + fine] = sum(parts[1:], parts[0]).astype(BF)
    width, out = third.shape[-2:]
    for a in range(3):
        for b in range(3):
            for dj in range(2):
                for px in range(2):
                    for q in range(2):
                        e = 2 * dj + px - q
                        block = third[a, b, e] if 0 <= e < 3 else jnp.zeros((width, out), BF)
                        paired[a, b, dj, px * width : (px + 1) * width, q * out : (q + 1) * out] = block


def rest(*refs, cols):
    inner, sent, got = refs[0], refs[1 : 1 + cols], refs[1 + cols : 1 + 2 * cols]
    kernel, summed, paired, out = refs[1 + 2 * cols : 5 + 2 * cols]
    edge, coarse, near, far, grown, fine, spread = refs[5 + 2 * cols :]
    frames, rows, breadth, width = inner.shape
    tall = rows + 2
    top, bottom = lax.axis_index("row") == 0, lax.axis_index("row") == lax.axis_size("row") - 1
    leftmost, rightmost = lax.axis_index("col") == 0, lax.axis_index("col") == lax.axis_size("col") - 1

    even = lax.axis_index("col") % 2 == 0
    before, after = arrived("col", [g[...] for g in got])
    if cols == 1:
        own = [sent[0][0], sent[0][1]]
    else:
        own = [jnp.where(even, sent[1][0], sent[0][0]), jnp.where(even, sent[0][1], sent[1][1])]
    size, count = frames * tall, before.shape[1]
    for i, strip in enumerate([before[0], before[1], own[0], own[1], after[0], after[1]]):
        edge[i, :count] = strip.astype(F32)

    def part(e, places):
        lhs = jnp.concatenate([
            jnp.concatenate(
                [edge[i, a * tall + b : a * tall + b + size].astype(BF) for i in places], 0
            )
            for a in range(3) for b in range(3)
        ], 1)
        rhs = jnp.concatenate([kernel[a, b, e] for a in range(3) for b in range(3)], 0)
        found = jnp.dot(lhs, rhs, preferred_element_type=F32)
        return [found[i * size : (i + 1) * size] for i in range(len(places))]

    left0, fix0, right0 = part(0, [0, 1, 3])
    left1, right1 = part(1, [1, 4])
    left2, fix1, right2 = part(2, [2, 4, 5])
    left, right = left0 + left1 + left2, right0 + right1 + right2

    pitch = breadth + SLACK
    for t in range(frames):
        for r in range(rows):
            at = (t * tall + r) * pitch
            put(coarse, slice(at, at + breadth), inner[t, r])
    put(coarse, pl.ds(0, size, stride=pitch), fix0, add=True)
    put(coarse, pl.ds(breadth - 1, size, stride=pitch), fix1, add=True)
    put(coarse, pl.ds(breadth, size, stride=pitch), right)
    begin = take(coarse, pl.ds(0, size, stride=pitch))

    def outside(row):
        return (top & (row == 0)) | (bottom & (row == rows - 1))

    slot = lax.broadcasted_iota(jnp.int32, (breadth, width), 0)
    ends = rightmost & (slot == breadth - 1)
    for t in range(frames):
        for r in range(rows):
            at = (t * tall + r) * pitch
            lost = top if r == 0 else bottom if r == rows - 1 else None
            for dj in range(2):
                value = jnp.maximum(take(coarse, slice(at + dj, at + dj + breadth)), 0.0)
                gone = [g for g in (lost, ends if dj else None) if g is not None]
                if gone:
                    value = jnp.where(functools.reduce(jnp.logical_or, gone), 0.0, value)
                near[dj, t, r] = value.astype(BF)
    row = lax.broadcasted_iota(jnp.int32, (size, width), 0) % tall
    far[0, :size] = jnp.where(outside(row) | leftmost, 0.0, jnp.maximum(left, 0.0))
    far[1, :size] = jnp.where(outside(row), 0.0, jnp.maximum(begin, 0.0))

    corners, later = rows - 1, frames - 2
    short = later * tall
    taps = [
        jnp.concatenate([
            near[dj, a : a + later, di : di + corners].reshape(-1, width),
            far[dj, a * tall + di : a * tall + di + short].astype(BF),
        ], 0)
        for a in range(3) for di in range(2) for dj in range(2)
    ]
    found = jnp.dot(
        jnp.concatenate(taps, 1), summed[...].reshape(-1, summed.shape[-1]), preferred_element_type=F32
    )
    found = jnp.maximum(found, 0.0)
    full = later * corners * breadth
    half = found.shape[1] // 2
    for t in range(later):
        for i in range(corners):
            at, to = (t * corners + i) * breadth, (t * tall + i) * pitch + SLACK
            put(grown, slice(to, to + breadth), found[at : at + breadth])
    put(grown, pl.ds(SLACK - 1, short, stride=pitch), found[full:])
    slot = lax.broadcasted_iota(jnp.int32, (breadth, half), 0)
    side = lax.broadcasted_iota(jnp.int32, (breadth, half), 1) < half // 2
    begins = leftmost & (slot == 0) & side
    ends = rightmost & (slot == breadth - 1) & ~side
    for t in range(later):
        for i in range(corners):
            for py in range(2):
                blocks = range(py * half // LANES, (py + 1) * half // LANES)
                lost = (top if py == 0 and i == 0 else bottom if py == 1 and i == corners - 1 else None)
                for dj, gone in enumerate((begins, ends)):
                    gone = gone if lost is None else gone | lost
                    at = (t * tall + i) * pitch + SLACK - 1 + dj
                    value = take(grown, slice(at, at + breadth), blocks)
                    fine[dj, 2 * i + py, t] = jnp.where(gone, 0.0, value).astype(BF)

    high, kept, wide = 2 * corners - 2, later - 2, out.shape[-1]
    taps = [
        fine[dj, b : b + high, a : a + kept].reshape(-1, half)
        for a in range(3) for b in range(3) for dj in range(2)
    ]
    found = jnp.dot(
        jnp.concatenate(taps, 1), paired[...].reshape(-1, paired.shape[-1]), preferred_element_type=F32
    )
    for y in range(high):
        for t in range(kept):
            at = (y * kept + t) * breadth
            for q in range(2):
                spread[t, y, pl.ds(q, breadth, stride=2), :] = found[
                    at : at + breadth, q * wide : (q + 1) * wide
                ]
    out[...] = spread[...].astype(BF)


def per_device(latent, w_first, w_second, w_third):
    frames, height, breadth, width = latent.shape
    mid, fine = w_first.shape[-1], w_second.shape[-1]
    last = w_third.shape[-1]
    sections = lax.axis_size("section")
    pieces, got, left, by = [], [], EARLIER, 1
    while left > 0:
        take = min(left, frames)
        ring = [(i, (i + by) % sections) for i in range(sections)]
        got.insert(0, lax.ppermute(latent[frames - take :], "section", ring))
        pieces.insert(0, (take, by))
        left, by = left - take, by + 1
    summed, paired = call(
        kernels, [((3, 2, 2, mid, 4 * fine), BF), ((3, 3, 2, 2 * fine, 2 * last), BF)],
        [w_second, w_third], name="kernels",
    )
    total = frames + EARLIER
    rounds = len(swaps(lax.axis_size("row")))
    field, *sends = call(
        functools.partial(join_frames, pieces=pieces, rounds=rounds),
        [((total, height, breadth, width), BF)] + [((total, RIM, breadth, width), BF)] * rounds,
        [latent, *got], name="join_frames",
    )
    rows_got = exchange(sends, "row")
    tall = height + 2 * RIM
    cols = len(swaps(lax.axis_size("col")))
    sends = call(
        functools.partial(strips, rows=rounds), [((RIM, total * tall, width), BF)] * cols,
        [field, *rows_got], [(blocked(total * tall * breadth, width), F32)], name="strips",
    )
    cols_got = exchange(sends, "col")
    early = total - 2
    (inner,) = call(
        functools.partial(first_inner, rows=rounds), [((early, tall - 2, breadth, mid), F32)],
        [field, *rows_got, w_first], [((3, total, tall, breadth, width), BF)],
        flops=2 * 27 * early * (tall - 2) * breadth * width * mid, name="first_inner",
    )
    later, corners = early - 2, tall - 3
    size = early * tall
    (out,) = call(
        functools.partial(rest, cols=cols), [((frames, 2 * height, 2 * breadth, last), BF)],
        [inner, *sends, *cols_got, w_first, summed, paired],
        [
            ((6, total * tall + 8, width), F32),
            (blocked(size * (breadth + SLACK), mid), F32),
            ((2, early, tall - 2, breadth, mid), BF),
            ((2, size + 8, mid), F32),
            (blocked(later * tall * (breadth + SLACK), 4 * fine), F32),
            ((2, 2 * corners, later, breadth, 2 * fine), BF),
            ((frames, 2 * height, 2 * breadth, last), F32),
        ],
        flops=4 * 10**9, name="rest",
    )
    return out


def solution(mesh):
    in_specs = (P("section", "row", "col", None), P(), P(), P())
    out_specs = P("section", "row", "col", None)
    return jax.shard_map(
        per_device, mesh=mesh, in_specs=in_specs, out_specs=out_specs, check_vma=False
    )
```

time: 92.1 us -> 30.6 us (0.33)
  the two profiles are of different devices: /device:TPU:28 before, /device:TPU:0 now
where the time goes in v2:
time: 30.6 us; the launch traced here: 30.3 us
  Pallas kernels  11.3 us (37%)
  starting transfers between devices  8.88 us (29%)
  local copies, waits for them, and re-layouts  6.42 us (21%)
  waiting for transfers between devices  3.68 us (12%)
    pallas_call x5, Pallas kernels, call(): pl.pallas_call(body, out_shape=outs, in_specs=[spec] * len(args), out_spe...  11.3 us
    unnamed x8, local copies, waits for them, and re-layouts  5.54 us
    ppermute x2, starting transfers between devices, per_device(): got.insert(0, lax.ppermute(latent[frames - take:], 'section', ring))  4.49 us
    ppermute x3, starting transfers between devices, exchange(): lax.ppermute(s, axis, pairs)  4.39 us
    ppermute x2, waiting for transfers between devices, per_device(): got.insert(0, lax.ppermute(latent[frames - take:], 'section', ring))  3.67 us
    slice x1, local copies, waits for them, and re-layouts, per_device(): got.insert(0, lax.ppermute(latent[frames - take:], 'section', ring))  0.88 us
  transfers between devices with their start and end apart: 5, of which 1 were waited for; matrix products, arithmetic and copies ran while one was open for 3% of the time, Pallas kernels for 13%

profile of v2, /device:TPU:0, one launch (start us, length us, event | category | flops | bytes accessed | tf_op | source)
XLA Modules:
  0.0 30.3 jit_solution(14119038089718399764)
XLA Ops:
  0.0 3.0 %collective-permute-start.1 = (bf16[4,4,16,256]{3,2,1,0:T(8,128)(2,1)}, bf16[4,4,16,256]{3,2,1,0:T(8,128)(2,1)S(1)}, u32[]{:S(2)}, u32[]{:S(2)}) collective-permute-start(bf16[4,4,16,256]{3,2,1,0:T(8,128)(2,1)} %refs_0_.1), channel_id=1, source_target_pairs={{0,8},{8,16},{16,24},{24,0},{1,9},{9,17},{17,25},{25,1},{2,10},{10... | collective-permute-start | bytes 393224 | tf_op jit(solution)/shard_map/ppermute | solution.py:278
  3.0 0.9 %slice.3 = bf16[2,4,16,256]{3,2,1,0:T(8,128)(2,1)S(1)} slice(bf16[4,4,16,256]{3,2,1,0:T(8,128)(2,1)} %refs_0_.1), slice={[2:4], [0:4], [0:16], [0:256]} | slice | bytes 131072 | tf_op jit(solution)/shard_map/slice | solution.py:278
  3.8 1.5 %collective-permute-start = (bf16[2,4,16,256]{3,2,1,0:T(8,128)(2,1)S(1)}, bf16[2,4,16,256]{3,2,1,0:T(8,128)(2,1)S(1)}, u32[]{:S(2)}, u32[]{:S(2)}) collective-permute-start(bf16[2,4,16,256]{3,2,1,0:T(8,128)(2,1)S(1)} %slice.3), channel_id=1, source_target_pairs={{0,16},{8,24},{16,0},{24,8},{1,17},{9,25},{17,1},{25,9},{2,18},{10... | collective-permute-start | bytes 196616 | tf_op jit(solution)/shard_map/ppermute | solution.py:278
  5.4 3.7 %collective-permute-done.refs_1_ = bf16[2,4,16,256]{3,2,1,0:T(8,128)(2,1)S(1)} collective-permute-done((bf16[2,4,16,256]{3,2,1,0:T(8,128)(2,1)S(1)}, bf16[2,4,16,256]{3,2,1,0:T(8,128)(2,1)S(1)}, u32[]{:S(2)}, u32[]{:S(2)}) %collective-permute-start) | collective-permute-done | bytes 65568 | tf_op jit(solution)/shard_map/ppermute | solution.py:278
  9.0 0.0 collective-permute-done.1.refs_2_
  9.0 0.0 copy-start.2
  9.0 0.9 %copy-done.2 = bf16[4,4,16,256]{3,2,1,0:T(8,128)(2,1)S(1)} copy-done((bf16[4,4,16,256]{3,2,1,0:T(8,128)(2,1)S(1)}, bf16[4,4,16,256]{3,2,1,0:T(8,128)(2,1)}, u32[]{:S(2)}) %copy-start.2) | copy-done | bytes 131096
  10.0 0.1 collective-permute-start.2
  10.1 0.0 copy-start
  10.1 1.5 %copy-done = bf16[3,3,3,256,128]{4,3,2,1,0:T(8,128)(2,1)S(1)} copy-done((bf16[3,3,3,256,128]{4,3,2,1,0:T(8,128)(2,1)S(1)}, bf16[3,3,3,256,128]{4,3,2,1,0:T(8,128)(2,1)}, u32[]{:S(2)}) %copy-start) | copy-done | bytes 1769496
  11.6 0.0 copy-start.1
  11.6 1.2 %copy-done.1 = bf16[3,3,3,128,128]{4,3,2,1,0:T(8,128)(2,1)S(1)} copy-done((bf16[3,3,3,128,128]{4,3,2,1,0:T(8,128)(2,1)S(1)}, bf16[3,3,3,128,128]{4,3,2,1,0:T(8,128)(2,1)}, u32[]{:S(2)}) %copy-start.1) | copy-done | bytes 884760
  12.7 1.0 %kernels.1 = (bf16[3,2,2,256,512]{4,3,2,1,0:T(8,128)(2,1)S(1)}, bf16[3,3,2,256,256]{4,3,2,1,0:T(8,128)(2,1)S(1)}) custom-call(bf16[3,3,3,256,128]{4,3,2,1,0:T(8,128)(2,1)S(1)} %copy-done, bf16[3,3,3,128,128]{4,3,2,1,0:T(8,128)(2,1)S(1)} %copy-done.1), custom_call_target="tpu_custom_call" | custom-call | bytes 8159232 | tf_op jit(solution)/shard_map/kernels/pallas_call | solution.py:19
  13.8 0.0 collective-permute-done.2.refs_1_
  13.8 0.2 strips.1
  14.0 1.8 %collective-permute-start.3 = (bf16[2,80,256]{2,1,0:T(8,128)(2,1)S(1)}, bf16[2,80,256]{2,1,0:T(8,128)(2,1)S(1)}, u32[]{:S(2)}, u32[]{:S(2)}) collective-permute-start(bf16[2,80,256]{2,1,0:T(8,128)(2,1)S(1)} %get-tuple-element.13.refs_1_), channel_id=1, source_target_pairs={{0,1},{2,3},{1,0},{3,2},{4,5},{6,7},{5,4},{7,6},{8,9},{10,11},{9,8... | collective-permute-start | bytes 245768 | tf_op jit(solution)/shard_map/ppermute | solution.py:55
  15.8 2.5 %collective-permute-start.4 = (bf16[2,80,256]{2,1,0:T(8,128)(2,1)S(1)}, bf16[2,80,256]{2,1,0:T(8,128)(2,1)S(1)}, u32[]{:S(2)}, u32[]{:S(2)}) collective-permute-start(bf16[2,80,256]{2,1,0:T(8,128)(2,1)S(1)} %get-tuple-element.14.refs_2_), channel_id=1, source_target_pairs={{1,2},{3,0},{2,1},{0,3},{5,6},{7,4},{6,5},{4,7},{9,10},{11,8},{10,... | collective-permute-start | bytes 245768 | tf_op jit(solution)/shard_map/ppermute | solution.py:55
  18.3 0.0 copy-start.3
  18.3 2.0 %copy-done.3 = bf16[3,3,3,256,256]{4,3,2,1,0:T(8,128)(2,1)S(1)} copy-done((bf16[3,3,3,256,256]{4,3,2,1,0:T(8,128)(2,1)S(1)}, bf16[3,3,3,256,256]{4,3,2,1,0:T(8,128)(2,1)}, u32[]{:S(2)}) %copy-start.3) | copy-done | bytes 3538968
  20.3 2.9 %first_inner.1.refs_0_ = f32[8,6,16,256]{3,2,1,0:T(8,128)S(1)} custom-call(bf16[10,4,16,256]{3,2,1,0:T(8,128)(2,1)S(1)} %get-tuple-element.11.refs_0_, bf16[10,2,16,256]{3,2,1,0:T(8,128)(2,1)S(1)} %collective-permute-done.2.refs_1_, bf16[3,3,3,256,256]{4,3,2,1,0:T(8,128)(2,1)S(1)} %copy-done.3), custom_call_target="tpu_custom_call" | custom-call | flops 2717908992 | bytes 4816896 | tf_op jit(solution)/shard_map/first_inner/pallas_call | solution.py:19
  23.2 0.0 collective-permute-done.3.refs_3_
  23.2 0.0 collective-permute-done.4.refs_4_
  23.2 7.1 %rest.1 = bf16[4,8,32,128]{3,2,1,0:T(8,128)(2,1)} custom-call(f32[8,6,16,256]{3,2,1,0:T(8,128)S(1)} %first_inner.1.refs_0_, bf16[2,80,256]{2,1,0:T(8,128)(2,1)S(1)} %get-tuple-element.13.refs_1_, bf16[2,80,256]{2,1,0:T(8,128)(2,1)S(1)} %get-tuple-element.14.refs_2_, bf16[2,80,256]{2,1,0:T(8,128)(2,1)S(1)} %collective-permute-done.3.refs_3_, ...), custom_call_target="tpu_custom_call" | custom-call | flops 4000000000 | bytes 10420224 | tf_op jit(solution)/shard_map/rest/pallas_call | solution.py:19
  (1 shorter events, 0.0 us)
Async XLA Ops:
  0.0 9.0 %collective-permute-start.1 = (bf16[4,4,16,256]{3,2,1,0:T(8,128)(2,1)}, bf16[4,4,16,256]{3,2,1,0:T(8,128)(2,1)S(1)}, u32[]{:S(2)}, u32[]{:S(2)}) collective-permute-start(bf16[4,4,16,256]{3,2,1,0:T(8,128)(2,1)} %refs_0_.1), channel_id=1, source_target_pairs={{0,8},{8,16},{16,24},{24,0},{1,9},{9,17},{17,25},{25,1},{2,10},{10... | collective-permute-start | bytes 393224 | tf_op jit(solution)/shard_map/ppermute | solution.py:278
  3.8 5.2 %collective-permute-start = (bf16[2,4,16,256]{3,2,1,0:T(8,128)(2,1)S(1)}, bf16[2,4,16,256]{3,2,1,0:T(8,128)(2,1)S(1)}, u32[]{:S(2)}, u32[]{:S(2)}) collective-permute-start(bf16[2,4,16,256]{3,2,1,0:T(8,128)(2,1)S(1)} %slice.3), channel_id=1, source_target_pairs={{0,16},{8,24},{16,0},{24,8},{1,17},{9,25},{17,1},{25,9},{2,18},{10... | collective-permute-start | bytes 196616 | tf_op jit(solution)/shard_map/ppermute | solution.py:278
  9.0 0.9 %copy-start.2 = (bf16[4,4,16,256]{3,2,1,0:T(8,128)(2,1)S(1)}, bf16[4,4,16,256]{3,2,1,0:T(8,128)(2,1)}, u32[]{:S(2)}) copy-start(bf16[4,4,16,256]{3,2,1,0:T(8,128)(2,1)} %refs_0_.1) | copy-start | bytes 393220
  10.0 3.8 %collective-permute-start.2 = (bf16[10,2,16,256]{3,2,1,0:T(8,128)(2,1)S(1)}, bf16[10,2,16,256]{3,2,1,0:T(8,128)(2,1)S(1)}, u32[]{:S(2)}, u32[]{:S(2)}) collective-permute-start(bf16[10,2,16,256]{3,2,1,0:T(8,128)(2,1)S(1)} %get-tuple-element.12), channel_id=1, source_target_pairs={{0,4},{4,0},{1,5},{5,1},{2,6},{6,2},{3,7},{7,3},{8,12},{12,8},{9,1... | collective-permute-start | bytes 491528 | tf_op jit(solution)/shard_map/ppermute | solution.py:55
  10.1 1.5 %copy-start = (bf16[3,3,3,256,128]{4,3,2,1,0:T(8,128)(2,1)S(1)}, bf16[3,3,3,256,128]{4,3,2,1,0:T(8,128)(2,1)}, u32[]{:S(2)}) copy-start(bf16[3,3,3,256,128]{4,3,2,1,0:T(8,128)(2,1)} %second.1) | copy-start | bytes 5308420
  11.6 1.2 %copy-start.1 = (bf16[3,3,3,128,128]{4,3,2,1,0:T(8,128)(2,1)S(1)}, bf16[3,3,3,128,128]{4,3,2,1,0:T(8,128)(2,1)}, u32[]{:S(2)}) copy-start(bf16[3,3,3,128,128]{4,3,2,1,0:T(8,128)(2,1)} %third.1) | copy-start | bytes 2654212
  14.0 9.2 %collective-permute-start.3 = (bf16[2,80,256]{2,1,0:T(8,128)(2,1)S(1)}, bf16[2,80,256]{2,1,0:T(8,128)(2,1)S(1)}, u32[]{:S(2)}, u32[]{:S(2)}) collective-permute-start(bf16[2,80,256]{2,1,0:T(8,128)(2,1)S(1)} %get-tuple-element.13.refs_1_), channel_id=1, source_target_pairs={{0,1},{2,3},{1,0},{3,2},{4,5},{6,7},{5,4},{7,6},{8,9},{10,11},{9,8... | collective-permute-start | bytes 245768 | tf_op jit(solution)/shard_map/ppermute | solution.py:55
  15.8 7.4 %collective-permute-start.4 = (bf16[2,80,256]{2,1,0:T(8,128)(2,1)S(1)}, bf16[2,80,256]{2,1,0:T(8,128)(2,1)S(1)}, u32[]{:S(2)}, u32[]{:S(2)}) collective-permute-start(bf16[2,80,256]{2,1,0:T(8,128)(2,1)S(1)} %get-tuple-element.14.refs_2_), channel_id=1, source_target_pairs={{1,2},{3,0},{2,1},{0,3},{5,6},{7,4},{6,5},{4,7},{9,10},{11,8},{10,... | collective-permute-start | bytes 245768 | tf_op jit(solution)/shard_map/ppermute | solution.py:55
  18.3 2.0 %copy-start.3 = (bf16[3,3,3,256,256]{4,3,2,1,0:T(8,128)(2,1)S(1)}, bf16[3,3,3,256,256]{4,3,2,1,0:T(8,128)(2,1)}, u32[]{:S(2)}) copy-start(bf16[3,3,3,256,256]{4,3,2,1,0:T(8,128)(2,1)} %refs_5_.1) | copy-start | bytes 10616836

commit v3 on v2

--- a/solution.py
+++ b/solution.py
@@ -12,13 +12,13 @@
 RIM = 2
 
 
-def call(body, outs, args, scratch=(), flops=0, name=None):
+def call(body, outs, args, scratch=(), flops=0, name=None, space=pltpu.VMEM):
     spec = pl.BlockSpec(memory_space=pltpu.VMEM)
     outs = [jax.ShapeDtypeStruct(shape, kind) for shape, kind in outs]
     size = sum(a.size * a.dtype.itemsize for a in [*args, *outs])
     return pl.pallas_call(
-        body, out_shape=outs, in_specs=[spec] * len(args), out_specs=[spec] * len(outs),
-        scratch_shapes=[pltpu.VMEM(*s) for s in scratch], name=name,
+        body, out_shape=outs, in_specs=[pl.BlockSpec(memory_space=space)] * len(args), out_specs=[spec] * len(outs),
+        scratch_shapes=[pltpu.VMEM(*s) if isinstance(s, tuple) else s for s in scratch], name=name,
         cost_estimate=pl.CostEstimate(flops=flops, bytes_accessed=size, transcendentals=0),
         compiler_params=pltpu.CompilerParams(vmem_limit_bytes=32 << 20),
     )(*args)
@@ -126,10 +126,16 @@
     out[...] = found.reshape(out.shape)
 
 
-def kernels(second, third, summed, paired):
+def load(latent, first_from, second_from, third_from, own, first, summed, paired, second, third, sems):
+    pairs = [(second_from.at[a], second.at[a]) for a in range(3)]
+    pairs += [(third_from, third), (latent, own), (first_from, first)]
+    copies = [pltpu.make_async_copy(*pair, sems.at[k]) for k, pair in enumerate(pairs)]
+    for copy in copies:
+        copy.start()
     fine = second.shape[-1]
     reads = [[(0, 1), (2,)], [(0,), (1, 2)]]
     for a in range(3):
+        copies[a].wait()
         tap = [[second[a, b, e].astype(F32) for e in range(3)] for b in range(3)]
         for di in range(2):
             for dj in range(2):
@@ -139,6 +145,7 @@
                         at = (2 * py + px) * fine
                         summed[a, di, dj, :, at : at + fine] = sum(parts[1:], parts[0]).astype(BF)
     width, out = third.shape[-2:]
+    copies[3].wait()
     for a in range(3):
         for b in range(3):
             for dj in range(2):
@@ -147,6 +154,8 @@
                         e = 2 * dj + px - q
                         block = third[a, b, e] if 0 <= e < 3 else jnp.zeros((width, out), BF)
                         paired[a, b, dj, px * width : (px + 1) * width, q * out : (q + 1) * out] = block
+    copies[4].wait()
+    copies[5].wait()
 
 
 def rest(*refs, cols):
@@ -278,9 +287,15 @@
         got.insert(0, lax.ppermute(latent[frames - take :], "section", ring))
         pieces.insert(0, (take, by))
         left, by = left - take, by + 1
-    summed, paired = call(
-        kernels, [((3, 2, 2, mid, 4 * fine), BF), ((3, 3, 2, 2 * fine, 2 * last), BF)],
-        [w_second, w_third], name="kernels",
+    latent, w_first, summed, paired = call(
+        load,
+        [
+            (latent.shape, BF), (w_first.shape, BF),
+            ((3, 2, 2, mid, 4 * fine), BF), ((3, 3, 2, 2 * fine, 2 * last), BF),
+        ],
+        [latent, w_first, w_second, w_third],
+        [(w_second.shape, BF), (w_third.shape, BF), pltpu.SemaphoreType.DMA((6,))],
+        name="load", space=pltpu.HBM,
     )
     total = frames + EARLIER
     rounds = len(swaps(lax.axis_size("row")))

time: 30.6 us -> 30.7 us (level)
  Pallas kernels: 11.3 us -> 12.4 us
  waiting for transfers between devices: 3.68 us -> 2.78 us
    ppermute x2, waiting for transfers between devices: 3.67 us -> 0.01 us  [per_device(): got.insert(0, lax.ppermute(latent[frames - take:], 'section', ring))]
    ppermute x3, waiting for transfers between devices: 0.01 us -> 2.78 us  [exchange(): lax.ppermute(s, axis, pairs)]
    pallas_call x5, Pallas kernels: 11.3 us -> 12.4 us  [call(): pl.pallas_call(body, out_shape=outs, in_specs=[pl.BlockSpec(memory_space=...]
  transfers between devices with their start and end apart: 5 -> 5, of which waited for: 1 -> 2; matrix products, arithmetic and copies ran while one was open for 3% -> 3% of each run, Pallas kernels for 13% -> 17%
where the time goes in v3:
time: 30.7 us; the launch traced here: 30.4 us
  Pallas kernels  12.4 us (40%)
  starting transfers between devices  8.67 us (28%)
  local copies, waits for them, and re-layouts  6.42 us (21%)
  waiting for transfers between devices  2.78 us (9%)
    pallas_call x5, Pallas kernels, call(): pl.pallas_call(body, out_shape=outs, in_specs=[pl.BlockSpec(memory_space=...  12.4 us
    unnamed x8, local copies, waits for them, and re-layouts  5.55 us
    ppermute x2, starting transfers between devices, per_device(): got.insert(0, lax.ppermute(latent[frames - take:], 'section', ring))  4.49 us
    ppermute x3, starting transfers between devices, exchange(): lax.ppermute(s, axis, pairs)  4.19 us
    ppermute x3, waiting for transfers between devices, exchange(): lax.ppermute(s, axis, pairs)  2.78 us
    slice x1, local copies, waits for them, and re-layouts, per_device(): got.insert(0, lax.ppermute(latent[frames - take:], 'section', ring))  0.88 us
  transfers between devices with their start and end apart: 5, of which 2 were waited for; matrix products, arithmetic and copies ran while one was open for 3% of the time, Pallas kernels for 17%

profile of v3, /device:TPU:0, one launch (start us, length us, event | category | flops | bytes accessed | tf_op | source)
XLA Modules:
  0.0 30.4 jit_solution(14224547167973056596)
XLA Ops:
  0.0 3.0 %collective-permute-start.1 = (bf16[4,4,16,256]{3,2,1,0:T(8,128)(2,1)}, bf16[4,4,16,256]{3,2,1,0:T(8,128)(2,1)S(1)}, u32[]{:S(2)}, u32[]{:S(2)}) collective-permute-start(bf16[4,4,16,256]{3,2,1,0:T(8,128)(2,1)} %latent.1), channel_id=1, source_target_pairs={{0,8},{8,16},{16,24},{24,0},{1,9},{9,17},{17,25},{25,1},{2,10},{10... | collective-permute-start | bytes 393224 | tf_op jit(solution)/shard_map/ppermute | solution.py:287
  3.0 0.9 %slice.3 = bf16[2,4,16,256]{3,2,1,0:T(8,128)(2,1)S(1)} slice(bf16[4,4,16,256]{3,2,1,0:T(8,128)(2,1)} %latent.1), slice={[2:4], [0:4], [0:16], [0:256]} | slice | bytes 131072 | tf_op jit(solution)/shard_map/slice | solution.py:287
  3.8 1.5 %collective-permute-start = (bf16[2,4,16,256]{3,2,1,0:T(8,128)(2,1)S(1)}, bf16[2,4,16,256]{3,2,1,0:T(8,128)(2,1)S(1)}, u32[]{:S(2)}, u32[]{:S(2)}) collective-permute-start(bf16[2,4,16,256]{3,2,1,0:T(8,128)(2,1)S(1)} %slice.3), channel_id=1, source_target_pairs={{0,16},{8,24},{16,0},{24,8},{1,17},{9,25},{17,1},{25,9},{2,18},{10... | collective-permute-start | bytes 196616 | tf_op jit(solution)/shard_map/ppermute | solution.py:287
  5.4 0.0 copy-start
  5.4 2.0 %copy-done = bf16[3,3,3,256,256]{4,3,2,1,0:T(8,128)(2,1)S(1)} copy-done((bf16[3,3,3,256,256]{4,3,2,1,0:T(8,128)(2,1)S(1)}, bf16[3,3,3,256,256]{4,3,2,1,0:T(8,128)(2,1)}, u32[]{:S(2)}) %copy-start) | copy-done | bytes 3538968
  7.4 0.0 copy-start.1
  7.4 1.5 %copy-done.1 = bf16[3,3,3,256,128]{4,3,2,1,0:T(8,128)(2,1)S(1)} copy-done((bf16[3,3,3,256,128]{4,3,2,1,0:T(8,128)(2,1)S(1)}, bf16[3,3,3,256,128]{4,3,2,1,0:T(8,128)(2,1)}, u32[]{:S(2)}) %copy-start.1) | copy-done | bytes 1769496
  8.8 0.0 copy-start.2
  8.8 1.2 %copy-done.2 = bf16[3,3,3,128,128]{4,3,2,1,0:T(8,128)(2,1)S(1)} copy-done((bf16[3,3,3,128,128]{4,3,2,1,0:T(8,128)(2,1)S(1)}, bf16[3,3,3,128,128]{4,3,2,1,0:T(8,128)(2,1)}, u32[]{:S(2)}) %copy-start.2) | copy-done | bytes 884760
  10.0 0.0 copy-start.3
  10.0 0.9 %copy-done.3 = bf16[4,4,16,256]{3,2,1,0:T(8,128)(2,1)S(1)} copy-done((bf16[4,4,16,256]{3,2,1,0:T(8,128)(2,1)S(1)}, bf16[4,4,16,256]{3,2,1,0:T(8,128)(2,1)}, u32[]{:S(2)}) %copy-start.3) | copy-done | bytes 131096
  10.9 2.2 %load.1 = (bf16[4,4,16,256]{3,2,1,0:T(8,128)(2,1)S(1)}, bf16[3,3,3,256,256]{4,3,2,1,0:T(8,128)(2,1)S(1)}, bf16[3,2,2,256,512]{4,3,2,1,0:T(8,128)(2,1)S(1)}, bf16[3,3,2,256,256]{4,3,2,1,0:T(8,128)(2,1)S(1)}) custom-call(bf16[4,4,16,256]{3,2,1,0:T(8,128)(2,1)S(1)} %copy-done.3, bf16[3,3,3,256,256]{4,3,2,1,0:T(8,128)(2,1)S(1)} %copy-done, ...), custom_call_target="tpu_custom_call" | custom-call | bytes 15499264 | tf_op jit(solution)/shard_map/load/pallas_call | solution.py:19
  13.1 0.0 collective-permute-done.refs_1_
  13.2 0.0 collective-permute-done.1.refs_2_
  13.2 0.1 join_frames.1
  13.2 0.1 collective-permute-start.2
  13.3 1.4 %collective-permute-done.2.refs_1_ = bf16[10,2,16,256]{3,2,1,0:T(8,128)(2,1)S(1)} collective-permute-done((bf16[10,2,16,256]{3,2,1,0:T(8,128)(2,1)S(1)}, bf16[10,2,16,256]{3,2,1,0:T(8,128)(2,1)S(1)}, u32[]{:S(2)}, u32[]{:S(2)}) %collective-permute-start.2) | collective-permute-done | bytes 163872 | tf_op jit(solution)/shard_map/ppermute | solution.py:55
  14.7 0.2 strips.1
  14.9 1.6 %collective-permute-start.3 = (bf16[2,80,256]{2,1,0:T(8,128)(2,1)S(1)}, bf16[2,80,256]{2,1,0:T(8,128)(2,1)S(1)}, u32[]{:S(2)}, u32[]{:S(2)}) collective-permute-start(bf16[2,80,256]{2,1,0:T(8,128)(2,1)S(1)} %get-tuple-element.17.refs_1_), channel_id=1, source_target_pairs={{0,1},{2,3},{1,0},{3,2},{4,5},{6,7},{5,4},{7,6},{8,9},{10,11},{9,8... | collective-permute-start | bytes 245768 | tf_op jit(solution)/shard_map/ppermute | solution.py:55
  16.5 2.5 %collective-permute-start.4 = (bf16[2,80,256]{2,1,0:T(8,128)(2,1)S(1)}, bf16[2,80,256]{2,1,0:T(8,128)(2,1)S(1)}, u32[]{:S(2)}, u32[]{:S(2)}) collective-permute-start(bf16[2,80,256]{2,1,0:T(8,128)(2,1)S(1)} %get-tuple-element.18.refs_2_), channel_id=1, source_target_pairs={{1,2},{3,0},{2,1},{0,3},{5,6},{7,4},{6,5},{4,7},{9,10},{11,8},{10,... | collective-permute-start | bytes 245768 | tf_op jit(solution)/shard_map/ppermute | solution.py:55
  19.0 2.9 %first_inner.1.refs_0_ = f32[8,6,16,256]{3,2,1,0:T(8,128)S(1)} custom-call(bf16[10,4,16,256]{3,2,1,0:T(8,128)(2,1)S(1)} %get-tuple-element.14.refs_0_, bf16[10,2,16,256]{3,2,1,0:T(8,128)(2,1)S(1)} %collective-permute-done.2.refs_1_, bf16[3,3,3,256,256]{4,3,2,1,0:T(8,128)(2,1)S(1)} %get-tuple-element.16.refs_2_.refs_5_), custom_call_target="tpu_custom_call" | custom-call | flops 2717908992 | bytes 4816896 | tf_op jit(solution)/shard_map/first_inner/pallas_call | solution.py:19
  21.9 0.0 collective-permute-done.3.refs_3_
  21.9 1.4 %collective-permute-done.4.refs_4_ = bf16[2,80,256]{2,1,0:T(8,128)(2,1)S(1)} collective-permute-done((bf16[2,80,256]{2,1,0:T(8,128)(2,1)S(1)}, bf16[2,80,256]{2,1,0:T(8,128)(2,1)S(1)}, u32[]{:S(2)}, u32[]{:S(2)}) %collective-permute-start.4) | collective-permute-done | bytes 81952 | tf_op jit(solution)/shard_map/ppermute | solution.py:55
  23.3 7.1 %rest.1 = bf16[4,8,32,128]{3,2,1,0:T(8,128)(2,1)} custom-call(f32[8,6,16,256]{3,2,1,0:T(8,128)S(1)} %first_inner.1.refs_0_, bf16[2,80,256]{2,1,0:T(8,128)(2,1)S(1)} %get-tuple-element.17.refs_1_, bf16[2,80,256]{2,1,0:T(8,128)(2,1)S(1)} %get-tuple-element.18.refs_2_, bf16[2,80,256]{2,1,0:T(8,128)(2,1)S(1)} %collective-permute-done.3.refs_3_, ...), custom_call_target="tpu_custom_call" | custom-call | flops 4000000000 | bytes 10420224 | tf_op jit(solution)/shard_map/rest/pallas_call | solution.py:19
Async XLA Ops:
  0.0 13.2 %collective-permute-start.1 = (bf16[4,4,16,256]{3,2,1,0:T(8,128)(2,1)}, bf16[4,4,16,256]{3,2,1,0:T(8,128)(2,1)S(1)}, u32[]{:S(2)}, u32[]{:S(2)}) collective-permute-start(bf16[4,4,16,256]{3,2,1,0:T(8,128)(2,1)} %latent.1), channel_id=1, source_target_pairs={{0,8},{8,16},{16,24},{24,0},{1,9},{9,17},{17,25},{25,1},{2,10},{10... | collective-permute-start | bytes 393224 | tf_op jit(solution)/shard_map/ppermute | solution.py:287
  3.8 9.3 %collective-permute-start = (bf16[2,4,16,256]{3,2,1,0:T(8,128)(2,1)S(1)}, bf16[2,4,16,256]{3,2,1,0:T(8,128)(2,1)S(1)}, u32[]{:S(2)}, u32[]{:S(2)}) collective-permute-start(bf16[2,4,16,256]{3,2,1,0:T(8,128)(2,1)S(1)} %slice.3), channel_id=1, source_target_pairs={{0,16},{8,24},{16,0},{24,8},{1,17},{9,25},{17,1},{25,9},{2,18},{10... | collective-permute-start | bytes 196616 | tf_op jit(solution)/shard_map/ppermute | solution.py:287
  5.4 2.0 %copy-start = (bf16[3,3,3,256,256]{4,3,2,1,0:T(8,128)(2,1)S(1)}, bf16[3,3,3,256,256]{4,3,2,1,0:T(8,128)(2,1)}, u32[]{:S(2)}) copy-start(bf16[3,3,3,256,256]{4,3,2,1,0:T(8,128)(2,1)} %first_from.1) | copy-start | bytes 10616836
  7.4 1.5 %copy-start.1 = (bf16[3,3,3,256,128]{4,3,2,1,0:T(8,128)(2,1)S(1)}, bf16[3,3,3,256,128]{4,3,2,1,0:T(8,128)(2,1)}, u32[]{:S(2)}) copy-start(bf16[3,3,3,256,128]{4,3,2,1,0:T(8,128)(2,1)} %second_from.1) | copy-start | bytes 5308420
  8.8 1.2 %copy-start.2 = (bf16[3,3,3,128,128]{4,3,2,1,0:T(8,128)(2,1)S(1)}, bf16[3,3,3,128,128]{4,3,2,1,0:T(8,128)(2,1)}, u32[]{:S(2)}) copy-start(bf16[3,3,3,128,128]{4,3,2,1,0:T(8,128)(2,1)} %third_from.1) | copy-start | bytes 2654212
  10.0 0.9 %copy-start.3 = (bf16[4,4,16,256]{3,2,1,0:T(8,128)(2,1)S(1)}, bf16[4,4,16,256]{3,2,1,0:T(8,128)(2,1)}, u32[]{:S(2)}) copy-start(bf16[4,4,16,256]{3,2,1,0:T(8,128)(2,1)} %latent.1) | copy-start | bytes 393220
  13.2 1.5 %collective-permute-start.2 = (bf16[10,2,16,256]{3,2,1,0:T(8,128)(2,1)S(1)}, bf16[10,2,16,256]{3,2,1,0:T(8,128)(2,1)S(1)}, u32[]{:S(2)}, u32[]{:S(2)}) collective-permute-start(bf16[10,2,16,256]{3,2,1,0:T(8,128)(2,1)S(1)} %get-tuple-element.15), channel_id=1, source_target_pairs={{0,4},{4,0},{1,5},{5,1},{2,6},{6,2},{3,7},{7,3},{8,12},{12,8},{9,1... | collective-permute-start | bytes 491528 | tf_op jit(solution)/shard_map/ppermute | solution.py:55
  14.9 7.0 %collective-permute-start.3 = (bf16[2,80,256]{2,1,0:T(8,128)(2,1)S(1)}, bf16[2,80,256]{2,1,0:T(8,128)(2,1)S(1)}, u32[]{:S(2)}, u32[]{:S(2)}) collective-permute-start(bf16[2,80,256]{2,1,0:T(8,128)(2,1)S(1)} %get-tuple-element.17.refs_1_), channel_id=1, source_target_pairs={{0,1},{2,3},{1,0},{3,2},{4,5},{6,7},{5,4},{7,6},{8,9},{10,11},{9,8... | collective-permute-start | bytes 245768 | tf_op jit(solution)/shard_map/ppermute | solution.py:55
  16.5 6.8 %collective-permute-start.4 = (bf16[2,80,256]{2,1,0:T(8,128)(2,1)S(1)}, bf16[2,80,256]{2,1,0:T(8,128)(2,1)S(1)}, u32[]{:S(2)}, u32[]{:S(2)}) collective-permute-start(bf16[2,80,256]{2,1,0:T(8,128)(2,1)S(1)} %get-tuple-element.18.refs_2_), channel_id=1, source_target_pairs={{1,2},{3,0},{2,1},{0,3},{5,6},{7,4},{6,5},{4,7},{9,10},{11,8},{10,... | collective-permute-start | bytes 245768 | tf_op jit(solution)/shard_map/ppermute | solution.py:55

commit v4 on v2

--- a/solution.py
+++ b/solution.py
@@ -25,6 +25,7 @@
 
 
 LANES = 128
+COVER = 4 * 10**9
 SLACK = 8
 
 
@@ -67,8 +68,8 @@
 
 
 def join_frames(*refs, pieces, rounds):
-    own, got = refs[0], refs[1 : 1 + len(pieces)]
-    field, sends = refs[1 + len(pieces)], refs[2 + len(pieces) :]
+    own, got = refs[0], refs[2 : 2 + len(pieces)]
+    field, sends = refs[2 + len(pieces)], refs[3 + len(pieces) :]
     place, at = lax.axis_index("section"), 0
     for (take, by), ref in zip(pieces, got):
         field[at : at + take] = jnp.where(place >= by, ref[...], jnp.zeros_like(ref))
@@ -126,7 +127,8 @@
     out[...] = found.reshape(out.shape)
 
 
-def kernels(second, third, summed, paired):
+def kernels(second, third, summed, paired, ready):
+    ready[...] = jnp.zeros_like(ready)
     fine = second.shape[-1]
     reads = [[(0, 1), (2,)], [(0,), (1, 2)]]
     for a in range(3):
@@ -278,16 +280,17 @@
         got.insert(0, lax.ppermute(latent[frames - take :], "section", ring))
         pieces.insert(0, (take, by))
         left, by = left - take, by + 1
-    summed, paired = call(
-        kernels, [((3, 2, 2, mid, 4 * fine), BF), ((3, 3, 2, 2 * fine, 2 * last), BF)],
-        [w_second, w_third], name="kernels",
+    summed, paired, ready = call(
+        kernels,
+        [((3, 2, 2, mid, 4 * fine), BF), ((3, 3, 2, 2 * fine, 2 * last), BF), ((8, LANES), F32)],
+        [w_second, w_third], flops=COVER, name="kernels",
     )
     total = frames + EARLIER
     rounds = len(swaps(lax.axis_size("row")))
     field, *sends = call(
         functools.partial(join_frames, pieces=pieces, rounds=rounds),
         [((total, height, breadth, width), BF)] + [((total, RIM, breadth, width), BF)] * rounds,
-        [latent, *got], name="join_frames",
+        [latent, ready, *got], flops=COVER, name="join_frames",
     )
     rows_got = exchange(sends, "row")
     tall = height + 2 * RIM

time: 30.6 us -> 26.7 us (0.87)
  local copies, waits for them, and re-layouts: 6.42 us -> 3.53 us
  waiting for transfers between devices: 3.68 us -> 2.78 us
    ppermute x2, waiting for transfers between devices: 3.67 us -> 0.01 us  [per_device(): got.insert(0, lax.ppermute(latent[frames - take:], 'section', ring))]
    unnamed x8, local copies, waits for them, and re-layouts: 5.54 us -> 2.65 us
    ppermute x3, waiting for transfers between devices: 0.01 us -> 2.77 us  [exchange(): lax.ppermute(s, axis, pairs)]
  transfers between devices with their start and end apart: 5 -> 5, of which waited for: 1 -> 2; matrix products, arithmetic and copies ran while one was open for 3% -> 3% of each run, Pallas kernels for 13% -> 15%
where the time goes in v4:
time: 26.7 us; the launch traced here: 26.5 us
  Pallas kernels  11.3 us (42%)
  starting transfers between devices  8.81 us (33%)
  local copies, waits for them, and re-layouts  3.53 us (13%)
  waiting for transfers between devices  2.78 us (10%)
    pallas_call x5, Pallas kernels, call(): pl.pallas_call(body, out_shape=outs, in_specs=[spec] * len(args), out_spe...  11.3 us
    ppermute x2, starting transfers between devices, per_device(): got.insert(0, lax.ppermute(latent[frames - take:], 'section', ring))  4.49 us
    ppermute x3, starting transfers between devices, exchange(): lax.ppermute(s, axis, pairs)  4.32 us
    ppermute x3, waiting for transfers between devices, exchange(): lax.ppermute(s, axis, pairs)  2.77 us
    unnamed x8, local copies, waits for them, and re-layouts  2.65 us
    slice x1, local copies, waits for them, and re-layouts, per_device(): got.insert(0, lax.ppermute(latent[frames - take:], 'section', ring))  0.88 us
  transfers between devices with their start and end apart: 5, of which 2 were waited for; matrix products, arithmetic and copies ran while one was open for 3% of the time, Pallas kernels for 15%

profile of v4, /device:TPU:0, one launch (start us, length us, event | category | flops | bytes accessed | tf_op | source)
XLA Modules:
  0.0 26.5 jit_solution(9109302722699366097)
XLA Ops:
  0.0 3.0 %collective-permute-start.1 = (bf16[4,4,16,256]{3,2,1,0:T(8,128)(2,1)}, bf16[4,4,16,256]{3,2,1,0:T(8,128)(2,1)S(1)}, u32[]{:S(2)}, u32[]{:S(2)}) collective-permute-start(bf16[4,4,16,256]{3,2,1,0:T(8,128)(2,1)} %refs_0_.1), channel_id=1, source_target_pairs={{0,8},{8,16},{16,24},{24,0},{1,9},{9,17},{17,25},{25,1},{2,10},{10... | collective-permute-start | bytes 393224 | tf_op jit(solution)/shard_map/ppermute | solution.py:280
  3.0 0.9 %slice.3 = bf16[2,4,16,256]{3,2,1,0:T(8,128)(2,1)S(1)} slice(bf16[4,4,16,256]{3,2,1,0:T(8,128)(2,1)} %refs_0_.1), slice={[2:4], [0:4], [0:16], [0:256]} | slice | bytes 131072 | tf_op jit(solution)/shard_map/slice | solution.py:280
  3.8 0.0 copy-start
  3.8 1.5 %collective-permute-start = (bf16[2,4,16,256]{3,2,1,0:T(8,128)(2,1)S(1)}, bf16[2,4,16,256]{3,2,1,0:T(8,128)(2,1)S(1)}, u32[]{:S(2)}, u32[]{:S(2)}) collective-permute-start(bf16[2,4,16,256]{3,2,1,0:T(8,128)(2,1)S(1)} %slice.3), channel_id=1, source_target_pairs={{0,16},{8,24},{16,0},{24,8},{1,17},{9,25},{17,1},{25,9},{2,18},{10... | collective-permute-start | bytes 196616 | tf_op jit(solution)/shard_map/ppermute | solution.py:280
  5.4 0.0 copy-start.2
  5.4 1.5 %copy-done.2 = bf16[3,3,3,256,128]{4,3,2,1,0:T(8,128)(2,1)S(1)} copy-done((bf16[3,3,3,256,128]{4,3,2,1,0:T(8,128)(2,1)S(1)}, bf16[3,3,3,256,128]{4,3,2,1,0:T(8,128)(2,1)}, u32[]{:S(2)}) %copy-start.2) | copy-done | bytes 1769496
  6.8 0.0 copy-start.3
  6.8 1.2 %copy-done.3 = bf16[3,3,3,128,128]{4,3,2,1,0:T(8,128)(2,1)S(1)} copy-done((bf16[3,3,3,128,128]{4,3,2,1,0:T(8,128)(2,1)S(1)}, bf16[3,3,3,128,128]{4,3,2,1,0:T(8,128)(2,1)}, u32[]{:S(2)}) %copy-start.3) | copy-done | bytes 884760
  8.0 1.0 %kernels.1 = (bf16[3,2,2,256,512]{4,3,2,1,0:T(8,128)(2,1)S(1)}, bf16[3,3,2,256,256]{4,3,2,1,0:T(8,128)(2,1)S(1)}, f32[8,128]{1,0:T(8,128)S(1)}) custom-call(bf16[3,3,3,256,128]{4,3,2,1,0:T(8,128)(2,1)S(1)} %copy-done.2, bf16[3,3,3,128,128]{4,3,2,1,0:T(8,128)(2,1)S(1)} %copy-done.3), custom_call_target="tpu_custom_call" | custom-call | flops 4000000000 | bytes 8163328 | tf_op jit(solution)/shard_map/kernels/pallas_call | solution.py:19
  9.1 0.0 collective-permute-done.refs_2_
  9.1 0.0 collective-permute-done.1.refs_3_
  9.1 0.0 copy-done
  9.1 0.0 copy-start.1
  9.1 0.1 join_frames.1
  9.2 0.1 collective-permute-start.2
  9.2 1.4 %collective-permute-done.2.refs_1_ = bf16[10,2,16,256]{3,2,1,0:T(8,128)(2,1)S(1)} collective-permute-done((bf16[10,2,16,256]{3,2,1,0:T(8,128)(2,1)S(1)}, bf16[10,2,16,256]{3,2,1,0:T(8,128)(2,1)S(1)}, u32[]{:S(2)}, u32[]{:S(2)}) %collective-permute-start.2) | collective-permute-done | bytes 163872 | tf_op jit(solution)/shard_map/ppermute | solution.py:56
  10.6 0.2 strips.1
  10.8 1.8 %collective-permute-start.3 = (bf16[2,80,256]{2,1,0:T(8,128)(2,1)S(1)}, bf16[2,80,256]{2,1,0:T(8,128)(2,1)S(1)}, u32[]{:S(2)}, u32[]{:S(2)}) collective-permute-start(bf16[2,80,256]{2,1,0:T(8,128)(2,1)S(1)} %get-tuple-element.15.refs_1_), channel_id=1, source_target_pairs={{0,1},{2,3},{1,0},{3,2},{4,5},{6,7},{5,4},{7,6},{8,9},{10,11},{9,8... | collective-permute-start | bytes 245768 | tf_op jit(solution)/shard_map/ppermute | solution.py:56
  12.6 2.5 %collective-permute-start.4 = (bf16[2,80,256]{2,1,0:T(8,128)(2,1)S(1)}, bf16[2,80,256]{2,1,0:T(8,128)(2,1)S(1)}, u32[]{:S(2)}, u32[]{:S(2)}) collective-permute-start(bf16[2,80,256]{2,1,0:T(8,128)(2,1)S(1)} %get-tuple-element.16.refs_2_), channel_id=1, source_target_pairs={{1,2},{3,0},{2,1},{0,3},{5,6},{7,4},{6,5},{4,7},{9,10},{11,8},{10,... | collective-permute-start | bytes 245768 | tf_op jit(solution)/shard_map/ppermute | solution.py:56
  15.1 0.0 copy-done.1
  15.1 2.9 %first_inner.1.refs_0_ = f32[8,6,16,256]{3,2,1,0:T(8,128)S(1)} custom-call(bf16[10,4,16,256]{3,2,1,0:T(8,128)(2,1)S(1)} %get-tuple-element.13.refs_0_, bf16[10,2,16,256]{3,2,1,0:T(8,128)(2,1)S(1)} %collective-permute-done.2.refs_1_, bf16[3,3,3,256,256]{4,3,2,1,0:T(8,128)(2,1)S(1)} %copy-done.1), custom_call_target="tpu_custom_call" | custom-call | flops 2717908992 | bytes 4816896 | tf_op jit(solution)/shard_map/first_inner/pallas_call | solution.py:19
  18.0 0.0 collective-permute-done.3.refs_3_
  18.0 1.4 %collective-permute-done.4.refs_4_ = bf16[2,80,256]{2,1,0:T(8,128)(2,1)S(1)} collective-permute-done((bf16[2,80,256]{2,1,0:T(8,128)(2,1)S(1)}, bf16[2,80,256]{2,1,0:T(8,128)(2,1)S(1)}, u32[]{:S(2)}, u32[]{:S(2)}) %collective-permute-start.4) | collective-permute-done | bytes 81952 | tf_op jit(solution)/shard_map/ppermute | solution.py:56
  19.4 7.1 %rest.1 = bf16[4,8,32,128]{3,2,1,0:T(8,128)(2,1)} custom-call(f32[8,6,16,256]{3,2,1,0:T(8,128)S(1)} %first_inner.1.refs_0_, bf16[2,80,256]{2,1,0:T(8,128)(2,1)S(1)} %get-tuple-element.15.refs_1_, bf16[2,80,256]{2,1,0:T(8,128)(2,1)S(1)} %get-tuple-element.16.refs_2_, bf16[2,80,256]{2,1,0:T(8,128)(2,1)S(1)} %collective-permute-done.3.refs_3_, ...), custom_call_target="tpu_custom_call" | custom-call | flops 4000000000 | bytes 10420224 | tf_op jit(solution)/shard_map/rest/pallas_call | solution.py:19
Async XLA Ops:
  0.0 9.1 %collective-permute-start.1 = (bf16[4,4,16,256]{3,2,1,0:T(8,128)(2,1)}, bf16[4,4,16,256]{3,2,1,0:T(8,128)(2,1)S(1)}, u32[]{:S(2)}, u32[]{:S(2)}) collective-permute-start(bf16[4,4,16,256]{3,2,1,0:T(8,128)(2,1)} %refs_0_.1), channel_id=1, source_target_pairs={{0,8},{8,16},{16,24},{24,0},{1,9},{9,17},{17,25},{25,1},{2,10},{10... | collective-permute-start | bytes 393224 | tf_op jit(solution)/shard_map/ppermute | solution.py:280
  3.8 5.2 %copy-start = (bf16[4,4,16,256]{3,2,1,0:T(8,128)(2,1)S(1)}, bf16[4,4,16,256]{3,2,1,0:T(8,128)(2,1)}, u32[]{:S(2)}) copy-start(bf16[4,4,16,256]{3,2,1,0:T(8,128)(2,1)} %refs_0_.1) | copy-start | bytes 393220
  3.8 5.2 %collective-permute-start = (bf16[2,4,16,256]{3,2,1,0:T(8,128)(2,1)S(1)}, bf16[2,4,16,256]{3,2,1,0:T(8,128)(2,1)S(1)}, u32[]{:S(2)}, u32[]{:S(2)}) collective-permute-start(bf16[2,4,16,256]{3,2,1,0:T(8,128)(2,1)S(1)} %slice.3), channel_id=1, source_target_pairs={{0,16},{8,24},{16,0},{24,8},{1,17},{9,25},{17,1},{25,9},{2,18},{10... | collective-permute-start | bytes 196616 | tf_op jit(solution)/shard_map/ppermute | solution.py:280
  5.4 1.5 %copy-start.2 = (bf16[3,3,3,256,128]{4,3,2,1,0:T(8,128)(2,1)S(1)}, bf16[3,3,3,256,128]{4,3,2,1,0:T(8,128)(2,1)}, u32[]{:S(2)}) copy-start(bf16[3,3,3,256,128]{4,3,2,1,0:T(8,128)(2,1)} %second.1) | copy-start | bytes 5308420
  6.8 1.2 %copy-start.3 = (bf16[3,3,3,128,128]{4,3,2,1,0:T(8,128)(2,1)S(1)}, bf16[3,3,3,128,128]{4,3,2,1,0:T(8,128)(2,1)}, u32[]{:S(2)}) copy-start(bf16[3,3,3,128,128]{4,3,2,1,0:T(8,128)(2,1)} %third.1) | copy-start | bytes 2654212
  9.1 6.0 %copy-start.1 = (bf16[3,3,3,256,256]{4,3,2,1,0:T(8,128)(2,1)S(1)}, bf16[3,3,3,256,256]{4,3,2,1,0:T(8,128)(2,1)}, u32[]{:S(2)}) copy-start(bf16[3,3,3,256,256]{4,3,2,1,0:T(8,128)(2,1)} %refs_5_.1) | copy-start | bytes 10616836
  9.2 1.5 %collective-permute-start.2 = (bf16[10,2,16,256]{3,2,1,0:T(8,128)(2,1)S(1)}, bf16[10,2,16,256]{3,2,1,0:T(8,128)(2,1)S(1)}, u32[]{:S(2)}, u32[]{:S(2)}) collective-permute-start(bf16[10,2,16,256]{3,2,1,0:T(8,128)(2,1)S(1)} %get-tuple-element.14), channel_id=1, source_target_pairs={{0,4},{4,0},{1,5},{5,1},{2,6},{6,2},{3,7},{7,3},{8,12},{12,8},{9,1... | collective-permute-start | bytes 491528 | tf_op jit(solution)/shard_map/ppermute | solution.py:56
  10.8 7.2 %collective-permute-start.3 = (bf16[2,80,256]{2,1,0:T(8,128)(2,1)S(1)}, bf16[2,80,256]{2,1,0:T(8,128)(2,1)S(1)}, u32[]{:S(2)}, u32[]{:S(2)}) collective-permute-start(bf16[2,80,256]{2,1,0:T(8,128)(2,1)S(1)} %get-tuple-element.15.refs_1_), channel_id=1, source_target_pairs={{0,1},{2,3},{1,0},{3,2},{4,5},{6,7},{5,4},{7,6},{8,9},{10,11},{9,8... | collective-permute-start | bytes 245768 | tf_op jit(solution)/shard_map/ppermute | solution.py:56
  12.6 6.8 %collective-permute-start.4 = (bf16[2,80,256]{2,1,0:T(8,128)(2,1)S(1)}, bf16[2,80,256]{2,1,0:T(8,128)(2,1)S(1)}, u32[]{:S(2)}, u32[]{:S(2)}) collective-permute-start(bf16[2,80,256]{2,1,0:T(8,128)(2,1)S(1)} %get-tuple-element.16.refs_2_), channel_id=1, source_target_pairs={{1,2},{3,0},{2,1},{0,3},{5,6},{7,4},{6,5},{4,7},{9,10},{11,8},{10,... | collective-permute-start | bytes 245768 | tf_op jit(solution)/shard_map/ppermute | solution.py:56

commit v5 on v4

--- a/solution.py
+++ b/solution.py
@@ -29,10 +29,9 @@
 SLACK = 8
 
 
-def put(ref, rows, value, add=False):
+def put(ref, rows, value):
     for k in range(ref.shape[0]):
-        block = value[:, k * LANES : (k + 1) * LANES]
-        ref[k, rows, :] = ref[k, rows, :] + block if add else block
+        ref[k, rows, :] = value[:, k * LANES : (k + 1) * LANES]
 
 
 def take(ref, rows, blocks=None):
@@ -67,7 +66,7 @@
     return jnp.where(place > 0, before, zero), jnp.where(place < size - 1, after, zero)
 
 
-def join_frames(*refs, pieces, rounds):
+def join_frames(*refs, pieces):
     own, got = refs[0], refs[2 : 2 + len(pieces)]
     field, sends = refs[2 + len(pieces)], refs[3 + len(pieces) :]
     place, at = lax.axis_index("section"), 0
@@ -77,48 +76,65 @@
     field[at:] = own[...]
     even = lax.axis_index("row") % 2 == 0
     last = field.shape[1] - RIM
-    for k in range(rounds):
+    for k in range(len(sends)):
         start = jnp.where(even, 0, last) if k else jnp.where(even, last, 0)
         sends[k][...] = field[:, pl.ds(start, RIM)]
 
 
-def strips(*refs, rows):
+def rims(field, got, whole):
+    if whole:
+        got = [jnp.where(lax.axis_index("row") == 0, got[0][:, :RIM], got[0][:, -RIM:])]
+    else:
+        got = [g[...] for g in got]
+    return arrived("row", got)
+
+
+def strips(*refs, rows, whole):
     field, got = refs[0], refs[1 : 1 + rows]
-    sends, wide = refs[1 + rows : -1], refs[-1]
+    sends, own, wide = refs[1 + rows : -2], refs[-2], refs[-1]
     frames, height, breadth, width = field.shape
-    before, after = arrived("row", [g[...].astype(F32) for g in got])
-    tall = height + 2 * RIM
+    if whole:
+        upper = lax.axis_index("row") == 0
+    else:
+        before, after = rims(field, got, whole)
+    size = wide.shape[1] // frames
+    tall = size // breadth
     for t in range(frames):
-        whole = jnp.concatenate([before[t], field[t].astype(F32), after[t]], 0)
-        size = tall * breadth
-        put(wide, slice(t * size, (t + 1) * size), whole.reshape(size, width))
-    first, last = (
-        [take(wide, pl.ds(c, frames * tall, stride=breadth)).astype(BF) for c in cols]
-        for cols in ([0, 1], [breadth - 2, breadth - 1])
-    )
-    even = lax.axis_index("col") % 2 == 0
+        if whole:
+            a, b = field[t].astype(F32), got[0][t].astype(F32)
+            rows_of = [jnp.where(upper, a, b), jnp.where(upper, b, a)]
+        else:
+            rows_of = [before[t].astype(F32), field[t].astype(F32), after[t].astype(F32)]
+        put(wide, slice(t * size, (t + 1) * size), jnp.concatenate(rows_of, 0).reshape(size, width))
+    for i, c in enumerate([0, 1, breadth - 2, breadth - 1]):
+        own[i] = take(wide, pl.ds(c, frames * tall, stride=breadth)).astype(BF)
+    right = lax.axis_index("col") % 2 == 0
+    if whole:
+        right = right == (lax.axis_index("row") == 0)
     for k, send in enumerate(sends):
-        for i in range(RIM):
-            send[i] = jnp.where(even, first[i], last[i]) if k else jnp.where(even, last[i], first[i])
-
-
-def first_inner(*refs, rows):
-    field, got, kernel, out, wide = refs[0], refs[1 : 1 + rows], refs[1 + rows], refs[-2], refs[-1]
-    frames, height, breadth, width = field.shape
-    before, after = arrived("row", [g[...] for g in got])
+        start = jnp.where(right, 0, RIM) if k else jnp.where(right, RIM, 0)
+        send[...] = own[pl.ds(start, RIM)]
+
+
+def first_inner(*refs, rows, whole, begin):
+    field, got, kernel = refs[0], refs[1 : 1 + rows], refs[1 + rows]
+    out, wide = refs[-2:]
+    count = out.shape[0]
+    _, height, breadth, width = field.shape
+    before, after = rims(field, got, whole)
     tall = height + 2 * RIM
     size = tall * breadth
     col = lax.broadcasted_iota(jnp.int32, (size, width), 0) % breadth
-    for t in range(frames):
-        whole = jnp.concatenate([before[t], field[t], after[t]], 0)
-        wide[1, t] = whole
-        flat = whole.reshape(size, width).astype(F32)
+    for t in range(count + 2):
+        rows_of = jnp.concatenate([before[begin + t], field[begin + t], after[begin + t]], 0)
+        wide[1, t] = rows_of
+        flat = rows_of.reshape(size, width).astype(F32)
         lower = jnp.where(col == 0, 0.0, pltpu.roll(flat, 1, 0))
         upper = jnp.where(col == breadth - 1, 0.0, pltpu.roll(flat, size - 1, 0))
-        wide[0, t] = lower.astype(BF).reshape(whole.shape)
-        wide[2, t] = upper.astype(BF).reshape(whole.shape)
+        wide[0, t] = lower.astype(BF).reshape(rows_of.shape)
+        wide[2, t] = upper.astype(BF).reshape(rows_of.shape)
     taps = [
-        wide[e, a : a + frames - 2, b : b + tall - 2].reshape(-1, width)
+        wide[e, a : a + count, b : b + tall - 2].reshape(-1, width)
         for a in range(3) for b in range(3) for e in range(3)
     ]
     found = jnp.dot(
@@ -151,50 +167,61 @@
                         paired[a, b, dj, px * width : (px + 1) * width, q * out : (q + 1) * out] = block
 
 
-def rest(*refs, cols):
-    inner, sent, got = refs[0], refs[1 : 1 + cols], refs[1 + cols : 1 + 2 * cols]
-    kernel, summed, paired, out = refs[1 + 2 * cols : 5 + 2 * cols]
-    edge, coarse, near, far, grown, fine, spread = refs[5 + 2 * cols :]
-    frames, rows, breadth, width = inner.shape
+def rest(*refs, cols, parts, whole):
+    inner, own, got = refs[:parts], refs[parts], refs[parts + 1 : parts + 1 + cols]
+    kernel, summed, paired, out = refs[parts + 1 + cols : parts + 5 + cols]
+    edge, coarse, near, far, grown, fine, spread = refs[parts + 5 + cols :]
+    rows, breadth, width = inner[0].shape[1:]
+    frames = sum(part.shape[0] for part in inner)
     tall = rows + 2
     top, bottom = lax.axis_index("row") == 0, lax.axis_index("row") == lax.axis_size("row") - 1
     leftmost, rightmost = lax.axis_index("col") == 0, lax.axis_index("col") == lax.axis_size("col") - 1
 
-    even = lax.axis_index("col") % 2 == 0
-    before, after = arrived("col", [g[...] for g in got])
-    if cols == 1:
-        own = [sent[0][0], sent[0][1]]
-    else:
-        own = [jnp.where(even, sent[1][0], sent[0][0]), jnp.where(even, sent[0][1], sent[1][1])]
-    size, count = frames * tall, before.shape[1]
-    for i, strip in enumerate([before[0], before[1], own[0], own[1], after[0], after[1]]):
-        edge[i, :count] = strip.astype(F32)
-
-    def part(e, places):
-        lhs = jnp.concatenate([
-            jnp.concatenate(
-                [edge[i, a * tall + b : a * tall + b + size].astype(BF) for i in places], 0
-            )
-            for a in range(3) for b in range(3)
-        ], 1)
-        rhs = jnp.concatenate([kernel[a, b, e] for a in range(3) for b in range(3)], 0)
-        found = jnp.dot(lhs, rhs, preferred_element_type=F32)
-        return [found[i * size : (i + 1) * size] for i in range(len(places))]
-
-    left0, fix0, right0 = part(0, [0, 1, 3])
-    left1, right1 = part(1, [1, 4])
-    left2, fix1, right2 = part(2, [2, 4, 5])
-    left, right = left0 + left1 + left2, right0 + right1 + right2
+    got = [g[...] for g in got]
+    if whole:
+        got = [jnp.where(top, *got), jnp.where(top, *got[::-1])]
+    before, after = arrived("col", got)
+    size = frames * tall
+    for i in range(RIM):
+        edge[i], edge[RIM + i] = before[i], own[i]
+        edge[2 * RIM + i], edge[3 * RIM + i] = own[RIM + i], after[i]
+    lhs = jnp.concatenate([
+        jnp.concatenate(
+            [edge[i + e, a * tall : a * tall + size] for i in (0, 1, 4, 5)], 0
+        )
+        for a in range(3) for e in range(3)
+    ], 1)
+    rhs = jnp.concatenate([
+        jnp.concatenate([kernel[a, b, e] for b in range(3)], 1) for a in range(3) for e in range(3)
+    ], 0)
+    found = jnp.dot(lhs, rhs, preferred_element_type=F32)
+    row = lax.broadcasted_iota(jnp.int32, (size, width), 0) % tall
+
+    def placed(i):
+        total = 0.0
+        for b in range(3):
+            value = found[i * size : (i + 1) * size, b * width : (b + 1) * width]
+            if whole:
+                shift = jnp.where(top, -RIM, tall // 2 - RIM) + b
+                value = pltpu.roll(value, jnp.where(shift > 0, size - shift, -shift), 0)
+                value = jnp.where((row + shift >= 0) & (row + shift < tall), value, 0.0)
+            elif b:
+                value = pltpu.roll(value, size - b, 0)
+            total = total + value
+        return total
+
+    left, begin, end, right = [placed(i) for i in range(4)]
 
     pitch = breadth + SLACK
-    for t in range(frames):
-        for r in range(rows):
-            at = (t * tall + r) * pitch
-            put(coarse, slice(at, at + breadth), inner[t, r])
-    put(coarse, pl.ds(0, size, stride=pitch), fix0, add=True)
-    put(coarse, pl.ds(breadth - 1, size, stride=pitch), fix1, add=True)
+    at = 0
+    for part in inner:
+        for t in range(part.shape[0]):
+            for r in range(rows):
+                put(coarse, slice(at + r * pitch, at + r * pitch + breadth), part[t, r])
+            at += tall * pitch
+    put(coarse, pl.ds(0, size, stride=pitch), begin)
+    put(coarse, pl.ds(breadth - 1, size, stride=pitch), end)
     put(coarse, pl.ds(breadth, size, stride=pitch), right)
-    begin = take(coarse, pl.ds(0, size, stride=pitch))
 
     def outside(row):
         return (top & (row == 0)) | (bottom & (row == rows - 1))
@@ -286,33 +313,54 @@
         [w_second, w_third], flops=COVER, name="kernels",
     )
     total = frames + EARLIER
-    rounds = len(swaps(lax.axis_size("row")))
+    row_places, col_places = lax.axis_size("row"), lax.axis_size("col")
+    rounds, cols = len(swaps(row_places)), len(swaps(col_places))
+    whole = row_places == 2 and cols == 2 and height == 2 * RIM
+    payload = [] if whole else [((total, RIM, breadth, width), BF)] * rounds
     field, *sends = call(
-        functools.partial(join_frames, pieces=pieces, rounds=rounds),
-        [((total, height, breadth, width), BF)] + [((total, RIM, breadth, width), BF)] * rounds,
+        functools.partial(join_frames, pieces=pieces),
+        [((total, height, breadth, width), BF)] + payload,
         [latent, ready, *got], flops=COVER, name="join_frames",
     )
-    rows_got = exchange(sends, "row")
+    rows_got = exchange([field] if whole else sends, "row")
     tall = height + 2 * RIM
-    cols = len(swaps(lax.axis_size("col")))
-    sends = call(
-        functools.partial(strips, rows=rounds), [((RIM, total * tall, width), BF)] * cols,
-        [field, *rows_got], [(blocked(total * tall * breadth, width), F32)], name="strips",
-    )
-    cols_got = exchange(sends, "col")
+    sides = [((RIM, total * tall, width), BF)] * (1 if whole else cols)
+    *sends, own = call(
+        functools.partial(strips, rows=rounds, whole=whole),
+        sides + [((2 * RIM, total * tall, width), BF)], [field, *rows_got],
+        [(blocked(total * tall * breadth, width), F32)], name="strips",
+    )
     early = total - 2
-    (inner,) = call(
-        functools.partial(first_inner, rows=rounds), [((early, tall - 2, breadth, mid), F32)],
-        [field, *rows_got, w_first], [((3, total, tall, breadth, width), BF)],
-        flops=2 * 27 * early * (tall - 2) * breadth * width * mid, name="first_inner",
-    )
+
+    def inner(begin, count, *after):
+        return call(
+            functools.partial(first_inner, rows=rounds, whole=whole, begin=begin),
+            [((count, tall - 2, breadth, mid), F32)], [field, *rows_got, w_first, *after],
+            [((3, count + 2, tall, breadth, width), BF)],
+            flops=2 * 27 * count * (tall - 2) * breadth * width * mid, name="first_inner",
+        )
+
+    if whole:
+        pairs = [
+            (core * col_places + i, core * col_places + j)
+            for core, pairing in enumerate(swaps(col_places)) for i, j in pairing
+        ]
+        came = lax.ppermute(sends[0], ("row", "col"), pairs)
+        cut = 5 * early // 8
+        inners = inner(0, cut)
+        cols_got = [came, *exchange([came], "row")]
+        inners += inner(cut, early - cut, came)
+    else:
+        cols_got = exchange(sends, "col")
+        inners = inner(0, early)
     later, corners = early - 2, tall - 3
     size = early * tall
     (out,) = call(
-        functools.partial(rest, cols=cols), [((frames, 2 * height, 2 * breadth, last), BF)],
-        [inner, *sends, *cols_got, w_first, summed, paired],
+        functools.partial(rest, cols=cols, parts=len(inners), whole=whole),
+        [((frames, 2 * height, 2 * breadth, last), BF)],
+        [*inners, own, *cols_got, w_first, summed, paired],
         [
-            ((6, total * tall + 8, width), F32),
+            ((4 * RIM, total * tall, width), BF),
             (blocked(size * (breadth + SLACK), mid), F32),
             ((2, early, tall - 2, breadth, mid), BF),
             ((2, size + 8, mid), F32),

time: 26.7 us -> 25.7 us (0.963)
  starting transfers between devices: 8.81 us -> 7.45 us
  Pallas kernels: 11.3 us -> 11.9 us
  waiting for transfers between devices: 2.78 us -> 2.46 us
    ppermute x3 -> x2, starting transfers between devices: 4.32 us -> 1.19 us  [exchange(): lax.ppermute(s, axis, pairs)]
    ppermute x0 -> x1, starting transfers between devices: none -> 1.77 us  [per_device(): came = lax.ppermute(sends[0], ('row', 'col'), pairs)]
    ppermute x3 -> x2, waiting for transfers between devices: 2.77 us -> 1.62 us  [exchange(): lax.ppermute(s, axis, pairs)]
    ppermute x0 -> x1, waiting for transfers between devices: none -> 0.84 us  [per_device(): came = lax.ppermute(sends[0], ('row', 'col'), pairs)]
    pallas_call x5 -> x6, Pallas kernels: 11.3 us -> 11.9 us  [call(): pl.pallas_call(body, out_shape=outs, in_specs=[spec] * len(args), out_spe...]
  transfers between devices with their start and end apart: 5 -> 5, of which waited for: 2 -> 2; matrix products, arithmetic and copies ran while one was open for 3% -> 3% of each run, Pallas kernels for 15% -> 16%
where the time goes in v5:
time: 25.7 us; the launch traced here: 25.4 us
  Pallas kernels  11.9 us (46%)
  starting transfers between devices  7.45 us (29%)
  local copies, waits for them, and re-layouts  3.53 us (14%)
  waiting for transfers between devices  2.46 us (10%)
    pallas_call x6, Pallas kernels, call(): pl.pallas_call(body, out_shape=outs, in_specs=[spec] * len(args), out_spe...  11.9 us
    ppermute x2, starting transfers between devices, per_device(): got.insert(0, lax.ppermute(latent[frames - take:], 'section', ring))  4.49 us
    unnamed x8, local copies, waits for them, and re-layouts  2.65 us
    ppermute x1, starting transfers between devices, per_device(): came = lax.ppermute(sends[0], ('row', 'col'), pairs)  1.77 us
    ppermute x2, waiting for transfers between devices, exchange(): lax.ppermute(s, axis, pairs)  1.62 us
    ppermute x2, starting transfers between devices, exchange(): lax.ppermute(s, axis, pairs)  1.19 us
    slice x1, local copies, waits for them, and re-layouts, per_device(): got.insert(0, lax.ppermute(latent[frames - take:], 'section', ring))  0.88 us
    ppermute x1, waiting for transfers between devices, per_device(): came = lax.ppermute(sends[0], ('row', 'col'), pairs)  0.84 us
  transfers between devices with their start and end apart: 5, of which 2 were waited for; matrix products, arithmetic and copies ran while one was open for 3% of the time, Pallas kernels for 16%

profile of v5, /device:TPU:0, one launch (start us, length us, event | category | flops | bytes accessed | tf_op | source)
XLA Modules:
  0.0 25.4 jit_solution(4409898210409822403)
XLA Ops:
  0.0 3.0 %collective-permute-start.1 = (bf16[4,4,16,256]{3,2,1,0:T(8,128)(2,1)}, bf16[4,4,16,256]{3,2,1,0:T(8,128)(2,1)S(1)}, u32[]{:S(2)}, u32[]{:S(2)}) collective-permute-start(bf16[4,4,16,256]{3,2,1,0:T(8,128)(2,1)} %refs_0_.1), channel_id=1, source_target_pairs={{0,8},{8,16},{16,24},{24,0},{1,9},{9,17},{17,25},{25,1},{2,10},{10... | collective-permute-start | bytes 393224 | tf_op jit(solution)/shard_map/ppermute | solution.py:307
  3.0 0.9 %slice.3 = bf16[2,4,16,256]{3,2,1,0:T(8,128)(2,1)S(1)} slice(bf16[4,4,16,256]{3,2,1,0:T(8,128)(2,1)} %refs_0_.1), slice={[2:4], [0:4], [0:16], [0:256]} | slice | bytes 131072 | tf_op jit(solution)/shard_map/slice | solution.py:307
  3.8 0.0 copy-start.1
  3.8 1.5 %collective-permute-start = (bf16[2,4,16,256]{3,2,1,0:T(8,128)(2,1)S(1)}, bf16[2,4,16,256]{3,2,1,0:T(8,128)(2,1)S(1)}, u32[]{:S(2)}, u32[]{:S(2)}) collective-permute-start(bf16[2,4,16,256]{3,2,1,0:T(8,128)(2,1)S(1)} %slice.3), channel_id=1, source_target_pairs={{0,16},{8,24},{16,0},{24,8},{1,17},{9,25},{17,1},{25,9},{2,18},{10... | collective-permute-start | bytes 196616 | tf_op jit(solution)/shard_map/ppermute | solution.py:307
  5.4 0.0 copy-start.2
  5.4 1.5 %copy-done.2 = bf16[3,3,3,256,128]{4,3,2,1,0:T(8,128)(2,1)S(1)} copy-done((bf16[3,3,3,256,128]{4,3,2,1,0:T(8,128)(2,1)S(1)}, bf16[3,3,3,256,128]{4,3,2,1,0:T(8,128)(2,1)}, u32[]{:S(2)}) %copy-start.2) | copy-done | bytes 1769496
  6.8 0.0 copy-start.3
  6.8 1.2 %copy-done.3 = bf16[3,3,3,128,128]{4,3,2,1,0:T(8,128)(2,1)S(1)} copy-done((bf16[3,3,3,128,128]{4,3,2,1,0:T(8,128)(2,1)S(1)}, bf16[3,3,3,128,128]{4,3,2,1,0:T(8,128)(2,1)}, u32[]{:S(2)}) %copy-start.3) | copy-done | bytes 884760
  8.0 1.0 %kernels.1 = (bf16[3,2,2,256,512]{4,3,2,1,0:T(8,128)(2,1)S(1)}, bf16[3,3,2,256,256]{4,3,2,1,0:T(8,128)(2,1)S(1)}, f32[8,128]{1,0:T(8,128)S(1)}) custom-call(bf16[3,3,3,256,128]{4,3,2,1,0:T(8,128)(2,1)S(1)} %copy-done.2, bf16[3,3,3,128,128]{4,3,2,1,0:T(8,128)(2,1)S(1)} %copy-done.3), custom_call_target="tpu_custom_call" | custom-call | flops 4000000000 | bytes 8163328 | tf_op jit(solution)/shard_map/kernels/pallas_call | solution.py:19
  9.1 0.0 collective-permute-done.refs_2_
  9.1 0.0 collective-permute-done.1.refs_3_
  9.1 0.0 copy-done.1
  9.1 0.0 copy-start
  9.2 0.1 collective-permute-start.2
  9.2 1.6 %collective-permute-done.2.refs_1_ = bf16[10,4,16,256]{3,2,1,0:T(8,128)(2,1)S(1)} collective-permute-done((bf16[10,4,16,256]{3,2,1,0:T(8,128)(2,1)S(1)}, bf16[10,4,16,256]{3,2,1,0:T(8,128)(2,1)S(1)}, u32[]{:S(2)}, u32[]{:S(2)}) %collective-permute-start.2) | collective-permute-done | bytes 327712 | tf_op jit(solution)/shard_map/ppermute | solution.py:55
  10.8 0.2 strips.1
  11.1 1.8 %collective-permute-start.3 = (bf16[2,80,256]{2,1,0:T(8,128)(2,1)S(1)}, bf16[2,80,256]{2,1,0:T(8,128)(2,1)S(1)}, u32[]{:S(2)}, u32[]{:S(2)}) collective-permute-start(bf16[2,80,256]{2,1,0:T(8,128)(2,1)S(1)} %get-tuple-element.11), channel_id=1, source_target_pairs={{0,1},{2,3},{1,0},{3,2},{5,6},{7,4},{6,5},{4,7},{8,9},{10,11},{9,8... | collective-permute-start | bytes 245768 | tf_op jit(solution)/shard_map/ppermute | solution.py:348
  12.9 0.0 copy-done
  12.9 1.9 %first_inner.2.refs_0_ = f32[5,6,16,256]{3,2,1,0:T(8,128)S(1)} custom-call(bf16[10,4,16,256]{3,2,1,0:T(8,128)(2,1)S(1)} %join_frames.1.refs_0_, bf16[10,4,16,256]{3,2,1,0:T(8,128)(2,1)S(1)} %collective-permute-done.2.refs_1_, bf16[3,3,3,256,256]{4,3,2,1,0:T(8,128)(2,1)S(1)} %copy-done), custom_call_target="tpu_custom_call" | custom-call | flops 1698693120 | bytes 4685824 | tf_op jit(solution)/shard_map/first_inner/pallas_call | solution.py:19
  14.8 0.8 %collective-permute-done.3.refs_3_ = bf16[2,80,256]{2,1,0:T(8,128)(2,1)S(1)} collective-permute-done((bf16[2,80,256]{2,1,0:T(8,128)(2,1)S(1)}, bf16[2,80,256]{2,1,0:T(8,128)(2,1)S(1)}, u32[]{:S(2)}, u32[]{:S(2)}) %collective-permute-start.3) | collective-permute-done | bytes 81952 | tf_op jit(solution)/shard_map/ppermute | solution.py:348
  15.6 1.1 %collective-permute-start.4 = (bf16[2,80,256]{2,1,0:T(8,128)(2,1)S(1)}, bf16[2,80,256]{2,1,0:T(8,128)(2,1)S(1)}, u32[]{:S(2)}, u32[]{:S(2)}) collective-permute-start(bf16[2,80,256]{2,1,0:T(8,128)(2,1)S(1)} %collective-permute-done.3.refs_3_), channel_id=1, source_target_pairs={{0,4},{4,0},{1,5},{5,1},{2,6},{6,2},{3,7},{7,3},{8,12},{12,8},{9,1... | collective-permute-start | bytes 245768 | tf_op jit(solution)/shard_map/ppermute | solution.py:55
  16.7 1.2 %first_inner.3.refs_1_ = f32[3,6,16,256]{3,2,1,0:T(8,128)S(1)} custom-call(bf16[10,4,16,256]{3,2,1,0:T(8,128)(2,1)S(1)} %join_frames.1.refs_0_, bf16[10,4,16,256]{3,2,1,0:T(8,128)(2,1)S(1)} %collective-permute-done.2.refs_1_, bf16[3,3,3,256,256]{4,3,2,1,0:T(8,128)(2,1)S(1)} %copy-done, bf16[2,80,256]{2,1,0:T(8,128)(2,1)S(1)} %collective-permute-done.3.refs_3_), custom_call_target="tpu_custom_call" | custom-call | flops 1019215872 | bytes 4571136 | tf_op jit(solution)/shard_map/first_inner/pallas_call | solution.py:19
  17.9 0.0 collective-permute-done.4.refs_4_
  17.9 7.5 %rest.1 = bf16[4,8,32,128]{3,2,1,0:T(8,128)(2,1)} custom-call(f32[5,6,16,256]{3,2,1,0:T(8,128)S(1)} %first_inner.2.refs_0_, f32[3,6,16,256]{3,2,1,0:T(8,128)S(1)} %first_inner.3.refs_1_, bf16[4,80,256]{2,1,0:T(8,128)(2,1)S(1)} %get-tuple-element.12.refs_2_, bf16[2,80,256]{2,1,0:T(8,128)(2,1)S(1)} %collective-permute-done.3.refs_3_, ...), custom_call_target="tpu_custom_call" | custom-call | flops 4000000000 | bytes 10420224 | tf_op jit(solution)/shard_map/rest/pallas_call | solution.py:19
  (1 shorter events, 0.0 us)
Async XLA Ops:
  0.0 9.1 %collective-permute-start.1 = (bf16[4,4,16,256]{3,2,1,0:T(8,128)(2,1)}, bf16[4,4,16,256]{3,2,1,0:T(8,128)(2,1)S(1)}, u32[]{:S(2)}, u32[]{:S(2)}) collective-permute-start(bf16[4,4,16,256]{3,2,1,0:T(8,128)(2,1)} %refs_0_.1), channel_id=1, source_target_pairs={{0,8},{8,16},{16,24},{24,0},{1,9},{9,17},{17,25},{25,1},{2,10},{10... | collective-permute-start | bytes 393224 | tf_op jit(solution)/shard_map/ppermute | solution.py:307
  3.8 5.2 %copy-start.1 = (bf16[4,4,16,256]{3,2,1,0:T(8,128)(2,1)S(1)}, bf16[4,4,16,256]{3,2,1,0:T(8,128)(2,1)}, u32[]{:S(2)}) copy-start(bf16[4,4,16,256]{3,2,1,0:T(8,128)(2,1)} %refs_0_.1) | copy-start | bytes 393220
  3.8 5.2 %collective-permute-start = (bf16[2,4,16,256]{3,2,1,0:T(8,128)(2,1)S(1)}, bf16[2,4,16,256]{3,2,1,0:T(8,128)(2,1)S(1)}, u32[]{:S(2)}, u32[]{:S(2)}) collective-permute-start(bf16[2,4,16,256]{3,2,1,0:T(8,128)(2,1)S(1)} %slice.3), channel_id=1, source_target_pairs={{0,16},{8,24},{16,0},{24,8},{1,17},{9,25},{17,1},{25,9},{2,18},{10... | collective-permute-start | bytes 196616 | tf_op jit(solution)/shard_map/ppermute | solution.py:307
  5.4 1.5 %copy-start.2 = (bf16[3,3,3,256,128]{4,3,2,1,0:T(8,128)(2,1)S(1)}, bf16[3,3,3,256,128]{4,3,2,1,0:T(8,128)(2,1)}, u32[]{:S(2)}) copy-start(bf16[3,3,3,256,128]{4,3,2,1,0:T(8,128)(2,1)} %second.1) | copy-start | bytes 5308420
  6.8 1.2 %copy-start.3 = (bf16[3,3,3,128,128]{4,3,2,1,0:T(8,128)(2,1)S(1)}, bf16[3,3,3,128,128]{4,3,2,1,0:T(8,128)(2,1)}, u32[]{:S(2)}) copy-start(bf16[3,3,3,128,128]{4,3,2,1,0:T(8,128)(2,1)} %third.1) | copy-start | bytes 2654212
  9.1 3.8 %copy-start = (bf16[3,3,3,256,256]{4,3,2,1,0:T(8,128)(2,1)S(1)}, bf16[3,3,3,256,256]{4,3,2,1,0:T(8,128)(2,1)}, u32[]{:S(2)}) copy-start(bf16[3,3,3,256,256]{4,3,2,1,0:T(8,128)(2,1)} %refs_5_.1) | copy-start | bytes 10616836
  9.2 1.7 %collective-permute-start.2 = (bf16[10,4,16,256]{3,2,1,0:T(8,128)(2,1)S(1)}, bf16[10,4,16,256]{3,2,1,0:T(8,128)(2,1)S(1)}, u32[]{:S(2)}, u32[]{:S(2)}) collective-permute-start(bf16[10,4,16,256]{3,2,1,0:T(8,128)(2,1)S(1)} %join_frames.1.refs_0_), channel_id=1, source_target_pairs={{0,4},{4,0},{1,5},{5,1},{2,6},{6,2},{3,7},{7,3},{8,12},{12,8},{9,1... | collective-permute-start | bytes 983048 | tf_op jit(solution)/shard_map/ppermute | solution.py:55
  11.1 4.5 %collective-permute-start.3 = (bf16[2,80,256]{2,1,0:T(8,128)(2,1)S(1)}, bf16[2,80,256]{2,1,0:T(8,128)(2,1)S(1)}, u32[]{:S(2)}, u32[]{:S(2)}) collective-permute-start(bf16[2,80,256]{2,1,0:T(8,128)(2,1)S(1)} %get-tuple-element.11), channel_id=1, source_target_pairs={{0,1},{2,3},{1,0},{3,2},{5,6},{7,4},{6,5},{4,7},{8,9},{10,11},{9,8... | collective-permute-start | bytes 245768 | tf_op jit(solution)/shard_map/ppermute | solution.py:348
  15.6 2.3 %collective-permute-start.4 = (bf16[2,80,256]{2,1,0:T(8,128)(2,1)S(1)}, bf16[2,80,256]{2,1,0:T(8,128)(2,1)S(1)}, u32[]{:S(2)}, u32[]{:S(2)}) collective-permute-start(bf16[2,80,256]{2,1,0:T(8,128)(2,1)S(1)} %collective-permute-done.3.refs_3_), channel_id=1, source_target_pairs={{0,4},{4,0},{1,5},{5,1},{2,6},{6,2},{3,7},{7,3},{8,12},{12,8},{9,1... | collective-permute-start | bytes 245768 | tf_op jit(solution)/shard_map/ppermute | solution.py:55

commit v6 on v5

--- a/solution.py
+++ b/solution.py
@@ -167,15 +167,17 @@
                         paired[a, b, dj, px * width : (px + 1) * width, q * out : (q + 1) * out] = block
 
 
-def rest(*refs, cols, parts, whole):
+def limits(axis):
+    return lax.axis_index(axis) == 0, lax.axis_index(axis) == lax.axis_size(axis) - 1
+
+
+def first_outer(*refs, cols, parts, whole):
     inner, own, got = refs[:parts], refs[parts], refs[parts + 1 : parts + 1 + cols]
-    kernel, summed, paired, out = refs[parts + 1 + cols : parts + 5 + cols]
-    edge, coarse, near, far, grown, fine, spread = refs[parts + 5 + cols :]
+    kernel, near, far, edge, coarse = refs[parts + 1 + cols :]
     rows, breadth, width = inner[0].shape[1:]
     frames = sum(part.shape[0] for part in inner)
     tall = rows + 2
-    top, bottom = lax.axis_index("row") == 0, lax.axis_index("row") == lax.axis_size("row") - 1
-    leftmost, rightmost = lax.axis_index("col") == 0, lax.axis_index("col") == lax.axis_size("col") - 1
+    (top, bottom), (leftmost, rightmost) = limits("row"), limits("col")
 
     got = [g[...] for g in got]
     if whole:
@@ -242,6 +244,11 @@
     far[0, :size] = jnp.where(outside(row) | leftmost, 0.0, jnp.maximum(left, 0.0))
     far[1, :size] = jnp.where(outside(row), 0.0, jnp.maximum(begin, 0.0))
 
+
+def second_conv(near, far, summed, fine, grown):
+    _, frames, rows, breadth, width = near.shape
+    tall, pitch = rows + 2, breadth + SLACK
+    (top, bottom), (leftmost, rightmost) = limits("row"), limits("col")
     corners, later = rows - 1, frames - 2
     short = later * tall
     taps = [
@@ -277,7 +284,10 @@
                     value = take(grown, slice(at, at + breadth), blocks)
                     fine[dj, 2 * i + py, t] = jnp.where(gone, 0.0, value).astype(BF)
 
-    high, kept, wide = 2 * corners - 2, later - 2, out.shape[-1]
+
+def third_conv(fine, paired, out, spread):
+    _, high, later, breadth, half = fine.shape
+    high, kept, wide = high - 2, later - 2, out.shape[-1]
     taps = [
         fine[dj, b : b + high, a : a + kept].reshape(-1, half)
         for a in range(3) for b in range(3) for dj in range(2)
@@ -355,20 +365,21 @@
         inners = inner(0, early)
     later, corners = early - 2, tall - 3
     size = early * tall
+    near, far = call(
+        functools.partial(first_outer, cols=cols, parts=len(inners), whole=whole),
+        [((2, early, tall - 2, breadth, mid), BF), ((2, size + 8, mid), F32)],
+        [*inners, own, *cols_got, w_first],
+        [((4 * RIM, total * tall, width), BF), (blocked(size * (breadth + SLACK), mid), F32)],
+        flops=10**9, name="first_outer",
+    )
+    (second,) = call(
+        second_conv, [((2, 2 * corners, later, breadth, 2 * fine), BF)], [near, far, summed],
+        [(blocked(later * tall * (breadth + SLACK), 4 * fine), F32)],
+        flops=2 * 10**9, name="second_conv",
+    )
     (out,) = call(
-        functools.partial(rest, cols=cols, parts=len(inners), whole=whole),
-        [((frames, 2 * height, 2 * breadth, last), BF)],
-        [*inners, own, *cols_got, w_first, summed, paired],
-        [
-            ((4 * RIM, total * tall, width), BF),
-            (blocked(size * (breadth + SLACK), mid), F32),
-            ((2, early, tall - 2, breadth, mid), BF),
-            ((2, size + 8, mid), F32),
-            (blocked(later * tall * (breadth + SLACK), 4 * fine), F32),
-            ((2, 2 * corners, later, breadth, 2 * fine), BF),
-            ((frames, 2 * height, 2 * breadth, last), F32),
-        ],
-        flops=4 * 10**9, name="rest",
+        third_conv, [((frames, 2 * height, 2 * breadth, last), BF)], [second, paired],
+        [((frames, 2 * height, 2 * breadth, last), F32)], flops=10**9, name="third_conv",
     )
     return out
 

time: 25.7 us -> 23.7 us (0.922)
  Pallas kernels: 11.9 us -> 9.92 us
    pallas_call x6 -> x8, Pallas kernels: 11.9 us -> 9.92 us  [call(): pl.pallas_call(body, out_shape=outs, in_specs=[spec] * len(args), out_spe...]
  transfers between devices with their start and end apart: 5 -> 5, of which waited for: 2 -> 2; matrix products, arithmetic and copies ran while one was open for 3% -> 4% of each run, Pallas kernels for 16% -> 18%
where the time goes in v6:
time: 23.7 us; the launch traced here: 23.5 us
  Pallas kernels  9.92 us (42%)
  starting transfers between devices  7.45 us (31%)
  local copies, waits for them, and re-layouts  3.53 us (15%)
  waiting for transfers between devices  2.46 us (10%)
    pallas_call x8, Pallas kernels, call(): pl.pallas_call(body, out_shape=outs, in_specs=[spec] * len(args), out_spe...  9.92 us
    ppermute x2, starting transfers between devices, per_device(): got.insert(0, lax.ppermute(latent[frames - take:], 'section', ring))  4.49 us
    unnamed x8, local copies, waits for them, and re-layouts  2.65 us
    ppermute x1, starting transfers between devices, per_device(): came = lax.ppermute(sends[0], ('row', 'col'), pairs)  1.78 us
    ppermute x2, waiting for transfers between devices, exchange(): lax.ppermute(s, axis, pairs)  1.62 us
    ppermute x2, starting transfers between devices, exchange(): lax.ppermute(s, axis, pairs)  1.19 us
    slice x1, local copies, waits for them, and re-layouts, per_device(): got.insert(0, lax.ppermute(latent[frames - take:], 'section', ring))  0.88 us
    ppermute x1, waiting for transfers between devices, per_device(): came = lax.ppermute(sends[0], ('row', 'col'), pairs)  0.84 us
  transfers between devices with their start and end apart: 5, of which 2 were waited for; matrix products, arithmetic and copies ran while one was open for 4% of the time, Pallas kernels for 18%

profile of v6, /device:TPU:0, one launch (start us, length us, event | category | flops | bytes accessed | tf_op | source)
XLA Modules:
  0.0 23.5 jit_solution(1472965274191217615)
XLA Ops:
  0.0 3.0 %collective-permute-start.1 = (bf16[4,4,16,256]{3,2,1,0:T(8,128)(2,1)}, bf16[4,4,16,256]{3,2,1,0:T(8,128)(2,1)S(1)}, u32[]{:S(2)}, u32[]{:S(2)}) collective-permute-start(bf16[4,4,16,256]{3,2,1,0:T(8,128)(2,1)} %refs_0_.1), channel_id=1, source_target_pairs={{0,8},{8,16},{16,24},{24,0},{1,9},{9,17},{17,25},{25,1},{2,10},{10... | collective-permute-start | bytes 393224 | tf_op jit(solution)/shard_map/ppermute | solution.py:317
  3.0 0.9 %slice.3 = bf16[2,4,16,256]{3,2,1,0:T(8,128)(2,1)S(1)} slice(bf16[4,4,16,256]{3,2,1,0:T(8,128)(2,1)} %refs_0_.1), slice={[2:4], [0:4], [0:16], [0:256]} | slice | bytes 131072 | tf_op jit(solution)/shard_map/slice | solution.py:317
  3.8 0.0 copy-start.1
  3.8 1.5 %collective-permute-start = (bf16[2,4,16,256]{3,2,1,0:T(8,128)(2,1)S(1)}, bf16[2,4,16,256]{3,2,1,0:T(8,128)(2,1)S(1)}, u32[]{:S(2)}, u32[]{:S(2)}) collective-permute-start(bf16[2,4,16,256]{3,2,1,0:T(8,128)(2,1)S(1)} %slice.3), channel_id=1, source_target_pairs={{0,16},{8,24},{16,0},{24,8},{1,17},{9,25},{17,1},{25,9},{2,18},{10... | collective-permute-start | bytes 196616 | tf_op jit(solution)/shard_map/ppermute | solution.py:317
  5.4 0.0 copy-start.2
  5.4 1.5 %copy-done.2 = bf16[3,3,3,256,128]{4,3,2,1,0:T(8,128)(2,1)S(1)} copy-done((bf16[3,3,3,256,128]{4,3,2,1,0:T(8,128)(2,1)S(1)}, bf16[3,3,3,256,128]{4,3,2,1,0:T(8,128)(2,1)}, u32[]{:S(2)}) %copy-start.2) | copy-done | bytes 1769496
  6.8 0.0 copy-start.3
  6.8 1.2 %copy-done.3 = bf16[3,3,3,128,128]{4,3,2,1,0:T(8,128)(2,1)S(1)} copy-done((bf16[3,3,3,128,128]{4,3,2,1,0:T(8,128)(2,1)S(1)}, bf16[3,3,3,128,128]{4,3,2,1,0:T(8,128)(2,1)}, u32[]{:S(2)}) %copy-start.3) | copy-done | bytes 884760
  8.0 1.0 %kernels.1 = (bf16[3,2,2,256,512]{4,3,2,1,0:T(8,128)(2,1)S(1)}, bf16[3,3,2,256,256]{4,3,2,1,0:T(8,128)(2,1)S(1)}, f32[8,128]{1,0:T(8,128)S(1)}) custom-call(bf16[3,3,3,256,128]{4,3,2,1,0:T(8,128)(2,1)S(1)} %copy-done.2, bf16[3,3,3,128,128]{4,3,2,1,0:T(8,128)(2,1)S(1)} %copy-done.3), custom_call_target="tpu_custom_call" | custom-call | flops 4000000000 | bytes 8163328 | tf_op jit(solution)/shard_map/kernels/pallas_call | solution.py:19
  9.1 0.0 collective-permute-done.refs_2_
  9.1 0.0 collective-permute-done.1.refs_3_
  9.1 0.0 copy-done.1
  9.1 0.0 copy-start
  9.2 0.1 collective-permute-start.2
  9.2 1.6 %collective-permute-done.2.refs_1_ = bf16[10,4,16,256]{3,2,1,0:T(8,128)(2,1)S(1)} collective-permute-done((bf16[10,4,16,256]{3,2,1,0:T(8,128)(2,1)S(1)}, bf16[10,4,16,256]{3,2,1,0:T(8,128)(2,1)S(1)}, u32[]{:S(2)}, u32[]{:S(2)}) %collective-permute-start.2) | collective-permute-done | bytes 327712 | tf_op jit(solution)/shard_map/ppermute | solution.py:55
  10.8 0.2 %strips.1 = (bf16[2,80,256]{2,1,0:T(8,128)(2,1)S(1)}, bf16[4,80,256]{2,1,0:T(8,128)(2,1)S(1)}) custom-call(bf16[10,4,16,256]{3,2,1,0:T(8,128)(2,1)S(1)} %join_frames.1.refs_0_, bf16[10,4,16,256]{3,2,1,0:T(8,128)(2,1)S(1)} %collective-permute-done.2.refs_1_), custom_call_target="tpu_custom_call" | custom-call | bytes 901120 | tf_op jit(solution)/shard_map/strips/pallas_call | solution.py:19
  11.1 1.8 %collective-permute-start.3 = (bf16[2,80,256]{2,1,0:T(8,128)(2,1)S(1)}, bf16[2,80,256]{2,1,0:T(8,128)(2,1)S(1)}, u32[]{:S(2)}, u32[]{:S(2)}) collective-permute-start(bf16[2,80,256]{2,1,0:T(8,128)(2,1)S(1)} %get-tuple-element.13), channel_id=1, source_target_pairs={{0,1},{2,3},{1,0},{3,2},{5,6},{7,4},{6,5},{4,7},{8,9},{10,11},{9,8... | collective-permute-start | bytes 245768 | tf_op jit(solution)/shard_map/ppermute | solution.py:358
  12.9 0.0 copy-done
  12.9 1.9 %first_inner.2.refs_0_ = f32[5,6,16,256]{3,2,1,0:T(8,128)S(1)} custom-call(bf16[10,4,16,256]{3,2,1,0:T(8,128)(2,1)S(1)} %join_frames.1.refs_0_, bf16[10,4,16,256]{3,2,1,0:T(8,128)(2,1)S(1)} %collective-permute-done.2.refs_1_, bf16[3,3,3,256,256]{4,3,2,1,0:T(8,128)(2,1)S(1)} %copy-done), custom_call_target="tpu_custom_call" | custom-call | flops 1698693120 | bytes 4685824 | tf_op jit(solution)/shard_map/first_inner/pallas_call | solution.py:19
  14.8 0.8 %collective-permute-done.3.refs_3_ = bf16[2,80,256]{2,1,0:T(8,128)(2,1)S(1)} collective-permute-done((bf16[2,80,256]{2,1,0:T(8,128)(2,1)S(1)}, bf16[2,80,256]{2,1,0:T(8,128)(2,1)S(1)}, u32[]{:S(2)}, u32[]{:S(2)}) %collective-permute-start.3) | collective-permute-done | bytes 81952 | tf_op jit(solution)/shard_map/ppermute | solution.py:358
  15.6 1.1 %collective-permute-start.4 = (bf16[2,80,256]{2,1,0:T(8,128)(2,1)S(1)}, bf16[2,80,256]{2,1,0:T(8,128)(2,1)S(1)}, u32[]{:S(2)}, u32[]{:S(2)}) collective-permute-start(bf16[2,80,256]{2,1,0:T(8,128)(2,1)S(1)} %collective-permute-done.3.refs_3_), channel_id=1, source_target_pairs={{0,4},{4,0},{1,5},{5,1},{2,6},{6,2},{3,7},{7,3},{8,12},{12,8},{9,1... | collective-permute-start | bytes 245768 | tf_op jit(solution)/shard_map/ppermute | solution.py:55
  16.7 1.2 %first_inner.3.refs_1_ = f32[3,6,16,256]{3,2,1,0:T(8,128)S(1)} custom-call(bf16[10,4,16,256]{3,2,1,0:T(8,128)(2,1)S(1)} %join_frames.1.refs_0_, bf16[10,4,16,256]{3,2,1,0:T(8,128)(2,1)S(1)} %collective-permute-done.2.refs_1_, bf16[3,3,3,256,256]{4,3,2,1,0:T(8,128)(2,1)S(1)} %copy-done, bf16[2,80,256]{2,1,0:T(8,128)(2,1)S(1)} %collective-permute-done.3.refs_3_), custom_call_target="tpu_custom_call" | custom-call | flops 1019215872 | bytes 4571136 | tf_op jit(solution)/shard_map/first_inner/pallas_call | solution.py:19
  17.9 0.0 collective-permute-done.4.refs_4_
  17.9 1.4 %first_outer.1 = (bf16[2,8,6,16,256]{4,3,2,1,0:T(8,128)(2,1)S(1)}, f32[2,72,256]{2,1,0:T(8,128)S(1)}) custom-call(f32[5,6,16,256]{3,2,1,0:T(8,128)S(1)} %first_inner.2.refs_0_, f32[3,6,16,256]{3,2,1,0:T(8,128)S(1)} %first_inner.3.refs_1_, bf16[4,80,256]{2,1,0:T(8,128)(2,1)S(1)} %get-tuple-element.14.refs_2_, ...), custom_call_target="tpu_custom_call" | custom-call | flops 1000000000 | bytes 5586944 | tf_op jit(solution)/shard_map/first_outer/pallas_call | solution.py:19
  19.4 1.9 %second_conv.1.fine = bf16[2,10,6,16,256]{4,3,2,1,0:T(8,128)(2,1)S(1)} custom-call(bf16[2,8,6,16,256]{4,3,2,1,0:T(8,128)(2,1)S(1)} %get-tuple-element.15.near, f32[2,72,256]{2,1,0:T(8,128)S(1)} %get-tuple-element.16.far, bf16[3,2,2,256,512]{4,3,2,1,0:T(8,128)(2,1)S(1)} %get-tuple-element.17.summed), custom_call_target="tpu_custom_call" | custom-call | flops 2000000000 | bytes 5062656 | tf_op jit(solution)/shard_map/second_conv/pallas_call | solution.py:19
  21.3 2.1 %third_conv.1 = bf16[4,8,32,128]{3,2,1,0:T(8,128)(2,1)} custom-call(bf16[2,10,6,16,256]{4,3,2,1,0:T(8,128)(2,1)S(1)} %second_conv.1.fine, bf16[3,3,2,256,256]{4,3,2,1,0:T(8,128)(2,1)S(1)} %get-tuple-element.18.paired), custom_call_target="tpu_custom_call" | custom-call | flops 1000000000 | bytes 3604480 | tf_op jit(solution)/shard_map/third_conv/pallas_call | solution.py:19
  (1 shorter events, 0.0 us)
Async XLA Ops:
  0.0 9.1 %collective-permute-start.1 = (bf16[4,4,16,256]{3,2,1,0:T(8,128)(2,1)}, bf16[4,4,16,256]{3,2,1,0:T(8,128)(2,1)S(1)}, u32[]{:S(2)}, u32[]{:S(2)}) collective-permute-start(bf16[4,4,16,256]{3,2,1,0:T(8,128)(2,1)} %refs_0_.1), channel_id=1, source_target_pairs={{0,8},{8,16},{16,24},{24,0},{1,9},{9,17},{17,25},{25,1},{2,10},{10... | collective-permute-start | bytes 393224 | tf_op jit(solution)/shard_map/ppermute | solution.py:317
  3.8 5.2 %copy-start.1 = (bf16[4,4,16,256]{3,2,1,0:T(8,128)(2,1)S(1)}, bf16[4,4,16,256]{3,2,1,0:T(8,128)(2,1)}, u32[]{:S(2)}) copy-start(bf16[4,4,16,256]{3,2,1,0:T(8,128)(2,1)} %refs_0_.1) | copy-start | bytes 393220
  3.8 5.2 %collective-permute-start = (bf16[2,4,16,256]{3,2,1,0:T(8,128)(2,1)S(1)}, bf16[2,4,16,256]{3,2,1,0:T(8,128)(2,1)S(1)}, u32[]{:S(2)}, u32[]{:S(2)}) collective-permute-start(bf16[2,4,16,256]{3,2,1,0:T(8,128)(2,1)S(1)} %slice.3), channel_id=1, source_target_pairs={{0,16},{8,24},{16,0},{24,8},{1,17},{9,25},{17,1},{25,9},{2,18},{10... | collective-permute-start | bytes 196616 | tf_op jit(solution)/shard_map/ppermute | solution.py:317
  5.4 1.5 %copy-start.2 = (bf16[3,3,3,256,128]{4,3,2,1,0:T(8,128)(2,1)S(1)}, bf16[3,3,3,256,128]{4,3,2,1,0:T(8,128)(2,1)}, u32[]{:S(2)}) copy-start(bf16[3,3,3,256,128]{4,3,2,1,0:T(8,128)(2,1)} %second.1) | copy-start | bytes 5308420
  6.8 1.2 %copy-start.3 = (bf16[3,3,3,128,128]{4,3,2,1,0:T(8,128)(2,1)S(1)}, bf16[3,3,3,128,128]{4,3,2,1,0:T(8,128)(2,1)}, u32[]{:S(2)}) copy-start(bf16[3,3,3,128,128]{4,3,2,1,0:T(8,128)(2,1)} %third.1) | copy-start | bytes 2654212
  9.1 3.8 %copy-start = (bf16[3,3,3,256,256]{4,3,2,1,0:T(8,128)(2,1)S(1)}, bf16[3,3,3,256,256]{4,3,2,1,0:T(8,128)(2,1)}, u32[]{:S(2)}) copy-start(bf16[3,3,3,256,256]{4,3,2,1,0:T(8,128)(2,1)} %refs_5_.1) | copy-start | bytes 10616836
  9.2 1.7 %collective-permute-start.2 = (bf16[10,4,16,256]{3,2,1,0:T(8,128)(2,1)S(1)}, bf16[10,4,16,256]{3,2,1,0:T(8,128)(2,1)S(1)}, u32[]{:S(2)}, u32[]{:S(2)}) collective-permute-start(bf16[10,4,16,256]{3,2,1,0:T(8,128)(2,1)S(1)} %join_frames.1.refs_0_), channel_id=1, source_target_pairs={{0,4},{4,0},{1,5},{5,1},{2,6},{6,2},{3,7},{7,3},{8,12},{12,8},{9,1... | collective-permute-start | bytes 983048 | tf_op jit(solution)/shard_map/ppermute | solution.py:55
  11.1 4.5 %collective-permute-start.3 = (bf16[2,80,256]{2,1,0:T(8,128)(2,1)S(1)}, bf16[2,80,256]{2,1,0:T(8,128)(2,1)S(1)}, u32[]{:S(2)}, u32[]{:S(2)}) collective-permute-start(bf16[2,80,256]{2,1,0:T(8,128)(2,1)S(1)} %get-tuple-element.13), channel_id=1, source_target_pairs={{0,1},{2,3},{1,0},{3,2},{5,6},{7,4},{6,5},{4,7},{8,9},{10,11},{9,8... | collective-permute-start | bytes 245768 | tf_op jit(solution)/shard_map/ppermute | solution.py:358
  15.6 2.3 %collective-permute-start.4 = (bf16[2,80,256]{2,1,0:T(8,128)(2,1)S(1)}, bf16[2,80,256]{2,1,0:T(8,128)(2,1)S(1)}, u32[]{:S(2)}, u32[]{:S(2)}) collective-permute-start(bf16[2,80,256]{2,1,0:T(8,128)(2,1)S(1)} %collective-permute-done.3.refs_3_), channel_id=1, source_target_pairs={{0,4},{4,0},{1,5},{5,1},{2,6},{6,2},{3,7},{7,3},{8,12},{12,8},{9,1... | collective-permute-start | bytes 245768 | tf_op jit(solution)/shard_map/ppermute | solution.py:55

commit v7 on v6

--- a/solution.py
+++ b/solution.py
@@ -12,13 +12,14 @@
 RIM = 2
 
 
-def call(body, outs, args, scratch=(), flops=0, name=None):
+def call(body, outs, args, scratch=(), flops=0, name=None, to=pltpu.VMEM):
     spec = pl.BlockSpec(memory_space=pltpu.VMEM)
     outs = [jax.ShapeDtypeStruct(shape, kind) for shape, kind in outs]
     size = sum(a.size * a.dtype.itemsize for a in [*args, *outs])
     return pl.pallas_call(
-        body, out_shape=outs, in_specs=[spec] * len(args), out_specs=[spec] * len(outs),
-        scratch_shapes=[pltpu.VMEM(*s) for s in scratch], name=name,
+        body, out_shape=outs, in_specs=[spec] * len(args),
+        out_specs=[pl.BlockSpec(memory_space=to)] * len(outs), name=name,
+        scratch_shapes=[pltpu.VMEM(*s) if isinstance(s, tuple) else s for s in scratch],
         cost_estimate=pl.CostEstimate(flops=flops, bytes_accessed=size, transcendentals=0),
         compiler_params=pltpu.CompilerParams(vmem_limit_bytes=32 << 20),
     )(*args)
@@ -285,24 +286,37 @@
                     fine[dj, 2 * i + py, t] = jnp.where(gone, 0.0, value).astype(BF)
 
 
-def third_conv(fine, paired, out, spread):
+def third_conv(fine, paired, out, spread, ready, sems):
     _, high, later, breadth, half = fine.shape
     high, kept, wide = high - 2, later - 2, out.shape[-1]
-    taps = [
-        fine[dj, b : b + high, a : a + kept].reshape(-1, half)
-        for a in range(3) for b in range(3) for dj in range(2)
-    ]
-    found = jnp.dot(
-        jnp.concatenate(taps, 1), paired[...].reshape(-1, paired.shape[-1]), preferred_element_type=F32
-    )
-    for y in range(high):
-        for t in range(kept):
-            at = (y * kept + t) * breadth
-            for q in range(2):
-                spread[t, y, pl.ds(q, breadth, stride=2), :] = found[
-                    at : at + breadth, q * wide : (q + 1) * wide
-                ]
-    out[...] = spread[...].astype(BF)
+    steps = sems.shape[0]
+    count = kept // steps
+    kernel = paired[...].reshape(-1, paired.shape[-1])
+
+    def leave(step):
+        mine = pl.ds(step * count, count)
+        return pltpu.make_async_copy(ready.at[mine], out.at[mine], sems.at[step])
+
+    @pl.loop(0, steps)
+    def _(step):
+        begin = step * count
+        taps = [
+            fine[dj, b : b + high, pl.ds(begin + a, count)].reshape(-1, half)
+            for a in range(3) for b in range(3) for dj in range(2)
+        ]
+        found = jnp.dot(jnp.concatenate(taps, 1), kernel, preferred_element_type=F32)
+        for y in range(high):
+            for t in range(count):
+                at = (y * count + t) * breadth
+                for q in range(2):
+                    spread[t, y, pl.ds(q, breadth, stride=2), :] = found[
+                        at : at + breadth, q * wide : (q + 1) * wide
+                    ]
+        ready[pl.ds(begin, count)] = spread[...].astype(BF)
+        leave(step).start()
+
+    for step in range(steps):
+        leave(step).wait()
 
 
 def per_device(latent, w_first, w_second, w_third):
@@ -351,11 +365,17 @@
         )
 
     if whole:
-        pairs = [
-            (core * col_places + i, core * col_places + j)
-            for core, pairing in enumerate(swaps(col_places)) for i, j in pairing
-        ]
-        came = lax.ppermute(sends[0], ("row", "col"), pairs)
+        pairs = []
+        for section in range(sections):
+            for core, pairing in enumerate(swaps(col_places)):
+                at = (section * row_places + core) * col_places
+                for i, j in pairing:
+                    if abs(i - j) > 1 and sections % 2 == 0:
+                        to = ((section ^ 1) * row_places + core) * col_places
+                        pairs.append((at + i, to + i))
+                    else:
+                        pairs.append((at + i, at + j))
+        came = lax.ppermute(sends[0], ("section", "row", "col"), pairs)
         cut = 5 * early // 8
         inners = inner(0, cut)
         cols_got = [came, *exchange([came], "row")]
@@ -377,9 +397,14 @@
         [(blocked(later * tall * (breadth + SLACK), 4 * fine), F32)],
         flops=2 * 10**9, name="second_conv",
     )
+    steps = 2 if frames % 2 == 0 else 1
     (out,) = call(
         third_conv, [((frames, 2 * height, 2 * breadth, last), BF)], [second, paired],
-        [((frames, 2 * height, 2 * breadth, last), F32)], flops=10**9, name="third_conv",
+        [
+            ((frames // steps, 2 * height, 2 * breadth, last), F32),
+            ((frames, 2 * height, 2 * breadth, last), BF), pltpu.SemaphoreType.DMA((steps,)),
+        ],
+        flops=10**9, name="third_conv", to=pl.ANY,
     )
     return out
 

time: 23.7 us -> 23 us (0.970)
  starting transfers between devices: 7.45 us -> 6.34 us
  Pallas kernels: 9.92 us -> 10.2 us
    ppermute x2, starting transfers between devices: 1.19 us -> 0.07 us  [exchange(): lax.ppermute(s, axis, pairs)]
    pallas_call x8, Pallas kernels: 9.92 us -> 10.2 us  [call(): pl.pallas_call(body, out_shape=outs, in_specs=[spec] * len(args), out_spe...]
  transfers between devices with their start and end apart: 5 -> 5, of which waited for: 2 -> 3; matrix products, arithmetic and copies ran while one was open for 4% -> 4% of each run, Pallas kernels for 18% -> 18%
where the time goes in v7:
time: 23 us; the launch traced here: 22.7 us
  Pallas kernels  10.2 us (44%)
  starting transfers between devices  6.34 us (28%)
  local copies, waits for them, and re-layouts  3.53 us (15%)
  waiting for transfers between devices  2.53 us (11%)
    pallas_call x8, Pallas kernels, call(): pl.pallas_call(body, out_shape=outs, in_specs=[spec] * len(args), out_spe...  10.2 us
    ppermute x2, starting transfers between devices, per_device(): got.insert(0, lax.ppermute(latent[frames - take:], 'section', ring))  4.49 us
    unnamed x8, local copies, waits for them, and re-layouts  2.65 us
    ppermute x1, starting transfers between devices, per_device(): came = lax.ppermute(sends[0], ('section', 'row', 'col'), pairs)  1.78 us
    ppermute x2, waiting for transfers between devices, exchange(): lax.ppermute(s, axis, pairs)  1.68 us
    slice x1, local copies, waits for them, and re-layouts, per_device(): got.insert(0, lax.ppermute(latent[frames - take:], 'section', ring))  0.88 us
    ppermute x1, waiting for transfers between devices, per_device(): came = lax.ppermute(sends[0], ('section', 'row', 'col'), pairs)  0.84 us
  transfers between devices with their start and end apart: 5, of which 3 were waited for; matrix products, arithmetic and copies ran while one was open for 4% of the time, Pallas kernels for 18%

profile of v7, /device:TPU:0, one launch (start us, length us, event | category | flops | bytes accessed | tf_op | source)
XLA Modules:
  0.0 22.7 jit_solution(4282924709267592073)
XLA Ops:
  0.0 3.0 %collective-permute-start.1 = (bf16[4,4,16,256]{3,2,1,0:T(8,128)(2,1)}, bf16[4,4,16,256]{3,2,1,0:T(8,128)(2,1)S(1)}, u32[]{:S(2)}, u32[]{:S(2)}) collective-permute-start(bf16[4,4,16,256]{3,2,1,0:T(8,128)(2,1)} %refs_0_.1), channel_id=1, source_target_pairs={{0,8},{8,16},{16,24},{24,0},{1,9},{9,17},{17,25},{25,1},{2,10},{10... | collective-permute-start | bytes 393224 | tf_op jit(solution)/shard_map/ppermute | solution.py:331
  3.0 0.9 %slice.3 = bf16[2,4,16,256]{3,2,1,0:T(8,128)(2,1)S(1)} slice(bf16[4,4,16,256]{3,2,1,0:T(8,128)(2,1)} %refs_0_.1), slice={[2:4], [0:4], [0:16], [0:256]} | slice | bytes 131072 | tf_op jit(solution)/shard_map/slice | solution.py:331
  3.8 0.0 copy-start.1
  3.8 1.5 %collective-permute-start = (bf16[2,4,16,256]{3,2,1,0:T(8,128)(2,1)S(1)}, bf16[2,4,16,256]{3,2,1,0:T(8,128)(2,1)S(1)}, u32[]{:S(2)}, u32[]{:S(2)}) collective-permute-start(bf16[2,4,16,256]{3,2,1,0:T(8,128)(2,1)S(1)} %slice.3), channel_id=1, source_target_pairs={{0,16},{8,24},{16,0},{24,8},{1,17},{9,25},{17,1},{25,9},{2,18},{10... | collective-permute-start | bytes 196616 | tf_op jit(solution)/shard_map/ppermute | solution.py:331
  5.4 0.0 copy-start.2
  5.4 1.5 %copy-done.2 = bf16[3,3,3,256,128]{4,3,2,1,0:T(8,128)(2,1)S(1)} copy-done((bf16[3,3,3,256,128]{4,3,2,1,0:T(8,128)(2,1)S(1)}, bf16[3,3,3,256,128]{4,3,2,1,0:T(8,128)(2,1)}, u32[]{:S(2)}) %copy-start.2) | copy-done | bytes 1769496
  6.8 0.0 copy-start.3
  6.8 1.2 %copy-done.3 = bf16[3,3,3,128,128]{4,3,2,1,0:T(8,128)(2,1)S(1)} copy-done((bf16[3,3,3,128,128]{4,3,2,1,0:T(8,128)(2,1)S(1)}, bf16[3,3,3,128,128]{4,3,2,1,0:T(8,128)(2,1)}, u32[]{:S(2)}) %copy-start.3) | copy-done | bytes 884760
  8.0 1.0 %kernels.1 = (bf16[3,2,2,256,512]{4,3,2,1,0:T(8,128)(2,1)S(1)}, bf16[3,3,2,256,256]{4,3,2,1,0:T(8,128)(2,1)S(1)}, f32[8,128]{1,0:T(8,128)S(1)}) custom-call(bf16[3,3,3,256,128]{4,3,2,1,0:T(8,128)(2,1)S(1)} %copy-done.2, bf16[3,3,3,128,128]{4,3,2,1,0:T(8,128)(2,1)S(1)} %copy-done.3), custom_call_target="tpu_custom_call" | custom-call | flops 4000000000 | bytes 8163328 | tf_op jit(solution)/shard_map/kernels/pallas_call | solution.py:19
  9.1 0.0 collective-permute-done.refs_2_
  9.1 0.0 collective-permute-done.1.refs_3_
  9.1 0.0 copy-done.1
  9.1 0.0 copy-start
  9.2 0.1 collective-permute-start.2
  9.2 1.6 %collective-permute-done.2.refs_1_ = bf16[10,4,16,256]{3,2,1,0:T(8,128)(2,1)S(1)} collective-permute-done((bf16[10,4,16,256]{3,2,1,0:T(8,128)(2,1)S(1)}, bf16[10,4,16,256]{3,2,1,0:T(8,128)(2,1)S(1)}, u32[]{:S(2)}, u32[]{:S(2)}) %collective-permute-start.2) | collective-permute-done | bytes 327712 | tf_op jit(solution)/shard_map/ppermute | solution.py:56
  10.8 0.2 %strips.1 = (bf16[2,80,256]{2,1,0:T(8,128)(2,1)S(1)}, bf16[4,80,256]{2,1,0:T(8,128)(2,1)S(1)}) custom-call(bf16[10,4,16,256]{3,2,1,0:T(8,128)(2,1)S(1)} %join_frames.1.refs_0_, bf16[10,4,16,256]{3,2,1,0:T(8,128)(2,1)S(1)} %collective-permute-done.2.refs_1_), custom_call_target="tpu_custom_call" | custom-call | bytes 901120 | tf_op jit(solution)/shard_map/strips/pallas_call | solution.py:19
  11.1 1.8 %collective-permute-start.3 = (bf16[2,80,256]{2,1,0:T(8,128)(2,1)S(1)}, bf16[2,80,256]{2,1,0:T(8,128)(2,1)S(1)}, u32[]{:S(2)}, u32[]{:S(2)}) collective-permute-start(bf16[2,80,256]{2,1,0:T(8,128)(2,1)S(1)} %get-tuple-element.13), channel_id=1, source_target_pairs={{0,1},{2,3},{1,0},{3,2},{5,6},{7,15},{6,5},{4,12},{8,9},{10,11},{9... | collective-permute-start | bytes 245768 | tf_op jit(solution)/shard_map/ppermute | solution.py:378
  12.9 0.0 copy-done
  12.9 1.9 %first_inner.2.refs_0_ = f32[5,6,16,256]{3,2,1,0:T(8,128)S(1)} custom-call(bf16[10,4,16,256]{3,2,1,0:T(8,128)(2,1)S(1)} %join_frames.1.refs_0_, bf16[10,4,16,256]{3,2,1,0:T(8,128)(2,1)S(1)} %collective-permute-done.2.refs_1_, bf16[3,3,3,256,256]{4,3,2,1,0:T(8,128)(2,1)S(1)} %copy-done), custom_call_target="tpu_custom_call" | custom-call | flops 1698693120 | bytes 4685824 | tf_op jit(solution)/shard_map/first_inner/pallas_call | solution.py:19
  14.8 0.8 %collective-permute-done.3.refs_3_ = bf16[2,80,256]{2,1,0:T(8,128)(2,1)S(1)} collective-permute-done((bf16[2,80,256]{2,1,0:T(8,128)(2,1)S(1)}, bf16[2,80,256]{2,1,0:T(8,128)(2,1)S(1)}, u32[]{:S(2)}, u32[]{:S(2)}) %collective-permute-start.3) | collective-permute-done | bytes 81952 | tf_op jit(solution)/shard_map/ppermute | solution.py:378
  15.6 0.0 collective-permute-start.4
  15.6 1.2 %first_inner.3.refs_1_ = f32[3,6,16,256]{3,2,1,0:T(8,128)S(1)} custom-call(bf16[10,4,16,256]{3,2,1,0:T(8,128)(2,1)S(1)} %join_frames.1.refs_0_, bf16[10,4,16,256]{3,2,1,0:T(8,128)(2,1)S(1)} %collective-permute-done.2.refs_1_, bf16[3,3,3,256,256]{4,3,2,1,0:T(8,128)(2,1)S(1)} %copy-done, bf16[2,80,256]{2,1,0:T(8,128)(2,1)S(1)} %collective-permute-done.3.refs_3_), custom_call_target="tpu_custom_call" | custom-call | flops 1019215872 | bytes 4571136 | tf_op jit(solution)/shard_map/first_inner/pallas_call | solution.py:19
  16.8 0.1 collective-permute-done.4.refs_4_
  16.9 1.4 %first_outer.1 = (bf16[2,8,6,16,256]{4,3,2,1,0:T(8,128)(2,1)S(1)}, f32[2,72,256]{2,1,0:T(8,128)S(1)}) custom-call(f32[5,6,16,256]{3,2,1,0:T(8,128)S(1)} %first_inner.2.refs_0_, f32[3,6,16,256]{3,2,1,0:T(8,128)S(1)} %first_inner.3.refs_1_, bf16[4,80,256]{2,1,0:T(8,128)(2,1)S(1)} %get-tuple-element.14.refs_2_, ...), custom_call_target="tpu_custom_call" | custom-call | flops 1000000000 | bytes 5586944 | tf_op jit(solution)/shard_map/first_outer/pallas_call | solution.py:19
  18.3 1.9 %second_conv.1.fine = bf16[2,10,6,16,256]{4,3,2,1,0:T(8,128)(2,1)S(1)} custom-call(bf16[2,8,6,16,256]{4,3,2,1,0:T(8,128)(2,1)S(1)} %get-tuple-element.15.near, f32[2,72,256]{2,1,0:T(8,128)S(1)} %get-tuple-element.16.far, bf16[3,2,2,256,512]{4,3,2,1,0:T(8,128)(2,1)S(1)} %get-tuple-element.17.summed), custom_call_target="tpu_custom_call" | custom-call | flops 2000000000 | bytes 5062656 | tf_op jit(solution)/shard_map/second_conv/pallas_call | solution.py:19
  20.3 2.5 %third_conv.1 = bf16[4,8,32,128]{3,2,1,0:T(8,128)(2,1)} custom-call(bf16[2,10,6,16,256]{4,3,2,1,0:T(8,128)(2,1)S(1)} %second_conv.1.fine, bf16[3,3,2,256,256]{4,3,2,1,0:T(8,128)(2,1)S(1)} %get-tuple-element.18.paired), custom_call_target="tpu_custom_call" | custom-call | flops 1000000000 | bytes 3604480 | tf_op jit(solution)/shard_map/third_conv/pallas_call | solution.py:19
  (1 shorter events, 0.0 us)
Async XLA Ops:
  0.0 9.1 %collective-permute-start.1 = (bf16[4,4,16,256]{3,2,1,0:T(8,128)(2,1)}, bf16[4,4,16,256]{3,2,1,0:T(8,128)(2,1)S(1)}, u32[]{:S(2)}, u32[]{:S(2)}) collective-permute-start(bf16[4,4,16,256]{3,2,1,0:T(8,128)(2,1)} %refs_0_.1), channel_id=1, source_target_pairs={{0,8},{8,16},{16,24},{24,0},{1,9},{9,17},{17,25},{25,1},{2,10},{10... | collective-permute-start | bytes 393224 | tf_op jit(solution)/shard_map/ppermute | solution.py:331
  3.8 5.2 %copy-start.1 = (bf16[4,4,16,256]{3,2,1,0:T(8,128)(2,1)S(1)}, bf16[4,4,16,256]{3,2,1,0:T(8,128)(2,1)}, u32[]{:S(2)}) copy-start(bf16[4,4,16,256]{3,2,1,0:T(8,128)(2,1)} %refs_0_.1) | copy-start | bytes 393220
  3.8 5.2 %collective-permute-start = (bf16[2,4,16,256]{3,2,1,0:T(8,128)(2,1)S(1)}, bf16[2,4,16,256]{3,2,1,0:T(8,128)(2,1)S(1)}, u32[]{:S(2)}, u32[]{:S(2)}) collective-permute-start(bf16[2,4,16,256]{3,2,1,0:T(8,128)(2,1)S(1)} %slice.3), channel_id=1, source_target_pairs={{0,16},{8,24},{16,0},{24,8},{1,17},{9,25},{17,1},{25,9},{2,18},{10... | collective-permute-start | bytes 196616 | tf_op jit(solution)/shard_map/ppermute | solution.py:331
  5.4 1.5 %copy-start.2 = (bf16[3,3,3,256,128]{4,3,2,1,0:T(8,128)(2,1)S(1)}, bf16[3,3,3,256,128]{4,3,2,1,0:T(8,128)(2,1)}, u32[]{:S(2)}) copy-start(bf16[3,3,3,256,128]{4,3,2,1,0:T(8,128)(2,1)} %second.1) | copy-start | bytes 5308420
  6.8 1.2 %copy-start.3 = (bf16[3,3,3,128,128]{4,3,2,1,0:T(8,128)(2,1)S(1)}, bf16[3,3,3,128,128]{4,3,2,1,0:T(8,128)(2,1)}, u32[]{:S(2)}) copy-start(bf16[3,3,3,128,128]{4,3,2,1,0:T(8,128)(2,1)} %third.1) | copy-start | bytes 2654212
  9.1 3.8 %copy-start = (bf16[3,3,3,256,256]{4,3,2,1,0:T(8,128)(2,1)S(1)}, bf16[3,3,3,256,256]{4,3,2,1,0:T(8,128)(2,1)}, u32[]{:S(2)}) copy-start(bf16[3,3,3,256,256]{4,3,2,1,0:T(8,128)(2,1)} %refs_5_.1) | copy-start | bytes 10616836
  9.2 1.7 %collective-permute-start.2 = (bf16[10,4,16,256]{3,2,1,0:T(8,128)(2,1)S(1)}, bf16[10,4,16,256]{3,2,1,0:T(8,128)(2,1)S(1)}, u32[]{:S(2)}, u32[]{:S(2)}) collective-permute-start(bf16[10,4,16,256]{3,2,1,0:T(8,128)(2,1)S(1)} %join_frames.1.refs_0_), channel_id=1, source_target_pairs={{0,4},{4,0},{1,5},{5,1},{2,6},{6,2},{3,7},{7,3},{8,12},{12,8},{9,1... | collective-permute-start | bytes 983048 | tf_op jit(solution)/shard_map/ppermute | solution.py:56
  11.1 4.5 %collective-permute-start.3 = (bf16[2,80,256]{2,1,0:T(8,128)(2,1)S(1)}, bf16[2,80,256]{2,1,0:T(8,128)(2,1)S(1)}, u32[]{:S(2)}, u32[]{:S(2)}) collective-permute-start(bf16[2,80,256]{2,1,0:T(8,128)(2,1)S(1)} %get-tuple-element.13), channel_id=1, source_target_pairs={{0,1},{2,3},{1,0},{3,2},{5,6},{7,15},{6,5},{4,12},{8,9},{10,11},{9... | collective-permute-start | bytes 245768 | tf_op jit(solution)/shard_map/ppermute | solution.py:378
  15.6 1.3 %collective-permute-start.4 = (bf16[2,80,256]{2,1,0:T(8,128)(2,1)S(1)}, bf16[2,80,256]{2,1,0:T(8,128)(2,1)S(1)}, u32[]{:S(2)}, u32[]{:S(2)}) collective-permute-start(bf16[2,80,256]{2,1,0:T(8,128)(2,1)S(1)} %collective-permute-done.3.refs_3_), channel_id=1, source_target_pairs={{0,4},{4,0},{1,5},{5,1},{2,6},{6,2},{3,7},{7,3},{8,12},{12,8},{9,1... | collective-permute-start | bytes 245768 | tf_op jit(solution)/shard_map/ppermute | solution.py:56

commit v8 on v7

--- a/solution.py
+++ b/solution.py
@@ -7,18 +7,19 @@
 from jax.experimental.pallas import tpu as pltpu
 from jax.sharding import PartitionSpec as P
 
+
 BF, F32 = jnp.bfloat16, jnp.float32
 EARLIER = 6
 RIM = 2
 
 
-def call(body, outs, args, scratch=(), flops=0, name=None, to=pltpu.VMEM):
+def call(body, outs, args, scratch=(), flops=0, to=pltpu.VMEM):
     spec = pl.BlockSpec(memory_space=pltpu.VMEM)
     outs = [jax.ShapeDtypeStruct(shape, kind) for shape, kind in outs]
     size = sum(a.size * a.dtype.itemsize for a in [*args, *outs])
     return pl.pallas_call(
         body, out_shape=outs, in_specs=[spec] * len(args),
-        out_specs=[pl.BlockSpec(memory_space=to)] * len(outs), name=name,
+        out_specs=[pl.BlockSpec(memory_space=to)] * len(outs),
         scratch_shapes=[pltpu.VMEM(*s) if isinstance(s, tuple) else s for s in scratch],
         cost_estimate=pl.CostEstimate(flops=flops, bytes_accessed=size, transcendentals=0),
         compiler_params=pltpu.CompilerParams(vmem_limit_bytes=32 << 20),
@@ -65,6 +66,15 @@
         before, after = jnp.where(even, got[1], got[0]), jnp.where(even, got[0], got[1])
     zero = jnp.zeros_like(before)
     return jnp.where(place > 0, before, zero), jnp.where(place < size - 1, after, zero)
+
+
+def lead(out):
+    out[...] = jnp.zeros_like(out)
+
+
+def tails(latent, lead, *outs):
+    for out in outs:
+        out[...] = latent[latent.shape[0] - out.shape[0] :]
 
 
 def join_frames(*refs, pieces):
@@ -82,7 +92,7 @@
         sends[k][...] = field[:, pl.ds(start, RIM)]
 
 
-def rims(field, got, whole):
+def rims(got, whole):
     if whole:
         got = [jnp.where(lax.axis_index("row") == 0, got[0][:, :RIM], got[0][:, -RIM:])]
     else:
@@ -93,11 +103,11 @@
 def strips(*refs, rows, whole):
     field, got = refs[0], refs[1 : 1 + rows]
     sends, own, wide = refs[1 + rows : -2], refs[-2], refs[-1]
-    frames, height, breadth, width = field.shape
+    frames, _, breadth, width = field.shape
     if whole:
         upper = lax.axis_index("row") == 0
     else:
-        before, after = rims(field, got, whole)
+        before, after = rims(got, whole)
     size = wide.shape[1] // frames
     tall = size // breadth
     for t in range(frames):
@@ -122,7 +132,7 @@
     out, wide = refs[-2:]
     count = out.shape[0]
     _, height, breadth, width = field.shape
-    before, after = rims(field, got, whole)
+    before, after = rims(got, whole)
     tall = height + 2 * RIM
     size = tall * breadth
     col = lax.broadcasted_iota(jnp.int32, (size, width), 0) % breadth
@@ -291,7 +301,6 @@
     high, kept, wide = high - 2, later - 2, out.shape[-1]
     steps = sems.shape[0]
     count = kept // steps
-    kernel = paired[...].reshape(-1, paired.shape[-1])
 
     def leave(step):
         mine = pl.ds(step * count, count)
@@ -304,6 +313,7 @@
             fine[dj, b : b + high, pl.ds(begin + a, count)].reshape(-1, half)
             for a in range(3) for b in range(3) for dj in range(2)
         ]
+        kernel = paired[...].reshape(-1, paired.shape[-1])
         found = jnp.dot(jnp.concatenate(taps, 1), kernel, preferred_element_type=F32)
         for y in range(high):
             for t in range(count):
@@ -324,17 +334,25 @@
     mid, fine = w_first.shape[-1], w_second.shape[-1]
     last = w_third.shape[-1]
     sections = lax.axis_size("section")
-    pieces, got, left, by = [], [], EARLIER, 1
+    pieces, left, by = [], EARLIER, 1
     while left > 0:
-        take = min(left, frames)
+        pieces.insert(0, (min(left, frames), by))
+        left, by = left - frames, by + 1
+    (first_of_all,) = call(lead, [((8, LANES), F32)], [], flops=COVER)
+    part = [take for take, _ in pieces if take < frames]
+    if part:
+        ends = list(call(
+            tails, [((take, height, breadth, width), BF) for take in part],
+            [latent, first_of_all],
+        ))
+    got = []
+    for take, by in pieces:
         ring = [(i, (i + by) % sections) for i in range(sections)]
-        got.insert(0, lax.ppermute(latent[frames - take :], "section", ring))
-        pieces.insert(0, (take, by))
-        left, by = left - take, by + 1
+        got.append(lax.ppermute(ends.pop(0) if take < frames else latent, "section", ring))
     summed, paired, ready = call(
         kernels,
         [((3, 2, 2, mid, 4 * fine), BF), ((3, 3, 2, 2 * fine, 2 * last), BF), ((8, LANES), F32)],
-        [w_second, w_third], flops=COVER, name="kernels",
+        [w_second, w_third], flops=COVER,
     )
     total = frames + EARLIER
     row_places, col_places = lax.axis_size("row"), lax.axis_size("col")
@@ -344,7 +362,7 @@
     field, *sends = call(
         functools.partial(join_frames, pieces=pieces),
         [((total, height, breadth, width), BF)] + payload,
-        [latent, ready, *got], flops=COVER, name="join_frames",
+        [latent, ready, *got], flops=COVER,
     )
     rows_got = exchange([field] if whole else sends, "row")
     tall = height + 2 * RIM
@@ -352,7 +370,7 @@
     *sends, own = call(
         functools.partial(strips, rows=rounds, whole=whole),
         sides + [((2 * RIM, total * tall, width), BF)], [field, *rows_got],
-        [(blocked(total * tall * breadth, width), F32)], name="strips",
+        [(blocked(total * tall * breadth, width), F32)],
     )
     early = total - 2
 
@@ -361,7 +379,7 @@
             functools.partial(first_inner, rows=rounds, whole=whole, begin=begin),
             [((count, tall - 2, breadth, mid), F32)], [field, *rows_got, w_first, *after],
             [((3, count + 2, tall, breadth, width), BF)],
-            flops=2 * 27 * count * (tall - 2) * breadth * width * mid, name="first_inner",
+            flops=2 * 27 * count * (tall - 2) * breadth * width * mid,
         )
 
     if whole:
@@ -390,12 +408,12 @@
         [((2, early, tall - 2, breadth, mid), BF), ((2, size + 8, mid), F32)],
         [*inners, own, *cols_got, w_first],
         [((4 * RIM, total * tall, width), BF), (blocked(size * (breadth + SLACK), mid), F32)],
-        flops=10**9, name="first_outer",
+        flops=10**9,
     )
     (second,) = call(
         second_conv, [((2, 2 * corners, later, breadth, 2 * fine), BF)], [near, far, summed],
         [(blocked(later * tall * (breadth + SLACK), 4 * fine), F32)],
-        flops=2 * 10**9, name="second_conv",
+        flops=2 * 10**9,
     )
     steps = 2 if frames % 2 == 0 else 1
     (out,) = call(
@@ -404,7 +422,7 @@
             ((frames // steps, 2 * height, 2 * breadth, last), F32),
             ((frames, 2 * height, 2 * breadth, last), BF), pltpu.SemaphoreType.DMA((steps,)),
         ],
-        flops=10**9, name="third_conv", to=pl.ANY,
+        flops=10**9, to=pl.ANY,
     )
     return out
 
@@ -412,6 +430,7 @@
 def solution(mesh):
     in_specs = (P("section", "row", "col", None), P(), P(), P())
     out_specs = P("section", "row", "col", None)
+
     return jax.shard_map(
         per_device, mesh=mesh, in_specs=in_specs, out_specs=out_specs, check_vma=False
     )

time: 23 us -> 22.7 us (0.987)
  local copies, waits for them, and re-layouts: 3.53 us -> 0.01 us
  waiting for transfers between devices: 2.53 us -> 5.9 us
    ppermute x2, waiting for transfers between devices: 0.01 us -> 3.43 us  [per_device(): lax.ppermute(ends.pop(0) if take < frames else latent, 'section', ring)]
    unnamed x8, local copies, waits for them, and re-layouts: 2.65 us -> 0.01 us
    slice x1 -> x0, local copies, waits for them, and re-layouts: 0.88 us -> none  [per_device(): got.insert(0, lax.ppermute(latent[frames - take:], 'section', ring))]
    pallas_call x8 -> x10, Pallas kernels: 10.2 us -> 10.1 us  [call(): pl.pallas_call(body, out_shape=outs, in_specs=[spec] * len(args), out_spe...]
  transfers between devices with their start and end apart: 5 -> 5, of which waited for: 3 -> 4; matrix products, arithmetic and copies ran while one was open for 4% -> 0% of each run, Pallas kernels for 18% -> 18%
where the time goes in v8:
time: 22.7 us; the launch traced here: 22.6 us
  Pallas kernels  10.1 us (44%)
  starting transfers between devices  6.52 us (29%)
  waiting for transfers between devices  5.9 us (26%)
    pallas_call x10, Pallas kernels, call(): pl.pallas_call(body, out_shape=outs, in_specs=[spec] * len(args), out_spe...  10.1 us
    ppermute x2, starting transfers between devices, per_device(): lax.ppermute(ends.pop(0) if take < frames else latent, 'section', ring)  4.61 us
    ppermute x2, waiting for transfers between devices, per_device(): lax.ppermute(ends.pop(0) if take < frames else latent, 'section', ring)  3.43 us
    ppermute x1, starting transfers between devices, per_device(): came = lax.ppermute(sends[0], ('section', 'row', 'col'), pairs)  1.82 us
    ppermute x2, waiting for transfers between devices, exchange(): lax.ppermute(s, axis, pairs)  1.68 us
    ppermute x1, waiting for transfers between devices, per_device(): came = lax.ppermute(sends[0], ('section', 'row', 'col'), pairs)  0.79 us
  transfers between devices with their start and end apart: 5, of which 4 were waited for; matrix products, arithmetic and copies ran while one was open for 0% of the time, Pallas kernels for 18%

profile of v8, /device:TPU:0, one launch (start us, length us, event | category | flops | bytes accessed | tf_op | source)
XLA Modules:
  0.0 22.6 jit_solution(10475965096250516024)
XLA Ops:
  0.0 0.0 copy-start.1
  0.0 0.0 copy-start.3
  0.0 0.0 copy-start.2
  0.0 3.0 %collective-permute-start.1 = (bf16[4,4,16,256]{3,2,1,0:T(8,128)(2,1)}, bf16[4,4,16,256]{3,2,1,0:T(8,128)(2,1)S(1)}, u32[]{:S(2)}, u32[]{:S(2)}) collective-permute-start(bf16[4,4,16,256]{3,2,1,0:T(8,128)(2,1)} %refs_0_.1), channel_id=1, source_target_pairs={{0,8},{8,16},{16,24},{24,0},{1,9},{9,17},{17,25},{25,1},{2,10},{10... | collective-permute-start | bytes 393224 | tf_op jit(solution)/shard_map/ppermute | solution.py:351
  3.0 0.0 copy-done.1
  3.0 1.6 %collective-permute-start = (bf16[2,4,16,256]{3,2,1,0:T(8,128)(2,1)S(1)}, bf16[2,4,16,256]{3,2,1,0:T(8,128)(2,1)S(1)}, u32[]{:S(2)}, u32[]{:S(2)}) collective-permute-start(bf16[2,4,16,256]{3,2,1,0:T(8,128)(2,1)S(1)} %shard_map.48), channel_id=1, source_target_pairs={{0,16},{8,24},{16,0},{24,8},{1,17},{9,25},{17,1},{25,9},{2,18},{10... | collective-permute-start | bytes 196616 | tf_op jit(solution)/shard_map/ppermute | solution.py:351
  4.6 0.0 copy-done.3
  4.6 0.0 copy-done.2
  4.6 1.0 %shard_map.46 = (bf16[3,2,2,256,512]{4,3,2,1,0:T(8,128)(2,1)S(1)}, bf16[3,3,2,256,256]{4,3,2,1,0:T(8,128)(2,1)S(1)}, f32[8,128]{1,0:T(8,128)S(1)}) custom-call(bf16[3,3,3,256,128]{4,3,2,1,0:T(8,128)(2,1)S(1)} %copy-done.2, bf16[3,3,3,128,128]{4,3,2,1,0:T(8,128)(2,1)S(1)} %copy-done.3), custom_call_target="tpu_custom_call" | custom-call | flops 4000000000 | bytes 8163328 | tf_op jit(solution)/shard_map/pallas_call | solution.py:20
  5.7 3.4 %collective-permute-done.refs_2_ = bf16[2,4,16,256]{3,2,1,0:T(8,128)(2,1)S(1)} collective-permute-done((bf16[2,4,16,256]{3,2,1,0:T(8,128)(2,1)S(1)}, bf16[2,4,16,256]{3,2,1,0:T(8,128)(2,1)S(1)}, u32[]{:S(2)}, u32[]{:S(2)}) %collective-permute-start) | collective-permute-done | bytes 65568 | tf_op jit(solution)/shard_map/ppermute | solution.py:351
  9.1 0.0 collective-permute-done.1.refs_3_
  9.1 0.0 copy-start
  9.2 0.1 collective-permute-start.2
  9.2 1.6 %collective-permute-done.2.refs_1_ = bf16[10,4,16,256]{3,2,1,0:T(8,128)(2,1)S(1)} collective-permute-done((bf16[10,4,16,256]{3,2,1,0:T(8,128)(2,1)S(1)}, bf16[10,4,16,256]{3,2,1,0:T(8,128)(2,1)S(1)}, u32[]{:S(2)}, u32[]{:S(2)}) %collective-permute-start.2) | collective-permute-done | bytes 327712 | tf_op jit(solution)/shard_map/ppermute | solution.py:57
  10.8 0.2 %shard_map.51 = (bf16[2,80,256]{2,1,0:T(8,128)(2,1)S(1)}, bf16[4,80,256]{2,1,0:T(8,128)(2,1)S(1)}) custom-call(bf16[10,4,16,256]{3,2,1,0:T(8,128)(2,1)S(1)} %shard_map.49.refs_0_, bf16[10,4,16,256]{3,2,1,0:T(8,128)(2,1)S(1)} %collective-permute-done.2.refs_1_), custom_call_target="tpu_custom_call" | custom-call | bytes 901120 | tf_op jit(solution)/shard_map/pallas_call | solution.py:20
  11.1 1.8 %collective-permute-start.3 = (bf16[2,80,256]{2,1,0:T(8,128)(2,1)S(1)}, bf16[2,80,256]{2,1,0:T(8,128)(2,1)S(1)}, u32[]{:S(2)}, u32[]{:S(2)}) collective-permute-start(bf16[2,80,256]{2,1,0:T(8,128)(2,1)S(1)} %get-tuple-element.13), channel_id=1, source_target_pairs={{0,1},{2,3},{1,0},{3,2},{5,6},{7,15},{6,5},{4,12},{8,9},{10,11},{9... | collective-permute-start | bytes 245768 | tf_op jit(solution)/shard_map/ppermute | solution.py:396
  12.9 0.0 copy-done
  12.9 1.9 %shard_map.50.refs_0_ = f32[5,6,16,256]{3,2,1,0:T(8,128)S(1)} custom-call(bf16[10,4,16,256]{3,2,1,0:T(8,128)(2,1)S(1)} %shard_map.49.refs_0_, bf16[10,4,16,256]{3,2,1,0:T(8,128)(2,1)S(1)} %collective-permute-done.2.refs_1_, bf16[3,3,3,256,256]{4,3,2,1,0:T(8,128)(2,1)S(1)} %copy-done), custom_call_target="tpu_custom_call" | custom-call | flops 1698693120 | bytes 4685824 | tf_op jit(solution)/shard_map/pallas_call | solution.py:20
  14.8 0.8 %collective-permute-done.3.refs_3_ = bf16[2,80,256]{2,1,0:T(8,128)(2,1)S(1)} collective-permute-done((bf16[2,80,256]{2,1,0:T(8,128)(2,1)S(1)}, bf16[2,80,256]{2,1,0:T(8,128)(2,1)S(1)}, u32[]{:S(2)}, u32[]{:S(2)}) %collective-permute-start.3) | collective-permute-done | bytes 81952 | tf_op jit(solution)/shard_map/ppermute | solution.py:396
  15.6 0.0 collective-permute-start.4
  15.6 1.2 %shard_map.52.refs_1_ = f32[3,6,16,256]{3,2,1,0:T(8,128)S(1)} custom-call(bf16[10,4,16,256]{3,2,1,0:T(8,128)(2,1)S(1)} %shard_map.49.refs_0_, bf16[10,4,16,256]{3,2,1,0:T(8,128)(2,1)S(1)} %collective-permute-done.2.refs_1_, bf16[3,3,3,256,256]{4,3,2,1,0:T(8,128)(2,1)S(1)} %copy-done, bf16[2,80,256]{2,1,0:T(8,128)(2,1)S(1)} %collective-permute-done.3.refs_3_), custom_call_target="tpu_custom_call" | custom-call | flops 1019215872 | bytes 4571136 | tf_op jit(solution)/shard_map/pallas_call | solution.py:20
  16.8 0.1 collective-permute-done.4.refs_4_
  16.9 1.4 %shard_map.53 = (bf16[2,8,6,16,256]{4,3,2,1,0:T(8,128)(2,1)S(1)}, f32[2,72,256]{2,1,0:T(8,128)S(1)}) custom-call(f32[5,6,16,256]{3,2,1,0:T(8,128)S(1)} %shard_map.50.refs_0_, f32[3,6,16,256]{3,2,1,0:T(8,128)S(1)} %shard_map.52.refs_1_, bf16[4,80,256]{2,1,0:T(8,128)(2,1)S(1)} %get-tuple-element.14.refs_2_, ...), custom_call_target="tpu_custom_call" | custom-call | flops 1000000000 | bytes 5586944 | tf_op jit(solution)/shard_map/pallas_call | solution.py:20
  18.3 1.9 %shard_map.54.fine = bf16[2,10,6,16,256]{4,3,2,1,0:T(8,128)(2,1)S(1)} custom-call(bf16[2,8,6,16,256]{4,3,2,1,0:T(8,128)(2,1)S(1)} %get-tuple-element.15.near, f32[2,72,256]{2,1,0:T(8,128)S(1)} %get-tuple-element.16.far, bf16[3,2,2,256,512]{4,3,2,1,0:T(8,128)(2,1)S(1)} %get-tuple-element.17.summed), custom_call_target="tpu_custom_call" | custom-call | flops 2000000000 | bytes 5062656 | tf_op jit(solution)/shard_map/pallas_call | solution.py:20
  20.3 2.3 %shard_map.55 = bf16[4,8,32,128]{3,2,1,0:T(8,128)(2,1)} custom-call(bf16[2,10,6,16,256]{4,3,2,1,0:T(8,128)(2,1)S(1)} %shard_map.54.fine, bf16[3,3,2,256,256]{4,3,2,1,0:T(8,128)(2,1)S(1)} %get-tuple-element.18.paired), custom_call_target="tpu_custom_call" | custom-call | flops 1000000000 | bytes 3604480 | tf_op jit(solution)/shard_map/pallas_call | solution.py:20
  (3 shorter events, 0.0 us)
Async XLA Ops:
  0.0 3.0 %copy-start.1 = (bf16[4,4,16,256]{3,2,1,0:T(8,128)(2,1)S(1)}, bf16[4,4,16,256]{3,2,1,0:T(8,128)(2,1)}, u32[]{:S(2)}) copy-start(bf16[4,4,16,256]{3,2,1,0:T(8,128)(2,1)} %refs_0_.1) | copy-start | bytes 393220
  0.0 4.6 %copy-start.3 = (bf16[3,3,3,128,128]{4,3,2,1,0:T(8,128)(2,1)S(1)}, bf16[3,3,3,128,128]{4,3,2,1,0:T(8,128)(2,1)}, u32[]{:S(2)}) copy-start(bf16[3,3,3,128,128]{4,3,2,1,0:T(8,128)(2,1)} %third.1) | copy-start | bytes 2654212
  0.0 4.6 %copy-start.2 = (bf16[3,3,3,256,128]{4,3,2,1,0:T(8,128)(2,1)S(1)}, bf16[3,3,3,256,128]{4,3,2,1,0:T(8,128)(2,1)}, u32[]{:S(2)}) copy-start(bf16[3,3,3,256,128]{4,3,2,1,0:T(8,128)(2,1)} %second.1) | copy-start | bytes 5308420
  0.0 9.1 %collective-permute-start.1 = (bf16[4,4,16,256]{3,2,1,0:T(8,128)(2,1)}, bf16[4,4,16,256]{3,2,1,0:T(8,128)(2,1)S(1)}, u32[]{:S(2)}, u32[]{:S(2)}) collective-permute-start(bf16[4,4,16,256]{3,2,1,0:T(8,128)(2,1)} %refs_0_.1), channel_id=1, source_target_pairs={{0,8},{8,16},{16,24},{24,0},{1,9},{9,17},{17,25},{25,1},{2,10},{10... | collective-permute-start | bytes 393224 | tf_op jit(solution)/shard_map/ppermute | solution.py:351
  3.0 6.1 %collective-permute-start = (bf16[2,4,16,256]{3,2,1,0:T(8,128)(2,1)S(1)}, bf16[2,4,16,256]{3,2,1,0:T(8,128)(2,1)S(1)}, u32[]{:S(2)}, u32[]{:S(2)}) collective-permute-start(bf16[2,4,16,256]{3,2,1,0:T(8,128)(2,1)S(1)} %shard_map.48), channel_id=1, source_target_pairs={{0,16},{8,24},{16,0},{24,8},{1,17},{9,25},{17,1},{25,9},{2,18},{10... | collective-permute-start | bytes 196616 | tf_op jit(solution)/shard_map/ppermute | solution.py:351
  9.1 3.8 %copy-start = (bf16[3,3,3,256,256]{4,3,2,1,0:T(8,128)(2,1)S(1)}, bf16[3,3,3,256,256]{4,3,2,1,0:T(8,128)(2,1)}, u32[]{:S(2)}) copy-start(bf16[3,3,3,256,256]{4,3,2,1,0:T(8,128)(2,1)} %refs_5_.1) | copy-start | bytes 10616836
  9.2 1.7 %collective-permute-start.2 = (bf16[10,4,16,256]{3,2,1,0:T(8,128)(2,1)S(1)}, bf16[10,4,16,256]{3,2,1,0:T(8,128)(2,1)S(1)}, u32[]{:S(2)}, u32[]{:S(2)}) collective-permute-start(bf16[10,4,16,256]{3,2,1,0:T(8,128)(2,1)S(1)} %shard_map.49.refs_0_), channel_id=1, source_target_pairs={{0,4},{4,0},{1,5},{5,1},{2,6},{6,2},{3,7},{7,3},{8,12},{12,8},{9,1... | collective-permute-start | bytes 983048 | tf_op jit(solution)/shard_map/ppermute | solution.py:57
  11.1 4.5 %collective-permute-start.3 = (bf16[2,80,256]{2,1,0:T(8,128)(2,1)S(1)}, bf16[2,80,256]{2,1,0:T(8,128)(2,1)S(1)}, u32[]{:S(2)}, u32[]{:S(2)}) collective-permute-start(bf16[2,80,256]{2,1,0:T(8,128)(2,1)S(1)} %get-tuple-element.13), channel_id=1, source_target_pairs={{0,1},{2,3},{1,0},{3,2},{5,6},{7,15},{6,5},{4,12},{8,9},{10,11},{9... | collective-permute-start | bytes 245768 | tf_op jit(solution)/shard_map/ppermute | solution.py:396
  15.6 1.3 %collective-permute-start.4 = (bf16[2,80,256]{2,1,0:T(8,128)(2,1)S(1)}, bf16[2,80,256]{2,1,0:T(8,128)(2,1)S(1)}, u32[]{:S(2)}, u32[]{:S(2)}) collective-permute-start(bf16[2,80,256]{2,1,0:T(8,128)(2,1)S(1)} %collective-permute-done.3.refs_3_), channel_id=1, source_target_pairs={{0,4},{4,0},{1,5},{5,1},{2,6},{6,2},{3,7},{7,3},{8,12},{12,8},{9,1... | collective-permute-start | bytes 245768 | tf_op jit(solution)/shard_map/ppermute | solution.py:57

commit v9 on v8

v9 whole, which is shorter than its diff:
```python
import functools

import jax
import jax.numpy as jnp
from jax import lax
from jax.experimental import pallas as pl
from jax.experimental.pallas import tpu as pltpu
from jax.sharding import PartitionSpec as P


BF, F32 = jnp.bfloat16, jnp.float32
EARLIER = 6
RIM = 2


def call(body, outs, args, scratch=(), flops=0, to=pltpu.VMEM):
    spec = pl.BlockSpec(memory_space=pltpu.VMEM)
    outs = [jax.ShapeDtypeStruct(shape, kind) for shape, kind in outs]
    size = sum(a.size * a.dtype.itemsize for a in [*args, *outs])
    return pl.pallas_call(
        body, out_shape=outs, in_specs=[spec] * len(args),
        out_specs=[pl.BlockSpec(memory_space=to)] * len(outs),
        scratch_shapes=[pltpu.VMEM(*s) if isinstance(s, tuple) else s for s in scratch],
        cost_estimate=pl.CostEstimate(flops=flops, bytes_accessed=size, transcendentals=0),
        compiler_params=pltpu.CompilerParams(vmem_limit_bytes=32 << 20),
    )(*args)


LANES = 128
COVER = 4 * 10**9
SLACK = 8


def put(ref, rows, value):
    for k in range(ref.shape[0]):
        ref[k, rows, :] = value[:, k * LANES : (k + 1) * LANES]


def take(ref, rows, blocks=None):
    blocks = range(ref.shape[0]) if blocks is None else blocks
    return jnp.concatenate([ref[k, rows, :] for k in blocks], 1)


def blocked(rows, width):
    return (width // LANES, rows, LANES)


def swaps(size):
    assert size % 2 == 0
    rounds = [[(i, i + 1) for i in range(0, size, 2)]]
    if size > 2:
        rounds.append([(i, (i + 1) % size) for i in range(1, size, 2)])
    return [pairs + [(j, i) for i, j in pairs] for pairs in rounds]


def exchange(sends, axis):
    return [lax.ppermute(s, axis, pairs) for s, pairs in zip(sends, swaps(lax.axis_size(axis)))]


def column_exchange(sends, sections):
    rows, cols = lax.axis_size("row"), lax.axis_size("col")
    got = []
    for send, pairing in zip(sends, swaps(cols)):
        pairs = []
        for group in range(sections * rows):
            section, row = divmod(group, rows)
            for i, j in pairing:
                far = abs(i - j) > 1 and sections % 2 == 0
                to = ((section ^ 1) * rows + row, i) if far else (group, j)
                pairs.append((group * cols + i, to[0] * cols + to[1]))
        got.append(lax.ppermute(send, ("section", "row", "col"), pairs))
    return got


def arrived(axis, got):
    place, size = lax.axis_index(axis), lax.axis_size(axis)
    even = place % 2 == 0
    if len(got) == 1:
        before = after = got[0]
    else:
        before, after = jnp.where(even, got[1], got[0]), jnp.where(even, got[0], got[1])
    zero = jnp.zeros_like(before)
    return jnp.where(place > 0, before, zero), jnp.where(place < size - 1, after, zero)


def lead(out):
    out[...] = jnp.zeros_like(out)


def tails(latent, lead, *outs):
    for out in outs:
        out[...] = latent[latent.shape[0] - out.shape[0] :]


def send_rows(field, sends):
    even = lax.axis_index("row") % 2 == 0
    last = field.shape[1] - RIM
    for k, send in enumerate(sends):
        start = jnp.where(even, 0, last) if k else jnp.where(even, last, 0)
        send[...] = field[:, pl.ds(start, RIM)]


def own_rows(latent, lead, *sends):
    send_rows(latent, sends)


def join_frames(*refs, pieces):
    got = refs[1 : 1 + len(pieces)]
    field, sends = refs[1 + len(pieces)], refs[2 + len(pieces) :]
    place, at = lax.axis_index("section"), 0
    for (take, by), ref in zip(pieces, got):
        field[at : at + take] = jnp.where(place >= by, ref[...], jnp.zeros_like(ref))
        at += take
    send_rows(field, sends)


def strips(fields, out, wide, narrow):
    tall, breadth, width = fields[0].shape[1:]
    size, at = tall * breadth, 0
    for field in fields:
        for t in range(field.shape[0]):
            put(wide, slice(at, at + size), field[t].astype(F32).reshape(size, width))
            at += size
    frames = at // size
    for i, c in enumerate([0, 1, breadth - 2, breadth - 1]):
        for r in range(tall):
            narrow[r * frames : (r + 1) * frames] = take(
                wide, pl.ds(r * breadth + c, frames, stride=size)
            )
        out[i] = narrow[...].astype(BF)


def send_columns(before, latent, *refs):
    sends, own, wide, narrow = refs[:-3], refs[-3], refs[-2], refs[-1]
    strips([before, latent], own, wide, narrow)
    right = lax.axis_index("col") % 2 == 0
    for k, send in enumerate(sends):
        start = jnp.where(right, 0, RIM) if k else jnp.where(right, RIM, 0)
        send[...] = own[pl.ds(start, RIM)]


def rim_columns(*refs, rows):
    own, wide, narrow = refs[-3:]
    fields = []
    for got in (refs[:rows], refs[rows : 2 * rows]):
        fields.append(jnp.concatenate(arrived("row", [g[...] for g in got]), 1))
    strips(fields, own, wide, narrow)


def turn_columns(*refs, cols, frames):
    got, side, sends, narrow = refs[:cols], refs[cols + 1], refs[cols + 2 : -1], refs[-1]
    before, after = arrived("col", [g[...] for g in got])
    even = lax.axis_index("row") % 2 == 0
    size = RIM * frames
    for i, strip in enumerate([before[0], before[1], after[0], after[1]]):
        side[i] = strip
        narrow[...] = strip.astype(F32)
        first, last = narrow[:size], narrow[narrow.shape[0] - size :]
        for k, send in enumerate(sends):
            value = jnp.where(even, first, last) if k else jnp.where(even, last, first)
            send[i] = value.astype(BF)


def first_inner(*refs, sources, rows, begin):
    out, wide = refs[-2:]
    kernel = refs[sources * (1 + rows)]
    count = out.shape[0]
    frames = []
    for k in range(sources):
        field, *got = refs[k * (1 + rows) : (k + 1) * (1 + rows)]
        before, after = arrived("row", [g[...] for g in got])
        frames += [(before, field, after, t) for t in range(field.shape[0])]
    height, breadth, width = frames[0][1].shape[1:]
    tall = height + 2 * RIM
    size = tall * breadth
    col = lax.broadcasted_iota(jnp.int32, (size, width), 0) % breadth
    for t in range(count + 2):
        *parts, at = frames[begin + t]
        rows_of = jnp.concatenate([part[at] for part in parts], 0)
        wide[1, t] = rows_of
        flat = rows_of.reshape(size, width).astype(F32)
        lower = jnp.where(col == 0, 0.0, pltpu.roll(flat, 1, 0))
        upper = jnp.where(col == breadth - 1, 0.0, pltpu.roll(flat, size - 1, 0))
        wide[0, t] = lower.astype(BF).reshape(rows_of.shape)
        wide[2, t] = upper.astype(BF).reshape(rows_of.shape)
    taps = [
        wide[e, a : a + count, b : b + tall - 2].reshape(-1, width)
        for a in range(3) for b in range(3) for e in range(3)
    ]
    found = jnp.dot(
        jnp.concatenate(taps, 1), kernel[...].reshape(-1, kernel.shape[-1]), preferred_element_type=F32
    )
    out[...] = found.reshape(out.shape)


def kernels(second, third, summed, paired, ready):
    ready[...] = jnp.zeros_like(ready)
    fine = second.shape[-1]
    reads = [[(0, 1), (2,)], [(0,), (1, 2)]]
    for a in range(3):
        tap = [[second[a, b, e].astype(F32) for e in range(3)] for b in range(3)]
        for di in range(2):
            for dj in range(2):
                for py in range(2):
                    for px in range(2):
                        parts = [tap[b][e] for b in reads[py][di] for e in reads[px][dj]]
                        at = (2 * py + px) * fine
                        summed[a, di, dj, :, at : at + fine] = sum(parts[1:], parts[0]).astype(BF)
    width, out = third.shape[-2:]
    for a in range(3):
        for b in range(3):
            for dj in range(2):
                for px in range(2):
                    for q in range(2):
                        e = 2 * dj + px - q
                        block = third[a, b, e] if 0 <= e < 3 else jnp.zeros((width, out), BF)
                        paired[a, b, dj, px * width : (px + 1) * width, q * out : (q + 1) * out] = block


def limits(axis):
    return lax.axis_index(axis) == 0, lax.axis_index(axis) == lax.axis_size(axis) - 1


def first_outer(*refs, parts, rounds):
    inner, own, rim, side = refs[:parts], *refs[parts : parts + 3]
    turned = refs[parts + 3 : parts + 3 + rounds]
    kernel, near, far, edge, moved, coarse = refs[parts + 3 + rounds :]
    rows, breadth, width = inner[0].shape[1:]
    frames = sum(part.shape[0] for part in inner)
    total, tall = frames + 2, rows + 2
    (top, bottom), (leftmost, rightmost) = limits("row"), limits("col")

    above, below = arrived("row", [g[...] for g in turned])
    ends = RIM * total
    full = tall * total
    for i in range(RIM):
        for k, (main, at) in enumerate([(side, i), (own, i), (own, RIM + i), (side, RIM + i)]):
            strip = edge.at[k * RIM + i]
            strip[ends : full - ends] = main[at].astype(F32)
            if main is own:
                strip[:ends] = rim[at, :ends].astype(F32)
                strip[full - ends : full] = rim[at, ends : 2 * ends].astype(F32)
            else:
                strip[:ends] = above[at].astype(F32)
                strip[full - ends : full] = below[at].astype(F32)
    for i in range(4 * RIM):
        for a in range(3):
            moved[i, a] = jnp.concatenate(
                [edge[i, r * total + a : r * total + a + frames] for r in range(tall)], 0
            ).astype(BF)
    size = rows * frames
    lhs = jnp.concatenate([
        jnp.concatenate(
            [moved[i + e, a, b * frames : b * frames + size] for i in (0, 1, 4, 5)], 0
        )
        for a in range(3) for b in range(3) for e in range(3)
    ], 1)
    found = jnp.dot(lhs, kernel[...].reshape(-1, kernel.shape[-1]), preferred_element_type=F32)
    left, begin, end, right = [found[i * size : (i + 1) * size] for i in range(4)]

    pitch = breadth + SLACK
    count = 0
    for part in inner:
        for t in range(part.shape[0]):
            for r in range(rows):
                at = (r * frames + count) * pitch
                put(coarse, slice(at, at + breadth), part[t, r])
            count += 1
    put(coarse, pl.ds(0, size, stride=pitch), begin)
    put(coarse, pl.ds(breadth - 1, size, stride=pitch), end)
    put(coarse, pl.ds(breadth, size, stride=pitch), right)

    slot = lax.broadcasted_iota(jnp.int32, (breadth, width), 0)
    ends = rightmost & (slot == breadth - 1)
    for r in range(rows):
        lost = top if r == 0 else bottom if r == rows - 1 else None
        for t in range(frames):
            at = (r * frames + t) * pitch
            for dj in range(2):
                value = jnp.maximum(take(coarse, slice(at + dj, at + dj + breadth)), 0.0)
                gone = [g for g in (lost, ends if dj else None) if g is not None]
                if gone:
                    value = jnp.where(functools.reduce(jnp.logical_or, gone), 0.0, value)
                near[dj, r, t] = value.astype(BF)
    row = lax.broadcasted_iota(jnp.int32, (size, width), 0) // frames
    outside = (top & (row == 0)) | (bottom & (row == rows - 1))
    far[0, :size] = jnp.where(outside | leftmost, 0.0, jnp.maximum(left, 0.0))
    far[1, :size] = jnp.where(outside, 0.0, jnp.maximum(begin, 0.0))


def second_conv(near, far, summed, fine, grown):
    _, rows, frames, breadth, width = near.shape
    pitch = breadth + SLACK
    (top, bottom), (leftmost, rightmost) = limits("row"), limits("col")
    corners, later = rows - 1, frames - 2
    short = corners * frames
    taps = [
        jnp.concatenate([
            near[dj, di : di + corners, a : a + later].reshape(-1, width),
            far[dj, di * frames + a : di * frames + a + short].astype(BF),
        ], 0)
        for a in range(3) for di in range(2) for dj in range(2)
    ]
    found = jnp.dot(
        jnp.concatenate(taps, 1), summed[...].reshape(-1, summed.shape[-1]), preferred_element_type=F32
    )
    found = jnp.maximum(found, 0.0)
    full = later * corners * breadth
    half = found.shape[1] // 2
    for i in range(corners):
        for t in range(later):
            at, to = (i * later + t) * breadth, (i * frames + t) * pitch + SLACK
            put(grown, slice(to, to + breadth), found[at : at + breadth])
    put(grown, pl.ds(SLACK - 1, short, stride=pitch), found[full:])
    slot = lax.broadcasted_iota(jnp.int32, (breadth, half), 0)
    side = lax.broadcasted_iota(jnp.int32, (breadth, half), 1) < half // 2
    begins = leftmost & (slot == 0) & side
    ends = rightmost & (slot == breadth - 1) & ~side
    for t in range(later):
        for i in range(corners):
            for py in range(2):
                blocks = range(py * half // LANES, (py + 1) * half // LANES)
                lost = (top if py == 0 and i == 0 else bottom if py == 1 and i == corners - 1 else None)
                for dj, gone in enumerate((begins, ends)):
                    gone = gone if lost is None else gone | lost
                    at = (i * frames + t) * pitch + SLACK - 1 + dj
                    value = take(grown, slice(at, at + breadth), blocks)
                    fine[dj, 2 * i + py, t] = jnp.where(gone, 0.0, value).astype(BF)


def third_conv(fine, paired, out, spread, ready, sems):
    _, high, later, breadth, half = fine.shape
    high, kept, wide = high - 2, later - 2, out.shape[-1]
    steps = sems.shape[0]
    count = kept // steps

    def leave(step):
        mine = pl.ds(step * count, count)
        return pltpu.make_async_copy(ready.at[mine], out.at[mine], sems.at[step])

    @pl.loop(0, steps)
    def _(step):
        begin = step * count
        taps = [
            fine[dj, b : b + high, pl.ds(begin + a, count)].reshape(-1, half)
            for a in range(3) for b in range(3) for dj in range(2)
        ]
        kernel = paired[...].reshape(-1, paired.shape[-1])
        found = jnp.dot(jnp.concatenate(taps, 1), kernel, preferred_element_type=F32)
        for y in range(high):
            for t in range(count):
                at = (y * count + t) * breadth
                for q in range(2):
                    spread[t, y, pl.ds(q, breadth, stride=2), :] = found[
                        at : at + breadth, q * wide : (q + 1) * wide
                    ]
        ready[pl.ds(begin, count)] = spread[...].astype(BF)
        leave(step).start()

    for step in range(steps):
        leave(step).wait()


def per_device(latent, w_first, w_second, w_third):
    frames, height, breadth, width = latent.shape
    mid, fine = w_first.shape[-1], w_second.shape[-1]
    last = w_third.shape[-1]
    sections = lax.axis_size("section")
    pieces, left, by = [], EARLIER, 1
    while left > 0:
        pieces.insert(0, (min(left, frames), by))
        left, by = left - frames, by + 1
    (first_of_all,) = call(lead, [((8, LANES), F32)], [], flops=COVER)
    part = [take for take, _ in pieces if take < frames]
    ends = []
    if part:
        ends = list(call(
            tails, [((take, height, breadth, width), BF) for take in part],
            [latent, first_of_all],
        ))
    got = []
    for take, by in pieces:
        ring = [(i, (i + by) % sections) for i in range(sections)]
        got.append(lax.ppermute(ends.pop(0) if take < frames else latent, "section", ring))

    rounds, cols = len(swaps(lax.axis_size("row"))), len(swaps(lax.axis_size("col")))
    total, tall = frames + EARLIER, height + 2 * RIM
    early = total - 2
    sends = call(own_rows, [((frames, RIM, breadth, width), BF)] * rounds, [latent, first_of_all])
    own_got = exchange(sends, "row")
    summed, paired, ready = call(
        kernels,
        [((3, 2, 2, mid, 4 * fine), BF), ((3, 3, 2, 2 * fine, 2 * last), BF), ((8, LANES), F32)],
        [w_second, w_third], flops=COVER,
    )

    def inner(fields, begin, count, *after):
        return call(
            functools.partial(first_inner, sources=len(fields), rows=rounds, begin=begin),
            [((count, tall - 2, breadth, mid), F32)],
            [a for field, rim in fields for a in (field, *rim)] + [w_first, *after],
            [((3, count + 2, tall, breadth, width), BF)],
            flops=2 * 27 * count * (tall - 2) * breadth * width * mid,
        )

    inners = inner([(latent, own_got)], 0, frames - 2, ready)
    earlier, *sends = call(
        functools.partial(join_frames, pieces=pieces),
        [((EARLIER, height, breadth, width), BF)] + [((EARLIER, RIM, breadth, width), BF)] * rounds,
        [inners[0], *got],
    )
    early_got = exchange(sends, "row")
    strip = ((2 * RIM, height * total, width), BF)
    scratch = [(blocked(total * height * breadth, width), F32), ((height * total, width), F32)]
    *sends, own = call(
        send_columns, [((RIM, height * total, width), BF)] * cols + [strip], [earlier, latent],
        scratch,
    )
    came = column_exchange(sends, sections)
    fields = [(earlier, early_got), (latent, own_got)]
    rest = early - (frames - 2)
    cut = rest // 2
    first_part = inner(fields, 0, cut, *sends)
    side, *sends = call(
        functools.partial(turn_columns, cols=cols, frames=total),
        [strip] + [((2 * RIM, RIM * total, width), BF)] * rounds, [*came, *first_part],
        [((height * total, width), F32)],
    )
    turned = exchange(sends, "row")
    (rim,) = call(
        functools.partial(rim_columns, rows=rounds), [strip], [*early_got, *own_got, side],
        scratch,
    )
    inners = first_part + inner(fields, cut, rest - cut, side) + inners
    size = (tall - 2) * early
    near, far = call(
        functools.partial(first_outer, parts=len(inners), rounds=rounds),
        [((2, tall - 2, early, breadth, mid), BF), ((2, size + 8, mid), F32)],
        [*inners, own, rim, side, *turned, w_first],
        [
            ((4 * RIM, tall * total, width), F32), ((4 * RIM, 3, tall * early, width), BF),
            (blocked(size * (breadth + SLACK), mid), F32),
        ],
        flops=10**9,
    )
    later, corners = early - 2, tall - 3
    (second,) = call(
        second_conv, [((2, 2 * corners, later, breadth, 2 * fine), BF)], [near, far, summed],
        [(blocked(corners * early * (breadth + SLACK), 4 * fine), F32)],
        flops=2 * 10**9,
    )
    steps = 2 if frames % 2 == 0 else 1
    (out,) = call(
        third_conv, [((frames, 2 * height, 2 * breadth, last), BF)], [second, paired],
        [
            ((frames // steps, 2 * height, 2 * breadth, last), F32),
            ((frames, 2 * height, 2 * breadth, last), BF), pltpu.SemaphoreType.DMA((steps,)),
        ],
        flops=10**9, to=pl.ANY,
    )
    return out


def solution(mesh):
    in_specs = (P("section", "row", "col", None), P(), P(), P())
    out_specs = P("section", "row", "col", None)

    return jax.shard_map(
        per_device, mesh=mesh, in_specs=in_specs, out_specs=out_specs, check_vma=False
    )
```

time: 22.7 us -> 22.3 us (0.982)
  waiting for transfers between devices: 5.9 us -> 5.17 us
    ppermute x1 -> x2, waiting for transfers between devices: 0.79 us -> 2.77 us  [column_exchange(): got.append(lax.ppermute(send, ('section', 'row', 'col'), pairs))]
    ppermute x2 -> x3, waiting for transfers between devices: 1.68 us -> 0.01 us  [exchange(): lax.ppermute(s, axis, pairs)]
    ppermute x2, waiting for transfers between devices: 3.43 us -> 2.39 us  [per_device(): lax.ppermute(ends.pop(0) if take < frames else latent, 'section', ring)]
    pallas_call x10 -> x14, Pallas kernels: 10.1 us -> 10.2 us  [call(): pl.pallas_call(body, out_shape=outs, in_specs=[spec] * len(args), out_spe...]
    ppermute x1 -> x2, starting transfers between devices: 1.82 us -> 1.82 us  [column_exchange(): got.append(lax.ppermute(send, ('section', 'row', 'col'), pairs))]
  transfers between devices with their start and end apart: 5 -> 7, of which waited for: 4 -> 3; matrix products, arithmetic and copies ran while one was open for 0% -> 0% of each run, Pallas kernels for 18% -> 22%
where the time goes in v9:
time: 22.3 us; the launch traced here: 22.2 us
  Pallas kernels  10.2 us (46%)
  starting transfers between devices  6.7 us (30%)
  waiting for transfers between devices  5.17 us (23%)
    pallas_call x14, Pallas kernels, call(): pl.pallas_call(body, out_shape=outs, in_specs=[spec] * len(args), out_spe...  10.2 us
    ppermute x2, starting transfers between devices, per_device(): lax.ppermute(ends.pop(0) if take < frames else latent, 'section', ring)  4.61 us
    ppermute x2, waiting for transfers between devices, column_exchange(): got.append(lax.ppermute(send, ('section', 'row', 'col'), pairs))  2.77 us
    ppermute x2, waiting for transfers between devices, per_device(): lax.ppermute(ends.pop(0) if take < frames else latent, 'section', ring)  2.39 us
    ppermute x2, starting transfers between devices, column_exchange(): got.append(lax.ppermute(send, ('section', 'row', 'col'), pairs))  1.82 us
  transfers between devices with their start and end apart: 7, of which 3 were waited for; matrix products, arithmetic and copies ran while one was open for 0% of the time, Pallas kernels for 22%

profile of v9, /device:TPU:0, one launch (start us, length us, event | category | flops | bytes accessed | tf_op | source)
XLA Modules:
  0.0 22.2 jit_solution(2871451523026861310)
XLA Ops:
  0.0 0.0 copy-start.1
  0.0 0.0 copy-start.3
  0.0 0.0 copy-start.2
  0.0 3.0 %collective-permute-start.2 = (bf16[4,4,16,256]{3,2,1,0:T(8,128)(2,1)}, bf16[4,4,16,256]{3,2,1,0:T(8,128)(2,1)S(1)}, u32[]{:S(2)}, u32[]{:S(2)}) collective-permute-start(bf16[4,4,16,256]{3,2,1,0:T(8,128)(2,1)} %refs_2_.5), channel_id=1, source_target_pairs={{0,8},{8,16},{16,24},{24,0},{1,9},{9,17},{17,25},{25,1},{2,10},{10... | collective-permute-start | bytes 393224 | tf_op jit(solution)/shard_map/ppermute | solution.py:384
  3.0 0.0 copy-done.1
  3.0 0.1 collective-permute-start
  3.1 0.0 copy-start
  3.1 1.6 %collective-permute-start.1 = (bf16[2,4,16,256]{3,2,1,0:T(8,128)(2,1)S(1)}, bf16[2,4,16,256]{3,2,1,0:T(8,128)(2,1)S(1)}, u32[]{:S(2)}, u32[]{:S(2)}) collective-permute-start(bf16[2,4,16,256]{3,2,1,0:T(8,128)(2,1)S(1)} %shard_map.50), channel_id=1, source_target_pairs={{0,16},{8,24},{16,0},{24,8},{1,17},{9,25},{17,1},{25,9},{2,18},{10... | collective-permute-start | bytes 196616 | tf_op jit(solution)/shard_map/ppermute | solution.py:384
  4.7 0.0 copy-done.3
  4.7 0.0 copy-done.2
  4.7 1.0 %shard_map.48 = (bf16[3,2,2,256,512]{4,3,2,1,0:T(8,128)(2,1)S(1)}, bf16[3,3,2,256,256]{4,3,2,1,0:T(8,128)(2,1)S(1)}, f32[8,128]{1,0:T(8,128)S(1)}) custom-call(bf16[3,3,3,256,128]{4,3,2,1,0:T(8,128)(2,1)S(1)} %copy-done.2, bf16[3,3,3,128,128]{4,3,2,1,0:T(8,128)(2,1)S(1)} %copy-done.3), custom_call_target="tpu_custom_call" | custom-call | flops 4000000000 | bytes 8163328 | tf_op jit(solution)/shard_map/pallas_call | solution.py:20
  5.8 0.0 collective-permute-done.refs_1_.refs_3_
  5.8 0.0 copy-done
  5.8 0.9 %shard_map.49.refs_0_.refs_2_ = f32[2,6,16,256]{3,2,1,0:T(8,128)S(1)} custom-call(bf16[4,4,16,256]{3,2,1,0:T(8,128)(2,1)S(1)} %copy-done.1, bf16[4,2,16,256]{3,2,1,0:T(8,128)(2,1)S(1)} %collective-permute-done.refs_1_.refs_3_, bf16[3,3,3,256,256]{4,3,2,1,0:T(8,128)(2,1)S(1)} %copy-done, f32[8,128]{1,0:T(8,128)S(1)} %get-tuple-element.17.refs_3_), custom_call_target="tpu_custom_call" | custom-call | flops 679477248 | bytes 3936256 | tf_op jit(solution)/shard_map/pallas_call | solution.py:20
  6.7 2.4 %collective-permute-done.1.refs_1_ = bf16[2,4,16,256]{3,2,1,0:T(8,128)(2,1)S(1)} collective-permute-done((bf16[2,4,16,256]{3,2,1,0:T(8,128)(2,1)S(1)}, bf16[2,4,16,256]{3,2,1,0:T(8,128)(2,1)S(1)}, u32[]{:S(2)}, u32[]{:S(2)}) %collective-permute-start.1) | collective-permute-done | bytes 65568 | tf_op jit(solution)/shard_map/ppermute | solution.py:384
  9.1 0.0 collective-permute-done.2.refs_2_
  9.1 0.1 collective-permute-start.3
  9.3 0.2 shard_map.52
  9.5 1.8 %collective-permute-start.4 = (bf16[2,40,256]{2,1,0:T(8,128)(2,1)S(1)}, bf16[2,40,256]{2,1,0:T(8,128)(2,1)S(1)}, u32[]{:S(2)}, u32[]{:S(2)}) collective-permute-start(bf16[2,40,256]{2,1,0:T(8,128)(2,1)S(1)} %get-tuple-element.20.refs_5_), channel_id=1, source_target_pairs={{0,1},{2,3},{1,0},{3,2},{4,5},{6,7},{5,4},{7,6},{8,9},{10,11},{9,8... | collective-permute-start | bytes 122888 | tf_op jit(solution)/shard_map/ppermute | solution.py:71
  11.3 0.0 collective-permute-start.5
  11.3 0.0 collective-permute-done.3.refs_1_.refs_0_
  11.3 1.2 %shard_map.53.refs_2_.refs_0_ = f32[3,6,16,256]{3,2,1,0:T(8,128)S(1)} custom-call(bf16[6,4,16,256]{3,2,1,0:T(8,128)(2,1)S(1)} %get-tuple-element.18.before.refs_0_, bf16[6,2,16,256]{3,2,1,0:T(8,128)(2,1)S(1)} %collective-permute-done.3.refs_1_.refs_0_, bf16[4,4,16,256]{3,2,1,0:T(8,128)(2,1)S(1)} %copy-done.1, ...), custom_call_target="tpu_custom_call" | custom-call | flops 1019215872 | bytes 4407296 | tf_op jit(solution)/shard_map/pallas_call | solution.py:20
  12.5 1.0 %collective-permute-done.4.refs_0_ = bf16[2,40,256]{2,1,0:T(8,128)(2,1)S(1)} collective-permute-done((bf16[2,40,256]{2,1,0:T(8,128)(2,1)S(1)}, bf16[2,40,256]{2,1,0:T(8,128)(2,1)S(1)}, u32[]{:S(2)}, u32[]{:S(2)}) %collective-permute-start.4) | collective-permute-done | bytes 40992 | tf_op jit(solution)/shard_map/ppermute | solution.py:71
  13.5 1.8 %collective-permute-done.5.refs_1_ = bf16[2,40,256]{2,1,0:T(8,128)(2,1)S(1)} collective-permute-done((bf16[2,40,256]{2,1,0:T(8,128)(2,1)S(1)}, bf16[2,40,256]{2,1,0:T(8,128)(2,1)S(1)}, u32[]{:S(2)}, u32[]{:S(2)}) %collective-permute-start.5) | collective-permute-done | bytes 40992 | tf_op jit(solution)/shard_map/ppermute | solution.py:71
  15.3 0.1 collective-permute-start.6
  15.4 1.2 %shard_map.55.refs_1_ = f32[3,6,16,256]{3,2,1,0:T(8,128)S(1)} custom-call(bf16[6,4,16,256]{3,2,1,0:T(8,128)(2,1)S(1)} %get-tuple-element.18.before.refs_0_, bf16[6,2,16,256]{3,2,1,0:T(8,128)(2,1)S(1)} %collective-permute-done.3.refs_1_.refs_0_, bf16[4,4,16,256]{3,2,1,0:T(8,128)(2,1)S(1)} %copy-done.1, ...), custom_call_target="tpu_custom_call" | custom-call | flops 1019215872 | bytes 4407296 | tf_op jit(solution)/shard_map/pallas_call | solution.py:20
  16.6 0.2 shard_map.56.refs_4_
  16.8 0.0 collective-permute-done.6.refs_6_
  16.8 1.1 %shard_map.57 = (bf16[2,6,8,16,256]{4,3,2,1,0:T(8,128)(2,1)S(1)}, f32[2,56,256]{2,1,0:T(8,128)S(1)}) custom-call(f32[3,6,16,256]{3,2,1,0:T(8,128)S(1)} %shard_map.53.refs_2_.refs_0_, f32[3,6,16,256]{3,2,1,0:T(8,128)S(1)} %shard_map.55.refs_1_, f32[2,6,16,256]{3,2,1,0:T(8,128)S(1)} %shard_map.49.refs_0_.refs_2_, ...), custom_call_target="tpu_custom_call" | custom-call | flops 1000000000 | bytes 5513216 | tf_op jit(solution)/shard_map/pallas_call | solution.py:20
  17.9 1.9 %shard_map.58.fine = bf16[2,10,6,16,256]{4,3,2,1,0:T(8,128)(2,1)S(1)} custom-call(bf16[2,6,8,16,256]{4,3,2,1,0:T(8,128)(2,1)S(1)} %get-tuple-element.25.near, f32[2,56,256]{2,1,0:T(8,128)S(1)} %get-tuple-element.26.far, bf16[3,2,2,256,512]{4,3,2,1,0:T(8,128)(2,1)S(1)} %get-tuple-element.27.summed), custom_call_target="tpu_custom_call" | custom-call | flops 2000000000 | bytes 5029888 | tf_op jit(solution)/shard_map/pallas_call | solution.py:20
  19.9 2.3 %shard_map.59 = bf16[4,8,32,128]{3,2,1,0:T(8,128)(2,1)} custom-call(bf16[2,10,6,16,256]{4,3,2,1,0:T(8,128)(2,1)S(1)} %shard_map.58.fine, bf16[3,3,2,256,256]{4,3,2,1,0:T(8,128)(2,1)S(1)} %get-tuple-element.28.paired), custom_call_target="tpu_custom_call" | custom-call | flops 1000000000 | bytes 3604480 | tf_op jit(solution)/shard_map/pallas_call | solution.py:20
  (5 shorter events, 0.1 us)
Async XLA Ops:
  0.0 3.0 %copy-start.1 = (bf16[4,4,16,256]{3,2,1,0:T(8,128)(2,1)S(1)}, bf16[4,4,16,256]{3,2,1,0:T(8,128)(2,1)}, u32[]{:S(2)}) copy-start(bf16[4,4,16,256]{3,2,1,0:T(8,128)(2,1)} %refs_2_.5) | copy-start | bytes 393220
  0.0 4.7 %copy-start.3 = (bf16[3,3,3,128,128]{4,3,2,1,0:T(8,128)(2,1)S(1)}, bf16[3,3,3,128,128]{4,3,2,1,0:T(8,128)(2,1)}, u32[]{:S(2)}) copy-start(bf16[3,3,3,128,128]{4,3,2,1,0:T(8,128)(2,1)} %third.1) | copy-start | bytes 2654212
  0.0 4.7 %copy-start.2 = (bf16[3,3,3,256,128]{4,3,2,1,0:T(8,128)(2,1)S(1)}, bf16[3,3,3,256,128]{4,3,2,1,0:T(8,128)(2,1)}, u32[]{:S(2)}) copy-start(bf16[3,3,3,256,128]{4,3,2,1,0:T(8,128)(2,1)} %second.1) | copy-start | bytes 5308420
  0.0 9.1 %collective-permute-start.2 = (bf16[4,4,16,256]{3,2,1,0:T(8,128)(2,1)}, bf16[4,4,16,256]{3,2,1,0:T(8,128)(2,1)S(1)}, u32[]{:S(2)}, u32[]{:S(2)}) collective-permute-start(bf16[4,4,16,256]{3,2,1,0:T(8,128)(2,1)} %refs_2_.5), channel_id=1, source_target_pairs={{0,8},{8,16},{16,24},{24,0},{1,9},{9,17},{17,25},{25,1},{2,10},{10... | collective-permute-start | bytes 393224 | tf_op jit(solution)/shard_map/ppermute | solution.py:384
  3.0 2.8 %collective-permute-start = (bf16[4,2,16,256]{3,2,1,0:T(8,128)(2,1)S(1)}, bf16[4,2,16,256]{3,2,1,0:T(8,128)(2,1)S(1)}, u32[]{:S(2)}, u32[]{:S(2)}) collective-permute-start(bf16[4,2,16,256]{3,2,1,0:T(8,128)(2,1)S(1)} %shard_map.47), channel_id=1, source_target_pairs={{0,4},{4,0},{1,5},{5,1},{2,6},{6,2},{3,7},{7,3},{8,12},{12,8},{9,1... | collective-permute-start | bytes 196616 | tf_op jit(solution)/shard_map/ppermute | solution.py:57
  3.1 2.7 %copy-start = (bf16[3,3,3,256,256]{4,3,2,1,0:T(8,128)(2,1)S(1)}, bf16[3,3,3,256,256]{4,3,2,1,0:T(8,128)(2,1)}, u32[]{:S(2)}) copy-start(bf16[3,3,3,256,256]{4,3,2,1,0:T(8,128)(2,1)} %refs_7_.1) | copy-start | bytes 10616836
  3.1 6.0 %collective-permute-start.1 = (bf16[2,4,16,256]{3,2,1,0:T(8,128)(2,1)S(1)}, bf16[2,4,16,256]{3,2,1,0:T(8,128)(2,1)S(1)}, u32[]{:S(2)}, u32[]{:S(2)}) collective-permute-start(bf16[2,4,16,256]{3,2,1,0:T(8,128)(2,1)S(1)} %shard_map.50), channel_id=1, source_target_pairs={{0,16},{8,24},{16,0},{24,8},{1,17},{9,25},{17,1},{25,9},{2,18},{10... | collective-permute-start | bytes 196616 | tf_op jit(solution)/shard_map/ppermute | solution.py:384
  9.1 2.1 %collective-permute-start.3 = (bf16[6,2,16,256]{3,2,1,0:T(8,128)(2,1)S(1)}, bf16[6,2,16,256]{3,2,1,0:T(8,128)(2,1)S(1)}, u32[]{:S(2)}, u32[]{:S(2)}) collective-permute-start(bf16[6,2,16,256]{3,2,1,0:T(8,128)(2,1)S(1)} %get-tuple-element.19), channel_id=1, source_target_pairs={{0,4},{4,0},{1,5},{5,1},{2,6},{6,2},{3,7},{7,3},{8,12},{12,8},{9,1... | collective-permute-start | bytes 294920 | tf_op jit(solution)/shard_map/ppermute | solution.py:57
  9.5 4.1 %collective-permute-start.4 = (bf16[2,40,256]{2,1,0:T(8,128)(2,1)S(1)}, bf16[2,40,256]{2,1,0:T(8,128)(2,1)S(1)}, u32[]{:S(2)}, u32[]{:S(2)}) collective-permute-start(bf16[2,40,256]{2,1,0:T(8,128)(2,1)S(1)} %get-tuple-element.20.refs_5_), channel_id=1, source_target_pairs={{0,1},{2,3},{1,0},{3,2},{4,5},{6,7},{5,4},{7,6},{8,9},{10,11},{9,8... | collective-permute-start | bytes 122888 | tf_op jit(solution)/shard_map/ppermute | solution.py:71
  11.3 4.0 %collective-permute-start.5 = (bf16[2,40,256]{2,1,0:T(8,128)(2,1)S(1)}, bf16[2,40,256]{2,1,0:T(8,128)(2,1)S(1)}, u32[]{:S(2)}, u32[]{:S(2)}) collective-permute-start(bf16[2,40,256]{2,1,0:T(8,128)(2,1)S(1)} %get-tuple-element.21.refs_6_), channel_id=1, source_target_pairs={{1,2},{3,11},{2,1},{0,8},{5,6},{7,15},{6,5},{4,12},{9,10},{11,3},{... | collective-permute-start | bytes 122888 | tf_op jit(solution)/shard_map/ppermute | solution.py:71
  15.3 1.5 %collective-permute-start.6 = (bf16[4,20,256]{2,1,0:T(8,128)(2,1)S(1)}, bf16[4,20,256]{2,1,0:T(8,128)(2,1)S(1)}, u32[]{:S(2)}, u32[]{:S(2)}) collective-permute-start(bf16[4,20,256]{2,1,0:T(8,128)(2,1)S(1)} %get-tuple-element.24), channel_id=1, source_target_pairs={{0,4},{4,0},{1,5},{5,1},{2,6},{6,2},{3,7},{7,3},{8,12},{12,8},{9,1... | collective-permute-start | bytes 122888 | tf_op jit(solution)/shard_map/ppermute | solution.py:57

commit v10 on v9

--- a/solution.py
+++ b/solution.py
@@ -13,14 +13,13 @@
 RIM = 2
 
 
-def call(body, outs, args, scratch=(), flops=0, to=pltpu.VMEM):
+def call(body, outs, args, scratch=(), flops=0):
     spec = pl.BlockSpec(memory_space=pltpu.VMEM)
     outs = [jax.ShapeDtypeStruct(shape, kind) for shape, kind in outs]
     size = sum(a.size * a.dtype.itemsize for a in [*args, *outs])
     return pl.pallas_call(
-        body, out_shape=outs, in_specs=[spec] * len(args),
-        out_specs=[pl.BlockSpec(memory_space=to)] * len(outs),
-        scratch_shapes=[pltpu.VMEM(*s) if isinstance(s, tuple) else s for s in scratch],
+        body, out_shape=outs, in_specs=[spec] * len(args), out_specs=[spec] * len(outs),
+        scratch_shapes=[pltpu.VMEM(*s) for s in scratch],
         cost_estimate=pl.CostEstimate(flops=flops, bytes_accessed=size, transcendentals=0),
         compiler_params=pltpu.CompilerParams(vmem_limit_bytes=32 << 20),
     )(*args)
@@ -328,37 +327,25 @@
                     fine[dj, 2 * i + py, t] = jnp.where(gone, 0.0, value).astype(BF)
 
 
-def third_conv(fine, paired, out, spread, ready, sems):
+def third_conv(fine, paired, out, spread):
     _, high, later, breadth, half = fine.shape
     high, kept, wide = high - 2, later - 2, out.shape[-1]
-    steps = sems.shape[0]
-    count = kept // steps
-
-    def leave(step):
-        mine = pl.ds(step * count, count)
-        return pltpu.make_async_copy(ready.at[mine], out.at[mine], sems.at[step])
-
-    @pl.loop(0, steps)
-    def _(step):
-        begin = step * count
+    kernel = paired[...].reshape(-1, paired.shape[-1])
+    step = high // 2
+    for begin in range(0, high, step):
         taps = [
-            fine[dj, b : b + high, pl.ds(begin + a, count)].reshape(-1, half)
+            fine[dj, begin + b : begin + b + step, a : a + kept].reshape(-1, half)
             for a in range(3) for b in range(3) for dj in range(2)
         ]
-        kernel = paired[...].reshape(-1, paired.shape[-1])
         found = jnp.dot(jnp.concatenate(taps, 1), kernel, preferred_element_type=F32)
-        for y in range(high):
-            for t in range(count):
-                at = (y * count + t) * breadth
+        for y in range(step):
+            for t in range(kept):
+                at = (y * kept + t) * breadth
                 for q in range(2):
-                    spread[t, y, pl.ds(q, breadth, stride=2), :] = found[
+                    spread[t, begin + y, pl.ds(q, breadth, stride=2), :] = found[
                         at : at + breadth, q * wide : (q + 1) * wide
                     ]
-        ready[pl.ds(begin, count)] = spread[...].astype(BF)
-        leave(step).start()
-
-    for step in range(steps):
-        leave(step).wait()
+    out[...] = spread[...].astype(BF)
 
 
 def per_device(latent, w_first, w_second, w_third):
@@ -421,16 +408,16 @@
     rest = early - (frames - 2)
     cut = rest // 2
     first_part = inner(fields, 0, cut, *sends)
+    (rim,) = call(
+        functools.partial(rim_columns, rows=rounds), [strip], [*early_got, *own_got, *first_part],
+        scratch,
+    )
     side, *sends = call(
         functools.partial(turn_columns, cols=cols, frames=total),
-        [strip] + [((2 * RIM, RIM * total, width), BF)] * rounds, [*came, *first_part],
+        [strip] + [((2 * RIM, RIM * total, width), BF)] * rounds, [*came, rim],
         [((height * total, width), F32)],
     )
     turned = exchange(sends, "row")
-    (rim,) = call(
-        functools.partial(rim_columns, rows=rounds), [strip], [*early_got, *own_got, side],
-        scratch,
-    )
     inners = first_part + inner(fields, cut, rest - cut, side) + inners
     size = (tall - 2) * early
     near, far = call(
@@ -449,14 +436,9 @@
         [(blocked(corners * early * (breadth + SLACK), 4 * fine), F32)],
         flops=2 * 10**9,
     )
-    steps = 2 if frames % 2 == 0 else 1
     (out,) = call(
         third_conv, [((frames, 2 * height, 2 * breadth, last), BF)], [second, paired],
-        [
-            ((frames // steps, 2 * height, 2 * breadth, last), F32),
-            ((frames, 2 * height, 2 * breadth, last), BF), pltpu.SemaphoreType.DMA((steps,)),
-        ],
-        flops=10**9, to=pl.ANY,
+        [((frames, 2 * height, 2 * breadth, last), F32)], flops=10**9,
     )
     return out
 

time: 22.3 us -> 21.9 us (0.982)
  no operation moved by 1% of the time
where the time goes in v10:
time: 21.9 us; the launch traced here: 21.8 us
  Pallas kernels  9.98 us (46%)
  starting transfers between devices  6.7 us (31%)
  waiting for transfers between devices  4.97 us (23%)
    pallas_call x14, Pallas kernels, call(): pl.pallas_call(body, out_shape=outs, in_specs=[spec] * len(args), out_spe...  9.98 us
    ppermute x2, starting transfers between devices, per_device(): lax.ppermute(ends.pop(0) if take < frames else latent, 'section', ring)  4.61 us
    ppermute x2, waiting for transfers between devices, column_exchange(): got.append(lax.ppermute(send, ('section', 'row', 'col'), pairs))  2.57 us
    ppermute x2, waiting for transfers between devices, per_device(): lax.ppermute(ends.pop(0) if take < frames else latent, 'section', ring)  2.39 us
    ppermute x2, starting transfers between devices, column_exchange(): got.append(lax.ppermute(send, ('section', 'row', 'col'), pairs))  1.82 us
  transfers between devices with their start and end apart: 7, of which 3 were waited for; matrix products, arithmetic and copies ran while one was open for 0% of the time, Pallas kernels for 22%

profile of v10, /device:TPU:0, one launch (start us, length us, event | category | flops | bytes accessed | tf_op | source)
XLA Modules:
  0.0 21.8 jit_solution(5386775767196948209)
XLA Ops:
  0.0 0.0 copy-start.1
  0.0 0.0 copy-start.3
  0.0 0.0 copy-start.2
  0.0 3.0 %collective-permute-start.2 = (bf16[4,4,16,256]{3,2,1,0:T(8,128)(2,1)}, bf16[4,4,16,256]{3,2,1,0:T(8,128)(2,1)S(1)}, u32[]{:S(2)}, u32[]{:S(2)}) collective-permute-start(bf16[4,4,16,256]{3,2,1,0:T(8,128)(2,1)} %refs_2_.5), channel_id=1, source_target_pairs={{0,8},{8,16},{16,24},{24,0},{1,9},{9,17},{17,25},{25,1},{2,10},{10... | collective-permute-start | bytes 393224 | tf_op jit(solution)/shard_map/ppermute | solution.py:371
  3.0 0.0 copy-done.1
  3.0 0.1 collective-permute-start
  3.1 0.0 copy-start
  3.1 1.6 %collective-permute-start.1 = (bf16[2,4,16,256]{3,2,1,0:T(8,128)(2,1)S(1)}, bf16[2,4,16,256]{3,2,1,0:T(8,128)(2,1)S(1)}, u32[]{:S(2)}, u32[]{:S(2)}) collective-permute-start(bf16[2,4,16,256]{3,2,1,0:T(8,128)(2,1)S(1)} %shard_map.50), channel_id=1, source_target_pairs={{0,16},{8,24},{16,0},{24,8},{1,17},{9,25},{17,1},{25,9},{2,18},{10... | collective-permute-start | bytes 196616 | tf_op jit(solution)/shard_map/ppermute | solution.py:371
  4.7 0.0 copy-done.3
  4.7 0.0 copy-done.2
  4.7 1.0 %shard_map.48 = (bf16[3,2,2,256,512]{4,3,2,1,0:T(8,128)(2,1)S(1)}, bf16[3,3,2,256,256]{4,3,2,1,0:T(8,128)(2,1)S(1)}, f32[8,128]{1,0:T(8,128)S(1)}) custom-call(bf16[3,3,3,256,128]{4,3,2,1,0:T(8,128)(2,1)S(1)} %copy-done.2, bf16[3,3,3,128,128]{4,3,2,1,0:T(8,128)(2,1)S(1)} %copy-done.3), custom_call_target="tpu_custom_call" | custom-call | flops 4000000000 | bytes 8163328 | tf_op jit(solution)/shard_map/pallas_call | solution.py:20
  5.8 0.0 collective-permute-done.refs_1_.refs_3_
  5.8 0.0 copy-done
  5.8 0.9 %shard_map.49.refs_0_.refs_2_ = f32[2,6,16,256]{3,2,1,0:T(8,128)S(1)} custom-call(bf16[4,4,16,256]{3,2,1,0:T(8,128)(2,1)S(1)} %copy-done.1, bf16[4,2,16,256]{3,2,1,0:T(8,128)(2,1)S(1)} %collective-permute-done.refs_1_.refs_3_, bf16[3,3,3,256,256]{4,3,2,1,0:T(8,128)(2,1)S(1)} %copy-done, f32[8,128]{1,0:T(8,128)S(1)} %get-tuple-element.17.refs_3_), custom_call_target="tpu_custom_call" | custom-call | flops 679477248 | bytes 3936256 | tf_op jit(solution)/shard_map/pallas_call | solution.py:20
  6.7 2.4 %collective-permute-done.1.refs_1_ = bf16[2,4,16,256]{3,2,1,0:T(8,128)(2,1)S(1)} collective-permute-done((bf16[2,4,16,256]{3,2,1,0:T(8,128)(2,1)S(1)}, bf16[2,4,16,256]{3,2,1,0:T(8,128)(2,1)S(1)}, u32[]{:S(2)}, u32[]{:S(2)}) %collective-permute-start.1) | collective-permute-done | bytes 65568 | tf_op jit(solution)/shard_map/ppermute | solution.py:371
  9.1 0.0 collective-permute-done.2.refs_2_
  9.1 0.1 collective-permute-start.3
  9.3 0.2 shard_map.52
  9.5 1.8 %collective-permute-start.4 = (bf16[2,40,256]{2,1,0:T(8,128)(2,1)S(1)}, bf16[2,40,256]{2,1,0:T(8,128)(2,1)S(1)}, u32[]{:S(2)}, u32[]{:S(2)}) collective-permute-start(bf16[2,40,256]{2,1,0:T(8,128)(2,1)S(1)} %get-tuple-element.20.refs_5_), channel_id=1, source_target_pairs={{0,1},{2,3},{1,0},{3,2},{4,5},{6,7},{5,4},{7,6},{8,9},{10,11},{9,8... | collective-permute-start | bytes 122888 | tf_op jit(solution)/shard_map/ppermute | solution.py:70
  11.3 0.0 collective-permute-start.5
  11.3 0.0 collective-permute-done.3.refs_1_.refs_0_
  11.3 1.2 %shard_map.53.refs_2_.refs_0_ = f32[3,6,16,256]{3,2,1,0:T(8,128)S(1)} custom-call(bf16[6,4,16,256]{3,2,1,0:T(8,128)(2,1)S(1)} %get-tuple-element.18.before.refs_0_, bf16[6,2,16,256]{3,2,1,0:T(8,128)(2,1)S(1)} %collective-permute-done.3.refs_1_.refs_0_, bf16[4,4,16,256]{3,2,1,0:T(8,128)(2,1)S(1)} %copy-done.1, ...), custom_call_target="tpu_custom_call" | custom-call | flops 1019215872 | bytes 4407296 | tf_op jit(solution)/shard_map/pallas_call | solution.py:20
  12.5 0.2 shard_map.54.refs_2_.refs_4_
  12.7 0.8 %collective-permute-done.4.refs_0_ = bf16[2,40,256]{2,1,0:T(8,128)(2,1)S(1)} collective-permute-done((bf16[2,40,256]{2,1,0:T(8,128)(2,1)S(1)}, bf16[2,40,256]{2,1,0:T(8,128)(2,1)S(1)}, u32[]{:S(2)}, u32[]{:S(2)}) %collective-permute-start.4) | collective-permute-done | bytes 40992 | tf_op jit(solution)/shard_map/ppermute | solution.py:70
  13.5 1.8 %collective-permute-done.5.refs_1_ = bf16[2,40,256]{2,1,0:T(8,128)(2,1)S(1)} collective-permute-done((bf16[2,40,256]{2,1,0:T(8,128)(2,1)S(1)}, bf16[2,40,256]{2,1,0:T(8,128)(2,1)S(1)}, u32[]{:S(2)}, u32[]{:S(2)}) %collective-permute-start.5) | collective-permute-done | bytes 40992 | tf_op jit(solution)/shard_map/ppermute | solution.py:70
  15.3 0.1 collective-permute-start.6
  15.4 1.2 %shard_map.56.refs_1_ = f32[3,6,16,256]{3,2,1,0:T(8,128)S(1)} custom-call(bf16[6,4,16,256]{3,2,1,0:T(8,128)(2,1)S(1)} %get-tuple-element.18.before.refs_0_, bf16[6,2,16,256]{3,2,1,0:T(8,128)(2,1)S(1)} %collective-permute-done.3.refs_1_.refs_0_, bf16[4,4,16,256]{3,2,1,0:T(8,128)(2,1)S(1)} %copy-done.1, ...), custom_call_target="tpu_custom_call" | custom-call | flops 1019215872 | bytes 4407296 | tf_op jit(solution)/shard_map/pallas_call | solution.py:20
  16.6 0.0 collective-permute-done.6.refs_6_
  16.6 1.1 %shard_map.57 = (bf16[2,6,8,16,256]{4,3,2,1,0:T(8,128)(2,1)S(1)}, f32[2,56,256]{2,1,0:T(8,128)S(1)}) custom-call(f32[3,6,16,256]{3,2,1,0:T(8,128)S(1)} %shard_map.53.refs_2_.refs_0_, f32[3,6,16,256]{3,2,1,0:T(8,128)S(1)} %shard_map.56.refs_1_, f32[2,6,16,256]{3,2,1,0:T(8,128)S(1)} %shard_map.49.refs_0_.refs_2_, ...), custom_call_target="tpu_custom_call" | custom-call | flops 1000000000 | bytes 5513216 | tf_op jit(solution)/shard_map/pallas_call | solution.py:20
  17.7 1.9 %shard_map.58.fine = bf16[2,10,6,16,256]{4,3,2,1,0:T(8,128)(2,1)S(1)} custom-call(bf16[2,6,8,16,256]{4,3,2,1,0:T(8,128)(2,1)S(1)} %get-tuple-element.25.near, f32[2,56,256]{2,1,0:T(8,128)S(1)} %get-tuple-element.26.far, bf16[3,2,2,256,512]{4,3,2,1,0:T(8,128)(2,1)S(1)} %get-tuple-element.27.summed), custom_call_target="tpu_custom_call" | custom-call | flops 2000000000 | bytes 5029888 | tf_op jit(solution)/shard_map/pallas_call | solution.py:20
  19.7 2.1 %shard_map.59 = bf16[4,8,32,128]{3,2,1,0:T(8,128)(2,1)} custom-call(bf16[2,10,6,16,256]{4,3,2,1,0:T(8,128)(2,1)S(1)} %shard_map.58.fine, bf16[3,3,2,256,256]{4,3,2,1,0:T(8,128)(2,1)S(1)} %get-tuple-element.28.paired), custom_call_target="tpu_custom_call" | custom-call | flops 1000000000 | bytes 3604480 | tf_op jit(solution)/shard_map/pallas_call | solution.py:20
  (5 shorter events, 0.1 us)
Async XLA Ops:
  0.0 3.0 %copy-start.1 = (bf16[4,4,16,256]{3,2,1,0:T(8,128)(2,1)S(1)}, bf16[4,4,16,256]{3,2,1,0:T(8,128)(2,1)}, u32[]{:S(2)}) copy-start(bf16[4,4,16,256]{3,2,1,0:T(8,128)(2,1)} %refs_2_.5) | copy-start | bytes 393220
  0.0 4.7 %copy-start.3 = (bf16[3,3,3,128,128]{4,3,2,1,0:T(8,128)(2,1)S(1)}, bf16[3,3,3,128,128]{4,3,2,1,0:T(8,128)(2,1)}, u32[]{:S(2)}) copy-start(bf16[3,3,3,128,128]{4,3,2,1,0:T(8,128)(2,1)} %third.1) | copy-start | bytes 2654212
  0.0 4.7 %copy-start.2 = (bf16[3,3,3,256,128]{4,3,2,1,0:T(8,128)(2,1)S(1)}, bf16[3,3,3,256,128]{4,3,2,1,0:T(8,128)(2,1)}, u32[]{:S(2)}) copy-start(bf16[3,3,3,256,128]{4,3,2,1,0:T(8,128)(2,1)} %second.1) | copy-start | bytes 5308420
  0.0 9.1 %collective-permute-start.2 = (bf16[4,4,16,256]{3,2,1,0:T(8,128)(2,1)}, bf16[4,4,16,256]{3,2,1,0:T(8,128)(2,1)S(1)}, u32[]{:S(2)}, u32[]{:S(2)}) collective-permute-start(bf16[4,4,16,256]{3,2,1,0:T(8,128)(2,1)} %refs_2_.5), channel_id=1, source_target_pairs={{0,8},{8,16},{16,24},{24,0},{1,9},{9,17},{17,25},{25,1},{2,10},{10... | collective-permute-start | bytes 393224 | tf_op jit(solution)/shard_map/ppermute | solution.py:371
  3.0 2.8 %collective-permute-start = (bf16[4,2,16,256]{3,2,1,0:T(8,128)(2,1)S(1)}, bf16[4,2,16,256]{3,2,1,0:T(8,128)(2,1)S(1)}, u32[]{:S(2)}, u32[]{:S(2)}) collective-permute-start(bf16[4,2,16,256]{3,2,1,0:T(8,128)(2,1)S(1)} %shard_map.47), channel_id=1, source_target_pairs={{0,4},{4,0},{1,5},{5,1},{2,6},{6,2},{3,7},{7,3},{8,12},{12,8},{9,1... | collective-permute-start | bytes 196616 | tf_op jit(solution)/shard_map/ppermute | solution.py:56
  3.1 2.7 %copy-start = (bf16[3,3,3,256,256]{4,3,2,1,0:T(8,128)(2,1)S(1)}, bf16[3,3,3,256,256]{4,3,2,1,0:T(8,128)(2,1)}, u32[]{:S(2)}) copy-start(bf16[3,3,3,256,256]{4,3,2,1,0:T(8,128)(2,1)} %refs_7_.1) | copy-start | bytes 10616836
  3.1 6.0 %collective-permute-start.1 = (bf16[2,4,16,256]{3,2,1,0:T(8,128)(2,1)S(1)}, bf16[2,4,16,256]{3,2,1,0:T(8,128)(2,1)S(1)}, u32[]{:S(2)}, u32[]{:S(2)}) collective-permute-start(bf16[2,4,16,256]{3,2,1,0:T(8,128)(2,1)S(1)} %shard_map.50), channel_id=1, source_target_pairs={{0,16},{8,24},{16,0},{24,8},{1,17},{9,25},{17,1},{25,9},{2,18},{10... | collective-permute-start | bytes 196616 | tf_op jit(solution)/shard_map/ppermute | solution.py:371
  9.1 2.1 %collective-permute-start.3 = (bf16[6,2,16,256]{3,2,1,0:T(8,128)(2,1)S(1)}, bf16[6,2,16,256]{3,2,1,0:T(8,128)(2,1)S(1)}, u32[]{:S(2)}, u32[]{:S(2)}) collective-permute-start(bf16[6,2,16,256]{3,2,1,0:T(8,128)(2,1)S(1)} %get-tuple-element.19), channel_id=1, source_target_pairs={{0,4},{4,0},{1,5},{5,1},{2,6},{6,2},{3,7},{7,3},{8,12},{12,8},{9,1... | collective-permute-start | bytes 294920 | tf_op jit(solution)/shard_map/ppermute | solution.py:56
  9.5 4.1 %collective-permute-start.4 = (bf16[2,40,256]{2,1,0:T(8,128)(2,1)S(1)}, bf16[2,40,256]{2,1,0:T(8,128)(2,1)S(1)}, u32[]{:S(2)}, u32[]{:S(2)}) collective-permute-start(bf16[2,40,256]{2,1,0:T(8,128)(2,1)S(1)} %get-tuple-element.20.refs_5_), channel_id=1, source_target_pairs={{0,1},{2,3},{1,0},{3,2},{4,5},{6,7},{5,4},{7,6},{8,9},{10,11},{9,8... | collective-permute-start | bytes 122888 | tf_op jit(solution)/shard_map/ppermute | solution.py:70
  11.3 4.0 %collective-permute-start.5 = (bf16[2,40,256]{2,1,0:T(8,128)(2,1)S(1)}, bf16[2,40,256]{2,1,0:T(8,128)(2,1)S(1)}, u32[]{:S(2)}, u32[]{:S(2)}) collective-permute-start(bf16[2,40,256]{2,1,0:T(8,128)(2,1)S(1)} %get-tuple-element.21.refs_6_), channel_id=1, source_target_pairs={{1,2},{3,11},{2,1},{0,8},{5,6},{7,15},{6,5},{4,12},{9,10},{11,3},{... | collective-permute-start | bytes 122888 | tf_op jit(solution)/shard_map/ppermute | solution.py:70
  15.3 1.3 %collective-permute-start.6 = (bf16[4,20,256]{2,1,0:T(8,128)(2,1)S(1)}, bf16[4,20,256]{2,1,0:T(8,128)(2,1)S(1)}, u32[]{:S(2)}, u32[]{:S(2)}) collective-permute-start(bf16[4,20,256]{2,1,0:T(8,128)(2,1)S(1)} %get-tuple-element.24), channel_id=1, source_target_pairs={{0,4},{4,0},{1,5},{5,1},{2,6},{6,2},{3,7},{7,3},{8,12},{12,8},{9,1... | collective-permute-start | bytes 122888 | tf_op jit(solution)/shard_map/ppermute | solution.py:56

commit v11 on v10

--- a/solution.py
+++ b/solution.py
@@ -62,10 +62,8 @@
     for send, pairing in zip(sends, swaps(cols)):
         pairs = []
         for group in range(sections * rows):
-            section, row = divmod(group, rows)
             for i, j in pairing:
-                far = abs(i - j) > 1 and sections % 2 == 0
-                to = ((section ^ 1) * rows + row, i) if far else (group, j)
+                to = (group ^ 1, i) if abs(i - j) > 1 else (group, j)
                 pairs.append((group * cols + i, to[0] * cols + to[1]))
         got.append(lax.ppermute(send, ("section", "row", "col"), pairs))
     return got
@@ -406,7 +404,7 @@
     came = column_exchange(sends, sections)
     fields = [(earlier, early_got), (latent, own_got)]
     rest = early - (frames - 2)
-    cut = rest // 2
+    cut = rest - 1
     first_part = inner(fields, 0, cut, *sends)
     (rim,) = call(
         functools.partial(rim_columns, rows=rounds), [strip], [*early_got, *own_got, *first_part],

time: 21.9 us -> 20.8 us (0.950)
  the two profiles are of different devices: /device:TPU:0 before, /device:TPU:17 now
where the time goes in v11:
time: 20.8 us; the launch traced here: 20.6 us
  Pallas kernels  10.1 us (49%)
  starting transfers between devices  7.01 us (34%)
  waiting for transfers between devices  3.36 us (16%)
    pallas_call x14, Pallas kernels, call(): pl.pallas_call(body, out_shape=outs, in_specs=[spec] * len(args), out_spe...  10.1 us
    ppermute x3, starting transfers between devices, exchange(): lax.ppermute(s, axis, pairs)  3.09 us
    ppermute x2, starting transfers between devices, per_device(): lax.ppermute(ends.pop(0) if take < frames else latent, 'section', ring)  2.56 us
    ppermute x2, waiting for transfers between devices, per_device(): lax.ppermute(ends.pop(0) if take < frames else latent, 'section', ring)  2.45 us
    ppermute x2, starting transfers between devices, column_exchange(): got.append(lax.ppermute(send, ('section', 'row', 'col'), pairs))  1.35 us
    ppermute x2, waiting for transfers between devices, column_exchange(): got.append(lax.ppermute(send, ('section', 'row', 'col'), pairs))  0.74 us
  transfers between devices with their start and end apart: 7, of which 3 were waited for; matrix products, arithmetic and copies ran while one was open for 0% of the time, Pallas kernels for 24%

profile of v11, /device:TPU:17, one launch (start us, length us, event | category | flops | bytes accessed | tf_op | source)
XLA Modules:
  0.0 20.6 jit_solution(10404258396297789081)
XLA Ops:
  0.0 0.0 copy-start.1
  0.0 0.0 copy-start.3
  0.0 0.0 copy-start.2
  0.0 1.3 %collective-permute-start.2 = (bf16[4,4,16,256]{3,2,1,0:T(8,128)(2,1)}, bf16[4,4,16,256]{3,2,1,0:T(8,128)(2,1)S(1)}, u32[]{:S(2)}, u32[]{:S(2)}) collective-permute-start(bf16[4,4,16,256]{3,2,1,0:T(8,128)(2,1)} %refs_2_.5), channel_id=1, source_target_pairs={{0,8},{8,16},{16,24},{24,0},{1,9},{9,17},{17,25},{25,1},{2,10},{10... | collective-permute-start | bytes 393224 | tf_op jit(solution)/shard_map/ppermute | solution.py:369
  1.3 0.0 copy-done.1
  1.3 1.0 %collective-permute-start = (bf16[4,2,16,256]{3,2,1,0:T(8,128)(2,1)S(1)}, bf16[4,2,16,256]{3,2,1,0:T(8,128)(2,1)S(1)}, u32[]{:S(2)}, u32[]{:S(2)}) collective-permute-start(bf16[4,2,16,256]{3,2,1,0:T(8,128)(2,1)S(1)} %shard_map.47), channel_id=1, source_target_pairs={{0,4},{4,0},{1,5},{5,1},{2,6},{6,2},{3,7},{7,3},{8,12},{12,8},{9,1... | collective-permute-start | bytes 196616 | tf_op jit(solution)/shard_map/ppermute | solution.py:56
  2.3 0.0 copy-start
  2.3 1.3 %collective-permute-start.1 = (bf16[2,4,16,256]{3,2,1,0:T(8,128)(2,1)S(1)}, bf16[2,4,16,256]{3,2,1,0:T(8,128)(2,1)S(1)}, u32[]{:S(2)}, u32[]{:S(2)}) collective-permute-start(bf16[2,4,16,256]{3,2,1,0:T(8,128)(2,1)S(1)} %shard_map.50), channel_id=1, source_target_pairs={{0,16},{8,24},{16,0},{24,8},{1,17},{9,25},{17,1},{25,9},{2,18},{10... | collective-permute-start | bytes 196616 | tf_op jit(solution)/shard_map/ppermute | solution.py:369
  3.6 0.0 copy-done.3
  3.6 0.0 copy-done.2
  3.6 1.0 %shard_map.48 = (bf16[3,2,2,256,512]{4,3,2,1,0:T(8,128)(2,1)S(1)}, bf16[3,3,2,256,256]{4,3,2,1,0:T(8,128)(2,1)S(1)}, f32[8,128]{1,0:T(8,128)S(1)}) custom-call(bf16[3,3,3,256,128]{4,3,2,1,0:T(8,128)(2,1)S(1)} %copy-done.2, bf16[3,3,3,128,128]{4,3,2,1,0:T(8,128)(2,1)S(1)} %copy-done.3), custom_call_target="tpu_custom_call" | custom-call | flops 4000000000 | bytes 8163328 | tf_op jit(solution)/shard_map/pallas_call | solution.py:20
  4.7 0.0 collective-permute-done.refs_1_.refs_3_
  4.7 0.0 copy-done
  4.7 0.9 %shard_map.49.refs_0_.refs_2_ = f32[2,6,16,256]{3,2,1,0:T(8,128)S(1)} custom-call(bf16[4,4,16,256]{3,2,1,0:T(8,128)(2,1)S(1)} %copy-done.1, bf16[4,2,16,256]{3,2,1,0:T(8,128)(2,1)S(1)} %collective-permute-done.refs_1_.refs_3_, bf16[3,3,3,256,256]{4,3,2,1,0:T(8,128)(2,1)S(1)} %copy-done, f32[8,128]{1,0:T(8,128)S(1)} %get-tuple-element.17.refs_3_), custom_call_target="tpu_custom_call" | custom-call | flops 679477248 | bytes 3936256 | tf_op jit(solution)/shard_map/pallas_call | solution.py:20
  5.6 2.4 %collective-permute-done.1.refs_1_ = bf16[2,4,16,256]{3,2,1,0:T(8,128)(2,1)S(1)} collective-permute-done((bf16[2,4,16,256]{3,2,1,0:T(8,128)(2,1)S(1)}, bf16[2,4,16,256]{3,2,1,0:T(8,128)(2,1)S(1)}, u32[]{:S(2)}, u32[]{:S(2)}) %collective-permute-start.1) | collective-permute-done | bytes 65568 | tf_op jit(solution)/shard_map/ppermute | solution.py:369
  8.0 0.0 collective-permute-done.2.refs_2_
  8.1 0.5 %collective-permute-start.3 = (bf16[6,2,16,256]{3,2,1,0:T(8,128)(2,1)S(1)}, bf16[6,2,16,256]{3,2,1,0:T(8,128)(2,1)S(1)}, u32[]{:S(2)}, u32[]{:S(2)}) collective-permute-start(bf16[6,2,16,256]{3,2,1,0:T(8,128)(2,1)S(1)} %get-tuple-element.19), channel_id=1, source_target_pairs={{0,4},{4,0},{1,5},{5,1},{2,6},{6,2},{3,7},{7,3},{8,12},{12,8},{9,1... | collective-permute-start | bytes 294920 | tf_op jit(solution)/shard_map/ppermute | solution.py:56
  8.6 0.2 shard_map.52
  8.8 1.4 %collective-permute-start.4 = (bf16[2,40,256]{2,1,0:T(8,128)(2,1)S(1)}, bf16[2,40,256]{2,1,0:T(8,128)(2,1)S(1)}, u32[]{:S(2)}, u32[]{:S(2)}) collective-permute-start(bf16[2,40,256]{2,1,0:T(8,128)(2,1)S(1)} %get-tuple-element.20.refs_5_), channel_id=1, source_target_pairs={{0,1},{2,3},{1,0},{3,2},{4,5},{6,7},{5,4},{7,6},{8,9},{10,11},{9,8... | collective-permute-start | bytes 122888 | tf_op jit(solution)/shard_map/ppermute | solution.py:68
  10.1 0.0 collective-permute-start.5
  10.1 0.0 collective-permute-done.3.refs_1_.refs_0_
  10.1 1.9 %shard_map.53.refs_2_.refs_0_ = f32[5,6,16,256]{3,2,1,0:T(8,128)S(1)} custom-call(bf16[6,4,16,256]{3,2,1,0:T(8,128)(2,1)S(1)} %get-tuple-element.18.before.refs_0_, bf16[6,2,16,256]{3,2,1,0:T(8,128)(2,1)S(1)} %collective-permute-done.3.refs_1_.refs_0_, bf16[4,4,16,256]{3,2,1,0:T(8,128)(2,1)S(1)} %copy-done.1, ...), custom_call_target="tpu_custom_call" | custom-call | flops 1698693120 | bytes 4603904 | tf_op jit(solution)/shard_map/pallas_call | solution.py:20
  12.1 0.2 shard_map.54.refs_2_.refs_4_
  12.2 0.0 collective-permute-done.4.refs_0_
  12.3 0.7 %collective-permute-done.5.refs_1_ = bf16[2,40,256]{2,1,0:T(8,128)(2,1)S(1)} collective-permute-done((bf16[2,40,256]{2,1,0:T(8,128)(2,1)S(1)}, bf16[2,40,256]{2,1,0:T(8,128)(2,1)S(1)}, u32[]{:S(2)}, u32[]{:S(2)}) %collective-permute-start.5) | collective-permute-done | bytes 40992 | tf_op jit(solution)/shard_map/ppermute | solution.py:68
  13.0 1.6 %collective-permute-start.6 = (bf16[4,20,256]{2,1,0:T(8,128)(2,1)S(1)}, bf16[4,20,256]{2,1,0:T(8,128)(2,1)S(1)}, u32[]{:S(2)}, u32[]{:S(2)}) collective-permute-start(bf16[4,20,256]{2,1,0:T(8,128)(2,1)S(1)} %get-tuple-element.24), channel_id=1, source_target_pairs={{0,4},{4,0},{1,5},{5,1},{2,6},{6,2},{3,7},{7,3},{8,12},{12,8},{9,1... | collective-permute-start | bytes 122888 | tf_op jit(solution)/shard_map/ppermute | solution.py:56
  14.6 0.7 %shard_map.56.refs_1_ = f32[1,6,16,256]{3,2,1,0:T(8,128)S(1)} custom-call(bf16[6,4,16,256]{3,2,1,0:T(8,128)(2,1)S(1)} %get-tuple-element.18.before.refs_0_, bf16[6,2,16,256]{3,2,1,0:T(8,128)(2,1)S(1)} %collective-permute-done.3.refs_1_.refs_0_, bf16[4,4,16,256]{3,2,1,0:T(8,128)(2,1)S(1)} %copy-done.1, ...), custom_call_target="tpu_custom_call" | custom-call | flops 339738624 | bytes 4210688 | tf_op jit(solution)/shard_map/pallas_call | solution.py:20
  15.3 0.2 collective-permute-done.6.refs_6_
  15.5 1.1 %shard_map.57 = (bf16[2,6,8,16,256]{4,3,2,1,0:T(8,128)(2,1)S(1)}, f32[2,56,256]{2,1,0:T(8,128)S(1)}) custom-call(f32[5,6,16,256]{3,2,1,0:T(8,128)S(1)} %shard_map.53.refs_2_.refs_0_, f32[1,6,16,256]{3,2,1,0:T(8,128)S(1)} %shard_map.56.refs_1_, f32[2,6,16,256]{3,2,1,0:T(8,128)S(1)} %shard_map.49.refs_0_.refs_2_, ...), custom_call_target="tpu_custom_call" | custom-call | flops 1000000000 | bytes 5513216 | tf_op jit(solution)/shard_map/pallas_call | solution.py:20
  16.6 1.9 %shard_map.58.fine = bf16[2,10,6,16,256]{4,3,2,1,0:T(8,128)(2,1)S(1)} custom-call(bf16[2,6,8,16,256]{4,3,2,1,0:T(8,128)(2,1)S(1)} %get-tuple-element.25.near, f32[2,56,256]{2,1,0:T(8,128)S(1)} %get-tuple-element.26.far, bf16[3,2,2,256,512]{4,3,2,1,0:T(8,128)(2,1)S(1)} %get-tuple-element.27.summed), custom_call_target="tpu_custom_call" | custom-call | flops 2000000000 | bytes 5029888 | tf_op jit(solution)/shard_map/pallas_call | solution.py:20
  18.5 2.1 %shard_map.59 = bf16[4,8,32,128]{3,2,1,0:T(8,128)(2,1)} custom-call(bf16[2,10,6,16,256]{4,3,2,1,0:T(8,128)(2,1)S(1)} %shard_map.58.fine, bf16[3,3,2,256,256]{4,3,2,1,0:T(8,128)(2,1)S(1)} %get-tuple-element.28.paired), custom_call_target="tpu_custom_call" | custom-call | flops 1000000000 | bytes 3604480 | tf_op jit(solution)/shard_map/pallas_call | solution.py:20
  (5 shorter events, 0.1 us)
Async XLA Ops:
  0.0 1.3 %copy-start.1 = (bf16[4,4,16,256]{3,2,1,0:T(8,128)(2,1)S(1)}, bf16[4,4,16,256]{3,2,1,0:T(8,128)(2,1)}, u32[]{:S(2)}) copy-start(bf16[4,4,16,256]{3,2,1,0:T(8,128)(2,1)} %refs_2_.5) | copy-start | bytes 393220
  0.0 3.6 %copy-start.3 = (bf16[3,3,3,128,128]{4,3,2,1,0:T(8,128)(2,1)S(1)}, bf16[3,3,3,128,128]{4,3,2,1,0:T(8,128)(2,1)}, u32[]{:S(2)}) copy-start(bf16[3,3,3,128,128]{4,3,2,1,0:T(8,128)(2,1)} %third.1) | copy-start | bytes 2654212
  0.0 3.6 %copy-start.2 = (bf16[3,3,3,256,128]{4,3,2,1,0:T(8,128)(2,1)S(1)}, bf16[3,3,3,256,128]{4,3,2,1,0:T(8,128)(2,1)}, u32[]{:S(2)}) copy-start(bf16[3,3,3,256,128]{4,3,2,1,0:T(8,128)(2,1)} %second.1) | copy-start | bytes 5308420
  0.0 8.0 %collective-permute-start.2 = (bf16[4,4,16,256]{3,2,1,0:T(8,128)(2,1)}, bf16[4,4,16,256]{3,2,1,0:T(8,128)(2,1)S(1)}, u32[]{:S(2)}, u32[]{:S(2)}) collective-permute-start(bf16[4,4,16,256]{3,2,1,0:T(8,128)(2,1)} %refs_2_.5), channel_id=1, source_target_pairs={{0,8},{8,16},{16,24},{24,0},{1,9},{9,17},{17,25},{25,1},{2,10},{10... | collective-permute-start | bytes 393224 | tf_op jit(solution)/shard_map/ppermute | solution.py:369
  1.3 3.4 %collective-permute-start = (bf16[4,2,16,256]{3,2,1,0:T(8,128)(2,1)S(1)}, bf16[4,2,16,256]{3,2,1,0:T(8,128)(2,1)S(1)}, u32[]{:S(2)}, u32[]{:S(2)}) collective-permute-start(bf16[4,2,16,256]{3,2,1,0:T(8,128)(2,1)S(1)} %shard_map.47), channel_id=1, source_target_pairs={{0,4},{4,0},{1,5},{5,1},{2,6},{6,2},{3,7},{7,3},{8,12},{12,8},{9,1... | collective-permute-start | bytes 196616 | tf_op jit(solution)/shard_map/ppermute | solution.py:56
  2.3 2.4 %copy-start = (bf16[3,3,3,256,256]{4,3,2,1,0:T(8,128)(2,1)S(1)}, bf16[3,3,3,256,256]{4,3,2,1,0:T(8,128)(2,1)}, u32[]{:S(2)}) copy-start(bf16[3,3,3,256,256]{4,3,2,1,0:T(8,128)(2,1)} %refs_7_.1) | copy-start | bytes 10616836
  2.3 5.7 %collective-permute-start.1 = (bf16[2,4,16,256]{3,2,1,0:T(8,128)(2,1)S(1)}, bf16[2,4,16,256]{3,2,1,0:T(8,128)(2,1)S(1)}, u32[]{:S(2)}, u32[]{:S(2)}) collective-permute-start(bf16[2,4,16,256]{3,2,1,0:T(8,128)(2,1)S(1)} %shard_map.50), channel_id=1, source_target_pairs={{0,16},{8,24},{16,0},{24,8},{1,17},{9,25},{17,1},{25,9},{2,18},{10... | collective-permute-start | bytes 196616 | tf_op jit(solution)/shard_map/ppermute | solution.py:369
  8.1 2.1 %collective-permute-start.3 = (bf16[6,2,16,256]{3,2,1,0:T(8,128)(2,1)S(1)}, bf16[6,2,16,256]{3,2,1,0:T(8,128)(2,1)S(1)}, u32[]{:S(2)}, u32[]{:S(2)}) collective-permute-start(bf16[6,2,16,256]{3,2,1,0:T(8,128)(2,1)S(1)} %get-tuple-element.19), channel_id=1, source_target_pairs={{0,4},{4,0},{1,5},{5,1},{2,6},{6,2},{3,7},{7,3},{8,12},{12,8},{9,1... | collective-permute-start | bytes 294920 | tf_op jit(solution)/shard_map/ppermute | solution.py:56
  8.8 3.5 %collective-permute-start.4 = (bf16[2,40,256]{2,1,0:T(8,128)(2,1)S(1)}, bf16[2,40,256]{2,1,0:T(8,128)(2,1)S(1)}, u32[]{:S(2)}, u32[]{:S(2)}) collective-permute-start(bf16[2,40,256]{2,1,0:T(8,128)(2,1)S(1)} %get-tuple-element.20.refs_5_), channel_id=1, source_target_pairs={{0,1},{2,3},{1,0},{3,2},{4,5},{6,7},{5,4},{7,6},{8,9},{10,11},{9,8... | collective-permute-start | bytes 122888 | tf_op jit(solution)/shard_map/ppermute | solution.py:68
  10.1 2.9 %collective-permute-start.5 = (bf16[2,40,256]{2,1,0:T(8,128)(2,1)S(1)}, bf16[2,40,256]{2,1,0:T(8,128)(2,1)S(1)}, u32[]{:S(2)}, u32[]{:S(2)}) collective-permute-start(bf16[2,40,256]{2,1,0:T(8,128)(2,1)S(1)} %get-tuple-element.21.refs_6_), channel_id=1, source_target_pairs={{1,2},{3,7},{2,1},{0,4},{5,6},{7,3},{6,5},{4,0},{9,10},{11,15},{10... | collective-permute-start | bytes 122888 | tf_op jit(solution)/shard_map/ppermute | solution.py:68
  13.0 2.4 %collective-permute-start.6 = (bf16[4,20,256]{2,1,0:T(8,128)(2,1)S(1)}, bf16[4,20,256]{2,1,0:T(8,128)(2,1)S(1)}, u32[]{:S(2)}, u32[]{:S(2)}) collective-permute-start(bf16[4,20,256]{2,1,0:T(8,128)(2,1)S(1)} %get-tuple-element.24), channel_id=1, source_target_pairs={{0,4},{4,0},{1,5},{5,1},{2,6},{6,2},{3,7},{7,3},{8,12},{12,8},{9,1... | collective-permute-start | bytes 122888 | tf_op jit(solution)/shard_map/ppermute | solution.py:56

commit v12 on v11

--- a/solution.py
+++ b/solution.py
@@ -134,6 +134,13 @@
     for k, send in enumerate(sends):
         start = jnp.where(right, 0, RIM) if k else jnp.where(right, RIM, 0)
         send[...] = own[pl.ds(start, RIM)]
+
+
+def join_and_send(*refs, pieces, rounds):
+    count = 1 + len(pieces)
+    latent, rest = refs[count], refs[count + 1 :]
+    join_frames(*refs[:count], *rest[: 1 + rounds], pieces=pieces)
+    send_columns(rest[0], latent, *rest[1 + rounds :])
 
 
 def rim_columns(*refs, rows):
@@ -389,22 +396,20 @@
         )
 
     inners = inner([(latent, own_got)], 0, frames - 2, ready)
-    earlier, *sends = call(
-        functools.partial(join_frames, pieces=pieces),
-        [((EARLIER, height, breadth, width), BF)] + [((EARLIER, RIM, breadth, width), BF)] * rounds,
-        [inners[0], *got],
-    )
-    early_got = exchange(sends, "row")
     strip = ((2 * RIM, height * total, width), BF)
     scratch = [(blocked(total * height * breadth, width), F32), ((height * total, width), F32)]
-    *sends, own = call(
-        send_columns, [((RIM, height * total, width), BF)] * cols + [strip], [earlier, latent],
-        scratch,
-    )
+    earlier, *sends, own = call(
+        functools.partial(join_and_send, pieces=pieces, rounds=rounds),
+        [((EARLIER, height, breadth, width), BF)] + [((EARLIER, RIM, breadth, width), BF)] * rounds
+        + [((RIM, height * total, width), BF)] * cols + [strip],
+        [inners[0], *got, latent], scratch,
+    )
+    early_got = exchange(sends[:rounds], "row")
+    sends = sends[rounds:]
     came = column_exchange(sends, sections)
     fields = [(earlier, early_got), (latent, own_got)]
     rest = early - (frames - 2)
-    cut = rest - 1
+    cut = 2 * rest // 3
     first_part = inner(fields, 0, cut, *sends)
     (rim,) = call(
         functools.partial(rim_columns, rows=rounds), [strip], [*early_got, *own_got, *first_part],

time: 20.8 us -> 20.7 us (level)
  the two profiles are of different devices: /device:TPU:17 before, /device:TPU:21 now
where the time goes in v12:
time: 20.7 us; the launch traced here: 20.6 us
  Pallas kernels  9.96 us (48%)
  starting transfers between devices  5.95 us (29%)
  waiting for transfers between devices  3.92 us (19%)
  local copies, waits for them, and re-layouts  0.65 us (3%)
    pallas_call x13, Pallas kernels, call(): pl.pallas_call(body, out_shape=outs, in_specs=[spec] * len(args), out_spe...  9.96 us
    ppermute x3, starting transfers between devices, exchange(): lax.ppermute(s, axis, pairs)  3.1 us
    ppermute x2, waiting for transfers between devices, per_device(): lax.ppermute(ends.pop(0) if take < frames else latent, 'section', ring)  2.83 us
    ppermute x2, starting transfers between devices, per_device(): lax.ppermute(ends.pop(0) if take < frames else latent, 'section', ring)  1.55 us
    ppermute x2, starting transfers between devices, column_exchange(): got.append(lax.ppermute(send, ('section', 'row', 'col'), pairs))  1.29 us
    ppermute x2, waiting for transfers between devices, column_exchange(): got.append(lax.ppermute(send, ('section', 'row', 'col'), pairs))  1.08 us
    unnamed x8, local copies, waits for them, and re-layouts  0.65 us
  transfers between devices with their start and end apart: 7, of which 2 were waited for; matrix products, arithmetic and copies ran while one was open for 0% of the time, Pallas kernels for 22%

profile of v12, /device:TPU:21, one launch (start us, length us, event | category | flops | bytes accessed | tf_op | source)
XLA Modules:
  0.0 20.6 jit_solution(17959592574748842681)
XLA Ops:
  0.0 0.0 copy-start.1
  0.0 0.0 copy-start.3
  0.0 0.0 copy-start.2
  0.0 1.3 %collective-permute-start.2 = (bf16[4,4,16,256]{3,2,1,0:T(8,128)(2,1)}, bf16[4,4,16,256]{3,2,1,0:T(8,128)(2,1)S(1)}, u32[]{:S(2)}, u32[]{:S(2)}) collective-permute-start(bf16[4,4,16,256]{3,2,1,0:T(8,128)(2,1)} %refs_2_.5), channel_id=1, source_target_pairs={{0,8},{8,16},{16,24},{24,0},{1,9},{9,17},{17,25},{25,1},{2,10},{10... | collective-permute-start | bytes 393224 | tf_op jit(solution)/shard_map/ppermute | solution.py:376
  1.3 0.0 copy-done.1
  1.3 1.0 %collective-permute-start = (bf16[4,2,16,256]{3,2,1,0:T(8,128)(2,1)S(1)}, bf16[4,2,16,256]{3,2,1,0:T(8,128)(2,1)S(1)}, u32[]{:S(2)}, u32[]{:S(2)}) collective-permute-start(bf16[4,2,16,256]{3,2,1,0:T(8,128)(2,1)S(1)} %shard_map.47), channel_id=1, source_target_pairs={{0,4},{4,0},{1,5},{5,1},{2,6},{6,2},{3,7},{7,3},{8,12},{12,8},{9,1... | collective-permute-start | bytes 196616 | tf_op jit(solution)/shard_map/ppermute | solution.py:56
  2.3 0.0 copy-start
  2.3 0.3 %collective-permute-start.1 = (bf16[2,4,16,256]{3,2,1,0:T(8,128)(2,1)S(1)}, bf16[2,4,16,256]{3,2,1,0:T(8,128)(2,1)S(1)}, u32[]{:S(2)}, u32[]{:S(2)}) collective-permute-start(bf16[2,4,16,256]{3,2,1,0:T(8,128)(2,1)S(1)} %shard_map.50), channel_id=1, source_target_pairs={{0,16},{8,24},{16,0},{24,8},{1,17},{9,25},{17,1},{25,9},{2,18},{10... | collective-permute-start | bytes 196616 | tf_op jit(solution)/shard_map/ppermute | solution.py:376
  2.6 0.0 copy-done.3
  2.6 0.0 copy-done.2
  2.6 1.0 %shard_map.48 = (bf16[3,2,2,256,512]{4,3,2,1,0:T(8,128)(2,1)S(1)}, bf16[3,3,2,256,256]{4,3,2,1,0:T(8,128)(2,1)S(1)}, f32[8,128]{1,0:T(8,128)S(1)}) custom-call(bf16[3,3,3,256,128]{4,3,2,1,0:T(8,128)(2,1)S(1)} %copy-done.2, bf16[3,3,3,128,128]{4,3,2,1,0:T(8,128)(2,1)S(1)} %copy-done.3), custom_call_target="tpu_custom_call" | custom-call | flops 4000000000 | bytes 8163328 | tf_op jit(solution)/shard_map/pallas_call | solution.py:20
  3.7 0.0 collective-permute-done.refs_1_.refs_3_
  3.7 0.6 %copy-done = bf16[3,3,3,256,256]{4,3,2,1,0:T(8,128)(2,1)S(1)} copy-done((bf16[3,3,3,256,256]{4,3,2,1,0:T(8,128)(2,1)S(1)}, bf16[3,3,3,256,256]{4,3,2,1,0:T(8,128)(2,1)}, u32[]{:S(2)}) %copy-start) | copy-done | bytes 3538968
  4.3 0.9 %shard_map.49.refs_0_.refs_2_ = f32[2,6,16,256]{3,2,1,0:T(8,128)S(1)} custom-call(bf16[4,4,16,256]{3,2,1,0:T(8,128)(2,1)S(1)} %copy-done.1, bf16[4,2,16,256]{3,2,1,0:T(8,128)(2,1)S(1)} %collective-permute-done.refs_1_.refs_3_, bf16[3,3,3,256,256]{4,3,2,1,0:T(8,128)(2,1)S(1)} %copy-done, f32[8,128]{1,0:T(8,128)S(1)} %get-tuple-element.17.refs_3_), custom_call_target="tpu_custom_call" | custom-call | flops 679477248 | bytes 3936256 | tf_op jit(solution)/shard_map/pallas_call | solution.py:20
  5.2 2.8 %collective-permute-done.1.refs_1_ = bf16[2,4,16,256]{3,2,1,0:T(8,128)(2,1)S(1)} collective-permute-done((bf16[2,4,16,256]{3,2,1,0:T(8,128)(2,1)S(1)}, bf16[2,4,16,256]{3,2,1,0:T(8,128)(2,1)S(1)}, u32[]{:S(2)}, u32[]{:S(2)}) %collective-permute-start.1) | collective-permute-done | bytes 65568 | tf_op jit(solution)/shard_map/ppermute | solution.py:376
  8.0 0.0 collective-permute-done.2.refs_2_
  8.0 0.2 shard_map.51
  8.2 0.5 %collective-permute-start.3 = (bf16[6,2,16,256]{3,2,1,0:T(8,128)(2,1)S(1)}, bf16[6,2,16,256]{3,2,1,0:T(8,128)(2,1)S(1)}, u32[]{:S(2)}, u32[]{:S(2)}) collective-permute-start(bf16[6,2,16,256]{3,2,1,0:T(8,128)(2,1)S(1)} %get-tuple-element.19), channel_id=1, source_target_pairs={{0,4},{4,0},{1,5},{5,1},{2,6},{6,2},{3,7},{7,3},{8,12},{12,8},{9,1... | collective-permute-start | bytes 294920 | tf_op jit(solution)/shard_map/ppermute | solution.py:56
  8.8 1.3 %collective-permute-start.4 = (bf16[2,40,256]{2,1,0:T(8,128)(2,1)S(1)}, bf16[2,40,256]{2,1,0:T(8,128)(2,1)S(1)}, u32[]{:S(2)}, u32[]{:S(2)}) collective-permute-start(bf16[2,40,256]{2,1,0:T(8,128)(2,1)S(1)} %get-tuple-element.20.refs_5_), channel_id=1, source_target_pairs={{0,1},{2,3},{1,0},{3,2},{4,5},{6,7},{5,4},{7,6},{8,9},{10,11},{9,8... | collective-permute-start | bytes 122888 | tf_op jit(solution)/shard_map/ppermute | solution.py:68
  10.0 0.0 collective-permute-start.5
  10.0 0.0 collective-permute-done.3.refs_1_.refs_0_
  10.1 1.6 %shard_map.52.refs_2_.refs_0_ = f32[4,6,16,256]{3,2,1,0:T(8,128)S(1)} custom-call(bf16[6,4,16,256]{3,2,1,0:T(8,128)(2,1)S(1)} %get-tuple-element.18.refs_0_, bf16[6,2,16,256]{3,2,1,0:T(8,128)(2,1)S(1)} %collective-permute-done.3.refs_1_.refs_0_, bf16[4,4,16,256]{3,2,1,0:T(8,128)(2,1)S(1)} %copy-done.1, ...), custom_call_target="tpu_custom_call" | custom-call | flops 1358954496 | bytes 4505600 | tf_op jit(solution)/shard_map/pallas_call | solution.py:20
  11.6 0.2 shard_map.53.refs_2_.refs_4_
  11.8 0.0 collective-permute-done.4.refs_0_
  11.8 1.1 %collective-permute-done.5.refs_1_ = bf16[2,40,256]{2,1,0:T(8,128)(2,1)S(1)} collective-permute-done((bf16[2,40,256]{2,1,0:T(8,128)(2,1)S(1)}, bf16[2,40,256]{2,1,0:T(8,128)(2,1)S(1)}, u32[]{:S(2)}, u32[]{:S(2)}) %collective-permute-start.5) | collective-permute-done | bytes 40992 | tf_op jit(solution)/shard_map/ppermute | solution.py:68
  12.9 1.6 %collective-permute-start.6 = (bf16[4,20,256]{2,1,0:T(8,128)(2,1)S(1)}, bf16[4,20,256]{2,1,0:T(8,128)(2,1)S(1)}, u32[]{:S(2)}, u32[]{:S(2)}) collective-permute-start(bf16[4,20,256]{2,1,0:T(8,128)(2,1)S(1)} %get-tuple-element.24), channel_id=1, source_target_pairs={{0,4},{4,0},{1,5},{5,1},{2,6},{6,2},{3,7},{7,3},{8,12},{12,8},{9,1... | collective-permute-start | bytes 122888 | tf_op jit(solution)/shard_map/ppermute | solution.py:56
  14.5 0.9 %shard_map.55.refs_1_ = f32[2,6,16,256]{3,2,1,0:T(8,128)S(1)} custom-call(bf16[6,4,16,256]{3,2,1,0:T(8,128)(2,1)S(1)} %get-tuple-element.18.refs_0_, bf16[6,2,16,256]{3,2,1,0:T(8,128)(2,1)S(1)} %collective-permute-done.3.refs_1_.refs_0_, bf16[4,4,16,256]{3,2,1,0:T(8,128)(2,1)S(1)} %copy-done.1, ...), custom_call_target="tpu_custom_call" | custom-call | flops 679477248 | bytes 4308992 | tf_op jit(solution)/shard_map/pallas_call | solution.py:20
  15.4 0.0 collective-permute-done.6.refs_6_
  15.4 1.1 %shard_map.56 = (bf16[2,6,8,16,256]{4,3,2,1,0:T(8,128)(2,1)S(1)}, f32[2,56,256]{2,1,0:T(8,128)S(1)}) custom-call(f32[4,6,16,256]{3,2,1,0:T(8,128)S(1)} %shard_map.52.refs_2_.refs_0_, f32[2,6,16,256]{3,2,1,0:T(8,128)S(1)} %shard_map.55.refs_1_, f32[2,6,16,256]{3,2,1,0:T(8,128)S(1)} %shard_map.49.refs_0_.refs_2_, ...), custom_call_target="tpu_custom_call" | custom-call | flops 1000000000 | bytes 5513216 | tf_op jit(solution)/shard_map/pallas_call | solution.py:20
  16.5 1.9 %shard_map.57.fine = bf16[2,10,6,16,256]{4,3,2,1,0:T(8,128)(2,1)S(1)} custom-call(bf16[2,6,8,16,256]{4,3,2,1,0:T(8,128)(2,1)S(1)} %get-tuple-element.25.near, f32[2,56,256]{2,1,0:T(8,128)S(1)} %get-tuple-element.26.far, bf16[3,2,2,256,512]{4,3,2,1,0:T(8,128)(2,1)S(1)} %get-tuple-element.27.summed), custom_call_target="tpu_custom_call" | custom-call | flops 2000000000 | bytes 5029888 | tf_op jit(solution)/shard_map/pallas_call | solution.py:20
  18.4 2.1 %shard_map.58 = bf16[4,8,32,128]{3,2,1,0:T(8,128)(2,1)} custom-call(bf16[2,10,6,16,256]{4,3,2,1,0:T(8,128)(2,1)S(1)} %shard_map.57.fine, bf16[3,3,2,256,256]{4,3,2,1,0:T(8,128)(2,1)S(1)} %get-tuple-element.28.paired), custom_call_target="tpu_custom_call" | custom-call | flops 1000000000 | bytes 3604480 | tf_op jit(solution)/shard_map/pallas_call | solution.py:20
  (4 shorter events, 0.1 us)
Async XLA Ops:
  0.0 1.3 %copy-start.1 = (bf16[4,4,16,256]{3,2,1,0:T(8,128)(2,1)S(1)}, bf16[4,4,16,256]{3,2,1,0:T(8,128)(2,1)}, u32[]{:S(2)}) copy-start(bf16[4,4,16,256]{3,2,1,0:T(8,128)(2,1)} %refs_2_.5) | copy-start | bytes 393220
  0.0 2.6 %copy-start.3 = (bf16[3,3,3,128,128]{4,3,2,1,0:T(8,128)(2,1)S(1)}, bf16[3,3,3,128,128]{4,3,2,1,0:T(8,128)(2,1)}, u32[]{:S(2)}) copy-start(bf16[3,3,3,128,128]{4,3,2,1,0:T(8,128)(2,1)} %third.1) | copy-start | bytes 2654212
  0.0 2.6 %copy-start.2 = (bf16[3,3,3,256,128]{4,3,2,1,0:T(8,128)(2,1)S(1)}, bf16[3,3,3,256,128]{4,3,2,1,0:T(8,128)(2,1)}, u32[]{:S(2)}) copy-start(bf16[3,3,3,256,128]{4,3,2,1,0:T(8,128)(2,1)} %second.1) | copy-start | bytes 5308420
  0.0 8.0 %collective-permute-start.2 = (bf16[4,4,16,256]{3,2,1,0:T(8,128)(2,1)}, bf16[4,4,16,256]{3,2,1,0:T(8,128)(2,1)S(1)}, u32[]{:S(2)}, u32[]{:S(2)}) collective-permute-start(bf16[4,4,16,256]{3,2,1,0:T(8,128)(2,1)} %refs_2_.5), channel_id=1, source_target_pairs={{0,8},{8,16},{16,24},{24,0},{1,9},{9,17},{17,25},{25,1},{2,10},{10... | collective-permute-start | bytes 393224 | tf_op jit(solution)/shard_map/ppermute | solution.py:376
  1.3 2.4 %collective-permute-start = (bf16[4,2,16,256]{3,2,1,0:T(8,128)(2,1)S(1)}, bf16[4,2,16,256]{3,2,1,0:T(8,128)(2,1)S(1)}, u32[]{:S(2)}, u32[]{:S(2)}) collective-permute-start(bf16[4,2,16,256]{3,2,1,0:T(8,128)(2,1)S(1)} %shard_map.47), channel_id=1, source_target_pairs={{0,4},{4,0},{1,5},{5,1},{2,6},{6,2},{3,7},{7,3},{8,12},{12,8},{9,1... | collective-permute-start | bytes 196616 | tf_op jit(solution)/shard_map/ppermute | solution.py:56
  2.3 2.0 %copy-start = (bf16[3,3,3,256,256]{4,3,2,1,0:T(8,128)(2,1)S(1)}, bf16[3,3,3,256,256]{4,3,2,1,0:T(8,128)(2,1)}, u32[]{:S(2)}) copy-start(bf16[3,3,3,256,256]{4,3,2,1,0:T(8,128)(2,1)} %refs_7_.1) | copy-start | bytes 10616836
  2.3 5.7 %collective-permute-start.1 = (bf16[2,4,16,256]{3,2,1,0:T(8,128)(2,1)S(1)}, bf16[2,4,16,256]{3,2,1,0:T(8,128)(2,1)S(1)}, u32[]{:S(2)}, u32[]{:S(2)}) collective-permute-start(bf16[2,4,16,256]{3,2,1,0:T(8,128)(2,1)S(1)} %shard_map.50), channel_id=1, source_target_pairs={{0,16},{8,24},{16,0},{24,8},{1,17},{9,25},{17,1},{25,9},{2,18},{10... | collective-permute-start | bytes 196616 | tf_op jit(solution)/shard_map/ppermute | solution.py:376
  8.2 1.8 %collective-permute-start.3 = (bf16[6,2,16,256]{3,2,1,0:T(8,128)(2,1)S(1)}, bf16[6,2,16,256]{3,2,1,0:T(8,128)(2,1)S(1)}, u32[]{:S(2)}, u32[]{:S(2)}) collective-permute-start(bf16[6,2,16,256]{3,2,1,0:T(8,128)(2,1)S(1)} %get-tuple-element.19), channel_id=1, source_target_pairs={{0,4},{4,0},{1,5},{5,1},{2,6},{6,2},{3,7},{7,3},{8,12},{12,8},{9,1... | collective-permute-start | bytes 294920 | tf_op jit(solution)/shard_map/ppermute | solution.py:56
  8.8 3.1 %collective-permute-start.4 = (bf16[2,40,256]{2,1,0:T(8,128)(2,1)S(1)}, bf16[2,40,256]{2,1,0:T(8,128)(2,1)S(1)}, u32[]{:S(2)}, u32[]{:S(2)}) collective-permute-start(bf16[2,40,256]{2,1,0:T(8,128)(2,1)S(1)} %get-tuple-element.20.refs_5_), channel_id=1, source_target_pairs={{0,1},{2,3},{1,0},{3,2},{4,5},{6,7},{5,4},{7,6},{8,9},{10,11},{9,8... | collective-permute-start | bytes 122888 | tf_op jit(solution)/shard_map/ppermute | solution.py:68
  10.0 2.9 %collective-permute-start.5 = (bf16[2,40,256]{2,1,0:T(8,128)(2,1)S(1)}, bf16[2,40,256]{2,1,0:T(8,128)(2,1)S(1)}, u32[]{:S(2)}, u32[]{:S(2)}) collective-permute-start(bf16[2,40,256]{2,1,0:T(8,128)(2,1)S(1)} %get-tuple-element.21.refs_6_), channel_id=1, source_target_pairs={{1,2},{3,7},{2,1},{0,4},{5,6},{7,3},{6,5},{4,0},{9,10},{11,15},{10... | collective-permute-start | bytes 122888 | tf_op jit(solution)/shard_map/ppermute | solution.py:68
  12.9 2.5 %collective-permute-start.6 = (bf16[4,20,256]{2,1,0:T(8,128)(2,1)S(1)}, bf16[4,20,256]{2,1,0:T(8,128)(2,1)S(1)}, u32[]{:S(2)}, u32[]{:S(2)}) collective-permute-start(bf16[4,20,256]{2,1,0:T(8,128)(2,1)S(1)} %get-tuple-element.24), channel_id=1, source_target_pairs={{0,4},{4,0},{1,5},{5,1},{2,6},{6,2},{3,7},{7,3},{8,12},{12,8},{9,1... | collective-permute-start | bytes 122888 | tf_op jit(solution)/shard_map/ppermute | solution.py:56
